TPU v7x, 32 devices: a whole 2x2x4 slice. The times are simulated.
32 devices in a mesh: dp: 2 (over y), seq: 4 (over z), tensor: 4 (over x, core).
Axes of the slice: x: 2, y: 2, z: 4, core: 2. Of those that a mesh axis runs over, the one named last changes fastest.
Arguments:
- layer_input: bfloat16 [6, 1024, 2048], P('dp', 'seq'), may hold values from -6 to 6
- lengths: int32 [6], P('dp'), may hold values from 256 to 1024, as said below
- cotangent: bfloat16 [6, 1024, 2048], P('dp', ('seq', 'tensor')), may hold values from -6 to 6
- ln1_gain: bfloat16 [2048], replicated, may hold values from 0.5 to 1.5
- ln1_bias: bfloat16 [2048], replicated, may hold values from -3 to 3
- w_query: bfloat16 [2048, 2048], P(None, 'tensor'), may hold values from -0.125 to 0.125
- b_query: bfloat16 [2048], P('tensor'), may hold values from -3 to 3
- w_kv: bfloat16 [2048, 256], replicated, may hold values from -0.125 to 0.125
- b_value: bfloat16 [128], replicated, may hold values from -3 to 3
- w_out: bfloat16 [2048, 2048], P('tensor'), may hold values from -0.5 to 0.5
- b_out: bfloat16 [2048], replicated, may hold values from -3 to 3
- ln2_gain: bfloat16 [2048], replicated, may hold values from 0.5 to 1.5
- ln2_bias: bfloat16 [2048], replicated, may hold values from -3 to 3
- w_up: bfloat16 [2048, 8192], P(None, 'tensor'), may hold values from -0.125 to 0.125
- b_up: bfloat16 [8192], P('tensor'), may hold values from -3 to 3
- w_down: bfloat16 [8192, 2048], P('tensor'), may hold values from -0.0625 to 0.0625
- b_down: bfloat16 [2048], replicated, may hold values from -3 to 3
Outputs:
- layer_output: bfloat16 [6, 1024, 2048], P('dp', ('seq', 'tensor'))
- input_grad: float32 [6, 1024, 2048], P('dp', ('seq', 'tensor'))
- g_w_query: float32 [2048, 2048], P(('dp', 'seq'), 'tensor')
- g_b_query: float32 [16, 128], P('tensor', ('dp', 'seq'))
- g_w_kv: float32 [2048, 256], P(('dp', 'seq', 'tensor'))
- g_b_value: float32 [128], P(('dp', 'seq', 'tensor'))
- g_w_out: float32 [2048, 2048], P('tensor', ('dp', 'seq'))
- g_w_up: float32 [2048, 8192], P(('dp', 'seq'), 'tensor')
- g_b_up: float32 [64, 128], P('tensor', ('dp', 'seq'))
- g_w_down: float32 [8192, 2048], P('tensor', ('dp', 'seq'))
- g_norms_biases: float32 [6, 2048], P(None, ('dp', 'seq', 'tensor'))
Inputs may be any that keep to these rules, and one draw needn't show every extreme that they name: `lengths`: the number of real tokens at the start of each row; the rest of the row is padding.
All inputs are finite; a program needn't handle non-finite values.
Results may differ from a plain program's by a relative error of at most 0.012.
Values may be sent and summed in bfloat16 or wider, within the bound.
A program may use at most 256 MiB of HBM per device.

v0:
```python
import math

import jax
import jax.numpy as jnp
from jax import lax
from jax.sharding import PartitionSpec as P

NORM_EPS = 1e-05


def normalize(values_in):
    row_mean = jnp.mean(values_in, -1, keepdims=True)
    centered = values_in - row_mean
    variance = jnp.mean(centered * centered, -1, keepdims=True)
    inv_std = lax.rsqrt(variance + NORM_EPS)
    return (centered * inv_std, inv_std)


def norm_back(grad_in, normed, inv_std, norm_gain):
    scaled = grad_in * norm_gain
    mean_scaled = jnp.mean(scaled, -1, keepdims=True)
    mean_mixed = jnp.mean(scaled * normed, -1, keepdims=True)
    return inv_std * (scaled - mean_scaled - normed * mean_mixed)


def across_rows(left_in, right_in):
    return lax.dot_general(
        left_in, right_in, (((0,), (0,)), ((), ())), preferred_element_type=jnp.float32
    )


def times_transposed(left_in, right_in):
    return lax.dot_general(
        left_in, right_in, (((1,), (1,)), ((), ())), preferred_element_type=jnp.float32
    )


def shards(
    layer_input,
    lengths,
    cotangent,
    ln1_gain,
    ln1_bias,
    w_query,
    b_query,
    w_kv,
    b_value,
    w_out,
    b_out,
    ln2_gain,
    ln2_bias,
    w_up,
    b_up,
    w_down,
    b_down,
):
    n_rows, seq_len, model_width = layer_input.shape
    share_len = seq_len // lax.axis_size("tensor")
    tensor_index = lax.axis_index("tensor")
    seq_index = lax.axis_index("seq")
    full_len = seq_len * lax.axis_size("seq")
    head_size = w_kv.shape[1] // 2
    num_heads = w_query.shape[1] // head_size
    q_scale = 1.0 / math.sqrt(head_size)

    def own_rows(values_in):
        return lax.dynamic_slice_in_dim(values_in, tensor_index * share_len, share_len, 1)

    positions = seq_index * seq_len + jnp.arange(seq_len, dtype=jnp.int32)
    key_places = jnp.arange(full_len, dtype=jnp.int32)
    is_valid = (positions[None, :] < lengths[:, None]).astype(jnp.float32)
    allowed_keys = (key_places[None, None, :] <= positions[None, :, None]) & (
        key_places[None, None, :] < lengths[:, None, None]
    )
    valid_own = own_rows(is_valid)
    x_float = layer_input.astype(jnp.float32)
    normed_x1, inv_one = normalize(x_float)
    normed_one = (normed_x1 * ln1_gain + ln1_bias).astype(jnp.bfloat16)
    flat_one = normed_one.reshape(n_rows * seq_len, model_width)
    queries = (
        (jnp.dot(flat_one, w_query, preferred_element_type=jnp.float32) + b_query) * q_scale
    ).astype(jnp.bfloat16)
    queries = queries.reshape(n_rows, seq_len, num_heads, head_size)
    kv_bias = jnp.concatenate([jnp.zeros((head_size,), jnp.float32), b_value.astype(jnp.float32)])
    kv_local = (jnp.dot(flat_one, w_kv, preferred_element_type=jnp.float32) + kv_bias).astype(
        jnp.bfloat16
    )
    kv_local = kv_local.reshape(n_rows, seq_len, 2 * head_size)
    kv_all = lax.all_gather(kv_local, "seq", axis=1, tiled=True)
    key_rows = kv_all[..., :head_size]
    value_rows = kv_all[..., head_size:]

    def scores_of(query_rows):
        raw_scores = jnp.einsum(
            "rshd,rld->rhsl", query_rows, key_rows, preferred_element_type=jnp.float32
        )
        return jnp.where(allowed_keys[:, None], raw_scores, -1e30)

    scores = scores_of(queries)
    row_max = jnp.max(scores, -1, keepdims=True)
    exp_scores = jnp.exp(scores - row_max)
    exp_total = jnp.sum(exp_scores, -1, keepdims=True)
    soft_probs = exp_scores / exp_total
    log_total = row_max + jnp.log(exp_total)
    mixed_heads = jnp.einsum(
        "rhsl,rld->rshd",
        soft_probs.astype(jnp.bfloat16),
        value_rows,
        preferred_element_type=jnp.float32,
    ).astype(jnp.bfloat16)
    mixed_heads = mixed_heads.reshape(n_rows * seq_len, num_heads * head_size)
    attn_part = jnp.dot(mixed_heads, w_out, preferred_element_type=jnp.float32).reshape(
        n_rows, seq_len, model_width
    )
    residual = x_float + (lax.psum(attn_part, "tensor") + b_out)
    normed_x2, inv_two = normalize(residual)
    normed_two = (normed_x2 * ln2_gain + ln2_bias).astype(jnp.bfloat16)
    resid_own = own_rows(residual)
    normed_x2_own = own_rows(normed_x2)
    flat_two = normed_two.reshape(n_rows * seq_len, model_width)
    pre_act = jnp.dot(flat_two, w_up, preferred_element_type=jnp.float32) + b_up
    activated, gelu_pull = jax.vjp(
        lambda inner_in: jax.nn.gelu(inner_in, approximate=True), pre_act
    )
    act_low = activated.astype(jnp.bfloat16)
    mlp_part = jnp.dot(act_low, w_down, preferred_element_type=jnp.float32).reshape(
        n_rows, seq_len, model_width
    )
    mlp_own = (
        lax.psum_scatter(
            mlp_part.astype(jnp.bfloat16), "tensor", scatter_dimension=1, tiled=True
        ).astype(jnp.float32)
        + b_down
    )
    y_own = (valid_own[..., None] * (resid_own + mlp_own)).astype(jnp.bfloat16)
    cot_full = lax.all_gather(cotangent, "tensor", axis=1, tiled=True)
    grad_y = cot_full.astype(jnp.float32) * is_valid[..., None]
    grad_y_low = grad_y.astype(jnp.bfloat16).reshape(n_rows * seq_len, model_width)
    grad_y_own = cotangent.astype(jnp.float32) * valid_own[..., None]
    g_w_down = across_rows(act_low, grad_y_low)
    grad_act = times_transposed(grad_y_low, w_down)
    grad_pre = gelu_pull(grad_act)[0].astype(jnp.bfloat16)
    g_w_up = across_rows(flat_two, grad_pre)
    g_b_up = jnp.sum(grad_pre.astype(jnp.float32), axis=0)
    grad_a2 = times_transposed(grad_pre, w_up).reshape(n_rows, seq_len, model_width)
    grad_n2 = lax.psum(grad_a2, "tensor")
    grad_resid = grad_y + norm_back(grad_n2, normed_x2, inv_two, ln2_gain)
    grad_resid_low = grad_resid.astype(jnp.bfloat16)
    grad_resid_own = own_rows(grad_resid)
    grad_n2_own = own_rows(grad_n2)
    grad_resid_own_low = own_rows(grad_resid_low)
    g_ln2_gain = jnp.sum(grad_n2_own * normed_x2_own, axis=(0, 1))
    g_ln2_bias = jnp.sum(grad_n2_own, axis=(0, 1))
    g_b_out = jnp.sum(grad_resid_own_low.astype(jnp.float32), axis=(0, 1))
    g_b_down = jnp.sum(grad_y_own, axis=(0, 1))
    flat_resid = grad_resid_low.reshape(n_rows * seq_len, model_width)
    g_w_out = across_rows(mixed_heads, flat_resid)
    grad_mixed = times_transposed(flat_resid, w_out).astype(jnp.bfloat16)
    grad_mixed = grad_mixed.reshape(n_rows, seq_len, num_heads, head_size)
    again_probs = jnp.exp(scores_of(queries) - log_total)
    grad_probs = jnp.einsum(
        "rshd,rld->rhsl", grad_mixed, value_rows, preferred_element_type=jnp.float32
    )
    inner_sum = jnp.sum(again_probs * grad_probs, -1, keepdims=True)
    grad_scores = (again_probs * (grad_probs - inner_sum)).astype(jnp.bfloat16)
    grad_query = jnp.einsum(
        "rhsl,rld->rshd", grad_scores, key_rows, preferred_element_type=jnp.float32
    ).astype(jnp.bfloat16)
    grad_keys = jnp.einsum(
        "rhsl,rshd->rld", grad_scores, queries, preferred_element_type=jnp.float32
    )
    grad_values = jnp.einsum(
        "rhsl,rshd->rld",
        again_probs.astype(jnp.bfloat16),
        grad_mixed,
        preferred_element_type=jnp.float32,
    )
    grad_kv = jnp.concatenate([grad_keys, grad_values], -1)
    grad_kv_own = lax.psum_scatter(
        grad_kv, ("seq", "tensor"), scatter_dimension=1, tiled=True
    ).astype(jnp.bfloat16)
    flat_query = grad_query.reshape(n_rows * seq_len, num_heads * head_size)
    g_w_query = across_rows(flat_one, flat_query) * q_scale
    g_b_query = jnp.sum(flat_query.astype(jnp.float32), axis=0) * q_scale
    grad_n1_part = (times_transposed(flat_query, w_query) * q_scale).reshape(
        n_rows, seq_len, model_width
    )
    grad_n1_own = lax.psum_scatter(
        grad_n1_part.astype(jnp.bfloat16), "tensor", scatter_dimension=1, tiled=True
    ).astype(jnp.float32)
    flat_kv = grad_kv_own.reshape(n_rows * share_len, 2 * head_size)
    grad_n1_own = grad_n1_own + times_transposed(flat_kv, w_kv).reshape(
        n_rows, share_len, model_width
    )
    one_own = own_rows(normed_one).reshape(n_rows * share_len, model_width)
    g_w_kv = across_rows(one_own, flat_kv)
    g_b_value = jnp.sum(flat_kv[:, head_size:].astype(jnp.float32), axis=0)
    normed_x1_own = own_rows(normed_x1)
    x_grad_own = grad_resid_own + norm_back(grad_n1_own, normed_x1_own, own_rows(inv_one), ln1_gain)
    g_ln1_gain = jnp.sum(grad_n1_own * normed_x1_own, axis=(0, 1))
    g_ln1_bias = jnp.sum(grad_n1_own, axis=(0, 1))
    query_table = g_b_query.reshape(num_heads, head_size)
    up_table = g_b_up.reshape(-1, 128)
    summed = (
        lax.psum_scatter(g_w_query, ("dp", "seq"), scatter_dimension=0, tiled=True),
        lax.psum_scatter(query_table, ("dp", "seq"), scatter_dimension=1, tiled=True),
        lax.psum_scatter(g_w_out, ("dp", "seq"), scatter_dimension=1, tiled=True),
        lax.psum_scatter(g_w_up, ("dp", "seq"), scatter_dimension=0, tiled=True),
        lax.psum_scatter(up_table, ("dp", "seq"), scatter_dimension=1, tiled=True),
        lax.psum_scatter(g_w_down, ("dp", "seq"), scatter_dimension=1, tiled=True),
    )
    small_grads = jnp.stack([g_ln1_gain, g_ln1_bias, g_ln2_gain, g_ln2_bias, g_b_out, g_b_down])
    shared = (
        lax.psum_scatter(g_w_kv, ("dp", "seq", "tensor"), scatter_dimension=0, tiled=True),
        lax.psum_scatter(small_grads, ("dp", "seq", "tensor"), scatter_dimension=1, tiled=True),
        lax.psum_scatter(g_b_value, ("dp", "seq", "tensor"), scatter_dimension=0, tiled=True),
    )
    return (
        y_own,
        x_grad_own,
        summed[0],
        summed[1],
        shared[0],
        shared[2],
        summed[2],
        summed[3],
        summed[4],
        summed[5],
        shared[1],
    )


def solution(mesh):
    placed = (
        P("dp", "seq", None),
        P("dp"),
        P("dp", ("seq", "tensor"), None),
        P(),
        P(),
        P(None, "tensor"),
        P("tensor"),
        P(),
        P(),
        P("tensor", None),
        P(),
        P(),
        P(),
        P(None, "tensor"),
        P("tensor"),
        P("tensor", None),
        P(),
    )
    return jax.shard_map(
        shards,
        mesh=mesh,
        in_specs=placed,
        out_specs=(
            P("dp", ("seq", "tensor"), None),
            P("dp", ("seq", "tensor"), None),
            P(("dp", "seq"), "tensor"),
            P("tensor", ("dp", "seq")),
            P(("dp", "seq", "tensor"), None),
            P(("dp", "seq", "tensor")),
            P("tensor", ("dp", "seq")),
            P(("dp", "seq"), "tensor"),
            P("tensor", ("dp", "seq")),
            P("tensor", ("dp", "seq")),
            P(None, ("dp", "seq", "tensor")),
        ),
        check_vma=False,
    )
```

profile of v0, /device:TPU:0, one launch (start us, length us, event | category | flops | bytes accessed | tf_op | source)
XLA Modules:
  0.0 1648.8 jit_solution(9399819819224728491)
XLA Ops:
  8.1 2.6 convert_reduce_fusion
  10.7 2.9 fusion.8
  13.7 3.3 fusion.6
  21.5 5.2 multiply_convert_fusion.3
  30.5 29.8 %all-gather.3.cloned.1.call-done = bf16[3,1024,256]{2,1,0:T(8,128)(2,1)} async-done(((bf16[3,256,256]{2,1,0:T(8,128)(2,1)}), bf16[3,1024,256]{2,1,0:T(8,128)(2,1)}) %all-gather.3.cloned.1.call-update) | async-done | bytes 1572880 | tf_op jit(solution)/shard_map/all_gather | solution.py:89
  60.4 7.9 fusion.4
  68.3 7.4 fusion.3
  75.8 6.5 fusion.28
  83.2 4.4 fusion.23
  89.3 4.1 fusion.19
  93.4 117.9 %all-reduce.7.cloned.1.call-done = f32[3,256,2048]{2,1,0:T(8,128)} async-done(((f32[3,256,2048]{2,1,0:T(8,128)}), f32[3,256,2048]{2,1,0:T(8,128)}) %all-reduce.7.cloned.1.call-update) | async-done | bytes 6291472 | tf_op jit(solution)/shard_map/psum | solution.py:115
  211.3 4.6 fusion.48
  216.8 4.1 add_convert_fusion
  222.1 2.8 slice-done.1
  224.9 8.5 fusion.49
  233.4 14.9 convert_reduce_fusion.1
  248.3 8.6 fusion.50
  257.0 13.3 convolution_convert_fusion
  270.3 106.6 %all-reduce.9.cloned.1.call-done = f32[3,256,2048]{2,1,0:T(8,128)} async-done(((f32[3,256,2048]{2,1,0:T(8,128)}), f32[3,256,2048]{2,1,0:T(8,128)}) %all-reduce.9.cloned.1.call-update) | async-done | bytes 6291472 | tf_op jit(solution)/shard_map/psum | solution.py:146
  376.9 5.9 multiply_reduce_fusion.2
  384.2 6.1 fusion.47
  391.9 2.8 convolution_convert_fusion.1
  394.7 2.4 reshape.237
  399.3 8.6 fusion
  407.9 6.7 fusion.2
  414.7 2.7 copy-done.2
  419.4 2.2 copy.64
  421.6 5.3 multiply_convert_fusion
  429.4 9.6 fusion.25
  439.0 6.1 convolution_bitcast_fusion.1
  445.8 4.0 pad_maximum_fusion
  449.8 5.0 copy.69
  454.8 98.2 %all-reduce.10 = bf16[3,1024,256]{2,0,1:T(4,128)(2,1)} all-reduce(f32[3,1024,256]{2,0,1:T(4,128)} %copy.69), channel_id=4, replica_groups=mesh['dp'=2,'seq'=4,'tensor'=4] {'seq','tensor'}, use_global_device_ids=true, to_apply=%region_13.14.clone | all-reduce | flops 786432 | bytes 4718592
  557.5 3.0 multiply_reduce_fusion.3
  560.5 3.9 multiply_reduce_fusion.5
  565.8 3.0 convolution_bitcast_fusion
  570.2 6.0 fusion.32
  576.3 5.7 convolution_multiply_fusion
  582.3 13.9 fusion.45
  596.3 12.5 fusion.51
  611.0 40.6 %all-reduce.2 = f32[128]{0:T(128)S(1)} all-reduce(f32[128]{0:T(128)S(1)} %convert_reduce_fusion.4), channel_id=8, replica_groups=mesh['dp'=2,'seq'=4,'tensor'=4] {'dp','seq','tensor'}, use_global_device_ids=true, to_apply=%region_21.22.clone | all-reduce | flops 128 | bytes 1024
  653.6 3.9 multiply_add_fusion.1
  657.5 99.5 %reduce-scatter.35.cloned.1.call-done = f32[64,6]{1,0:T(8,128)} async-done(((f32[2048,6]{1,0:T(8,128)}), f32[64,6]{1,0:T(8,128)}) %reduce-scatter.35.cloned.1.call-update) | async-done | bytes 1552
  758.4 135.5 %reduce-scatter.23.cloned.1.call-done = f32[64,256]{1,0:T(8,128)} async-done(((f32[2048,256]{1,0:T(8,128)}), f32[64,256]{1,0:T(8,128)}) %reduce-scatter.23.cloned.1.call-update) | async-done | bytes 65552 | tf_op jit(solution)/shard_map/reduce_scatter | solution.py:214
  893.9 89.4 %reduce-scatter.25.cloned.1.call-done = f32[512,256]{1,0:T(8,128)} async-done(((f32[512,2048]{1,0:T(8,128)}), f32[512,256]{1,0:T(8,128)}) %reduce-scatter.25.cloned.1.call-update) | async-done | bytes 524304 | tf_op jit(solution)/shard_map/reduce_scatter | solution.py:207
  983.4 92.0 %reduce-scatter.21.cloned.1.call-done = f32[256,512]{1,0:T(8,128)} async-done(((f32[2048,512]{1,0:T(8,128)}), f32[256,512]{1,0:T(8,128)}) %reduce-scatter.21.cloned.1.call-update) | async-done | bytes 524304 | tf_op jit(solution)/shard_map/reduce_scatter | solution.py:205
  1075.4 283.5 %reduce-scatter.29.cloned.1.call-done = f32[2048,256]{1,0:T(8,128)} async-done(((f32[2048,2048]{1,0:T(8,128)}), f32[2048,256]{1,0:T(8,128)}) %reduce-scatter.29.cloned.1.call-update) | async-done | bytes 2097168 | tf_op jit(solution)/shard_map/reduce_scatter | solution.py:210
  1358.9 282.9 %reduce-scatter.27.cloned.1.call-done = f32[256,2048]{1,0:T(8,128)} async-done(((f32[2048,2048]{1,0:T(8,128)}), f32[256,2048]{1,0:T(8,128)}) %reduce-scatter.27.cloned.1.call-update) | async-done | bytes 2097168 | tf_op jit(solution)/shard_map/reduce_scatter | solution.py:208
  (148 shorter events, 36.8 us)
Async XLA Ops:
  7.2 76.0 %copy-start = (bf16[512,2048]{1,0:T(8,128)(2,1)S(1)}, bf16[512,2048]{1,0:T(8,128)(2,1)}, u32[]{:S(2)}) copy-start(bf16[512,2048]{1,0:T(8,128)(2,1)} %param.26) | copy-start | bytes 6291460
  7.2 6.4 copy-start.22
  7.2 6.4 copy-start.23
  7.2 53.2 %all-gather.3.cloned.1.call-start = ((), (), s32[]{:S(2)}) async-start(), calls=%async_computation.10 | async-start | bytes 1966080 | tf_op jit(solution)/shard_map/all_gather | solution.py:89
  7.3 6.4 copy-start.3
  13.6 3.4 copy-start.20
  13.6 3.4 copy-start.18
  13.7 5.0 copy-start.16
  17.0 1.7 copy-start.8
  17.0 4.5 copy-start.30
  20.5 68.9 %all-gather.5.cloned.1.call-start = ((), (), s32[]{:S(2)}) async-start(), calls=%async_computation.13 | async-start | bytes 3932160 | tf_op jit(solution)/shard_map/all_gather | solution.py:136
  21.2 190.1 %all-reduce.7.cloned.1.call-start = ((), (), s32[]{:S(2)}) async-start(), calls=%async_computation.11 | async-start | bytes 12582912 | tf_op jit(solution)/shard_map/psum | solution.py:115
  21.5 8.2 copy-start.29
  68.3 7.5 copy-start.9
  82.3 0.9 copy-start.11
  83.2 4.5 copy-start.24
  83.2 4.5 copy-start.25
  83.2 4.6 copy-start.26
  83.2 4.6 copy-start.27
  87.7 289.2 %all-reduce.9.cloned.1.call-start = ((), (), s32[]{:S(2)}) async-start(), calls=%async_computation.14 | async-start | bytes 12582912 | tf_op jit(solution)/shard_map/psum | solution.py:146
  215.9 6.2 copy-start.1
  216.0 6.2 slice-start
  216.7 8.2 slice-start.1
  222.1 11.3 copy-start.14
  224.9 8.5 copy-start.13
  248.3 8.6 copy-start.32
  256.9 300.6 %reduce-scatter.17.cloned.1.call-start = ((), (), s32[]{:S(2)}) async-start(), calls=%async_computation.12 | async-start | bytes 3932160 | tf_op jit(solution)/shard_map/reduce_scatter | solution.py:130
  270.2 290.2 %reduce-scatter.19.cloned.1.call-start = ((), (), s32[]{:S(2)}) async-start(), calls=%async_computation.15 | async-start | bytes 3932160 | tf_op jit(solution)/shard_map/reduce_scatter | solution.py:188
  376.9 6.4 copy-start.4
  376.9 7.3 copy-start.6
  390.3 1.6 copy-start.5
  407.9 9.5 copy-start.10
  414.7 2.8 copy-start.2
  421.6 5.4 copy-start.28
  421.6 5.4 copy-start.31
  426.9 182.6 %reduce-scatter.33.cloned.1.call-start = ((), (), s32[]{:S(2)}) async-start(), calls=%async_computation.22 | async-start | bytes 73728
  429.1 223.1 %reduce-scatter.31.cloned.1.call-start = ((), (), s32[]{:S(2)}) async-start(), calls=%async_computation.21 | async-start | bytes 73728
  429.4 9.6 copy-start.7
  454.8 102.7 %copy-start.15 = (bf16[3,64,2048]{2,1,0:T(8,128)(2,1)S(1)}, bf16[3,64,2048]{2,1,0:T(8,128)(2,1)}, u32[]{:S(2)}) copy-start(bf16[3,64,2048]{2,1,0:T(8,128)(2,1)} %param.19) | copy-start | bytes 2359300
  454.8 105.7 %copy-start.19 = (f32[2048]{0:T(1024)S(1)}, f32[2048]{0:T(1024)}, u32[]{:S(2)}) copy-start(f32[2048]{0:T(1024)} %copy-done.18) | copy-start | bytes 24580
  555.3 201.7 %reduce-scatter.35.cloned.1.call-start = ((), (), s32[]{:S(2)}) async-start(), calls=%async_computation.23 | async-start | bytes 1081344
  560.5 8.4 copy-start.12
  565.8 328.1 %reduce-scatter.23.cloned.1.call-start = ((), (), s32[]{:S(2)}) async-start(), calls=%async_computation.17 | async-start | bytes 2162688 | tf_op jit(solution)/shard_map/reduce_scatter | solution.py:214
  568.8 414.5 %reduce-scatter.25.cloned.1.call-start = ((), (), s32[]{:S(2)}) async-start(), calls=%async_computation.18 | async-start | bytes 4718592 | tf_op jit(solution)/shard_map/reduce_scatter | solution.py:207
  570.2 6.1 copy-start.17
  576.2 499.1 %reduce-scatter.21.cloned.1.call-start = ((), (), s32[]{:S(2)}) async-start(), calls=%async_computation.16 | async-start | bytes 4718592 | tf_op jit(solution)/shard_map/reduce_scatter | solution.py:205
  582.0 776.9 %reduce-scatter.29.cloned.1.call-start = ((), (), s32[]{:S(2)}) async-start(), calls=%async_computation.20 | async-start | bytes 18874368 | tf_op jit(solution)/shard_map/reduce_scatter | solution.py:210
  596.2 1045.5 %reduce-scatter.27.cloned.1.call-start = ((), (), s32[]{:S(2)}) async-start(), calls=%async_computation.19 | async-start | bytes 18874368 | tf_op jit(solution)/shard_map/reduce_scatter | solution.py:208
  (1 other events, 0.7 us)
Sparse Core Ops, SparseCore 0:
  20.6 39.7 all-gather.2
  61.9 27.3 all-gather.4
  91.7 119.5 all-reduce.6
  257.0 119.7 all-reduce.8
  379.2 37.9 reduce-scatter.16
  427.1 42.3 reduce-scatter.18
  472.9 66.0 reduce-scatter.32
  555.4 63.4 reduce-scatter.30
  621.2 135.7 reduce-scatter.34
  759.7 134.2 reduce-scatter.22
  898.2 85.1 reduce-scatter.24
  987.4 87.9 reduce-scatter.20
  1079.7 279.1 reduce-scatter.28
  1363.1 278.6 reduce-scatter.26
where the time goes:
time: 1650 us
  waiting for transfers between devices  1240 us (75%)
  matrix products  150 us (9%)
  blocking collectives  139 us (8%)
  other arithmetic  64.6 us (4%)
  local copies, waits for them, and re-layouts  38.7 us (2%)
    reduce_scatter x1, waiting for transfers between devices, shards(): lax.psum_scatter(g_w_down, ('dp', 'seq'), scatter_dimension=1, tiled=True)  284 us
    reduce_scatter x1, waiting for transfers between devices, shards(): lax.psum_scatter(g_w_up, ('dp', 'seq'), scatter_dimension=0, tiled=True)  283 us
    unnamed x2, blocking collectives  139 us
    reduce_scatter x1, waiting for transfers between devices, shards(): lax.psum_scatter(g_w_kv, ('dp', 'seq', 'tensor'), scatter_dimension=0, ti...  136 us
    psum x1, waiting for transfers between devices, shards(): residual = x_float + (lax.psum(attn_part, 'tensor') + b_out)  118 us
    psum x1, waiting for transfers between devices, shards(): grad_n2 = lax.psum(grad_a2, 'tensor')  107 us
    unnamed x17, waiting for transfers between devices  100 us
    reduce_scatter x1, waiting for transfers between devices, shards(): lax.psum_scatter(g_w_query, ('dp', 'seq'), scatter_dimension=0, tiled=True)  92 us
  transfers between devices with their start and end apart: 14, of which 10 were waited for; matrix products, arithmetic and copies ran while one was open for 11% of the time, Pallas kernels for 0%

commit v1 on v0

v1 whole, which is shorter than its diff:
```python
import math

import jax
import jax.numpy as jnp
from jax import lax
from jax.sharding import PartitionSpec as P

NORM_EPS = 1e-05
BF16 = jnp.bfloat16
F32 = jnp.float32


def normalize(values_in):
    row_mean = jnp.mean(values_in, -1, keepdims=True)
    centered = values_in - row_mean
    variance = jnp.mean(centered * centered, -1, keepdims=True)
    inv_std = lax.rsqrt(variance + NORM_EPS)
    return (centered * inv_std, inv_std)


def norm_back(grad_in, normed, inv_std, norm_gain):
    scaled = grad_in * norm_gain
    mean_scaled = jnp.mean(scaled, -1, keepdims=True)
    mean_mixed = jnp.mean(scaled * normed, -1, keepdims=True)
    return inv_std * (scaled - mean_scaled - normed * mean_mixed)


def across_rows(left_in, right_in):
    return lax.dot_general(left_in, right_in, (((0,), (0,)), ((), ())), preferred_element_type=F32)


def times_transposed(left_in, right_in):
    return lax.dot_general(left_in, right_in, (((1,), (1,)), ((), ())), preferred_element_type=F32)


def dp_exchange(part_for):
    n_dp = lax.axis_size("dp")
    me = lax.axis_index("dp")
    arrived = []
    for k in range(1, n_dp):
        target = lax.rem(me + k, n_dp)
        pairs = [(i, (i + k) % n_dp) for i in range(n_dp)]
        arrived.append(lax.ppermute(part_for(target).astype(BF16), "dp", pairs))
    total = part_for(me)
    for piece in arrived:
        total = total + piece.astype(F32)
    return total


def two_stage(part_for, dim):
    total = dp_exchange(part_for)
    return lax.psum_scatter(total.astype(BF16), "seq", scatter_dimension=dim, tiled=True).astype(F32)


def shards(
    layer_input,
    lengths,
    cotangent,
    ln1_gain,
    ln1_bias,
    w_query,
    b_query,
    w_kv,
    b_value,
    w_out,
    b_out,
    ln2_gain,
    ln2_bias,
    w_up,
    b_up,
    w_down,
    b_down,
):
    n_rows, seq_len, model_width = layer_input.shape
    n_tensor = lax.axis_size("tensor")
    n_dp = lax.axis_size("dp")
    n_seq = lax.axis_size("seq")
    share_len = seq_len // n_tensor
    tensor_index = lax.axis_index("tensor")
    seq_index = lax.axis_index("seq")
    full_len = seq_len * n_seq
    head_size = w_kv.shape[1] // 2
    num_heads = w_query.shape[1] // head_size
    q_scale = 1.0 / math.sqrt(head_size)
    n_tok = n_rows * seq_len
    n_own = n_rows * share_len

    def own_rows(values_in):
        return lax.dynamic_slice_in_dim(values_in, tensor_index * share_len, share_len, 1)

    def gather_own(values_in):
        return lax.all_gather(values_in, "tensor", axis=1, tiled=True)

    def scatter_own(values_in):
        return lax.psum_scatter(
            values_in.astype(BF16).reshape(n_rows, seq_len, model_width), "tensor", scatter_dimension=1, tiled=True
        ).astype(F32)

    positions = seq_index * seq_len + jnp.arange(seq_len, dtype=jnp.int32)
    key_places = jnp.arange(full_len, dtype=jnp.int32)
    is_valid = (positions[None, :] < lengths[:, None]).astype(F32)
    allowed_keys = (key_places[None, None, :] <= positions[None, :, None]) & (
        key_places[None, None, :] < lengths[:, None, None]
    )
    valid_own = own_rows(is_valid)
    x_float = layer_input.astype(F32)
    normed_x1, inv_one = normalize(x_float)
    normed_one = (normed_x1 * ln1_gain + ln1_bias).astype(BF16)
    flat_one = normed_one.reshape(n_tok, model_width)
    kv_bias = jnp.concatenate([jnp.zeros((head_size,), F32), b_value.astype(F32)])
    kv_local = (jnp.dot(flat_one, w_kv, preferred_element_type=F32) + kv_bias).astype(BF16)
    kv_local = kv_local.reshape(n_rows, seq_len, 2 * head_size)
    kv_all = lax.all_gather(kv_local, "seq", axis=1, tiled=True)
    queries = ((jnp.dot(flat_one, w_query, preferred_element_type=F32) + b_query) * q_scale).astype(BF16)
    queries = queries.reshape(n_rows, seq_len, num_heads, head_size)
    key_rows = kv_all[..., :head_size]
    value_rows = kv_all[..., head_size:]
    grad_y_own = cotangent.astype(F32) * valid_own[..., None]
    grad_y_low = gather_own(grad_y_own.astype(BF16)).reshape(n_tok, model_width)

    def scores_of(query_rows):
        raw_scores = jnp.einsum("rshd,rld->rhsl", query_rows, key_rows, preferred_element_type=F32)
        return jnp.where(allowed_keys[:, None], raw_scores, -1e30)

    scores = scores_of(queries)
    row_max = jnp.max(scores, -1, keepdims=True)
    exp_scores = jnp.exp(scores - row_max)
    exp_total = jnp.sum(exp_scores, -1, keepdims=True)
    soft_probs = exp_scores / exp_total
    log_total = row_max + jnp.log(exp_total)
    mixed_heads = jnp.einsum(
        "rhsl,rld->rshd", soft_probs.astype(BF16), value_rows, preferred_element_type=F32
    ).astype(BF16)
    mixed_heads = mixed_heads.reshape(n_tok, num_heads * head_size)
    attn_own = scatter_own(jnp.dot(mixed_heads, w_out, preferred_element_type=F32))
    x_own = own_rows(x_float)
    resid_own = x_own + (attn_own + b_out)
    normed_x2, inv_two = normalize(resid_own)
    normed_two = (normed_x2 * ln2_gain + ln2_bias).astype(BF16)
    flat_two = gather_own(normed_two).reshape(n_tok, model_width)
    pre_act = jnp.dot(flat_two, w_up, preferred_element_type=F32) + b_up
    activated, gelu_pull = jax.vjp(lambda inner_in: jax.nn.gelu(inner_in, approximate=True), pre_act)
    act_low = activated.astype(BF16)
    grad_act = times_transposed(grad_y_low, w_down)
    grad_pre = gelu_pull(grad_act)[0].astype(BF16)

    half_width = model_width // n_dp

    def columns(values_in, d):
        return lax.dynamic_slice_in_dim(values_in, d * half_width, half_width, 1)

    grad_n2 = scatter_own(times_transposed(grad_pre, w_up))
    g_w_down = two_stage(lambda d: across_rows(act_low, columns(grad_y_low, d)), 1)
    g_w_up = two_stage(lambda d: across_rows(columns(flat_two, d), grad_pre), 0)
    g_b_up = jnp.sum(grad_pre.astype(F32), axis=0)
    mlp_own = scatter_own(jnp.dot(act_low, w_down, preferred_element_type=F32)) + b_down
    y_own = (valid_own[..., None] * (resid_own + mlp_own)).astype(BF16)
    grad_resid = grad_y_own + norm_back(grad_n2, normed_x2, inv_two, ln2_gain)
    grad_resid_low = grad_resid.astype(BF16)
    flat_resid = gather_own(grad_resid_low).reshape(n_tok, model_width)
    g_ln2_gain = jnp.sum(grad_n2 * normed_x2, axis=(0, 1))
    g_ln2_bias = jnp.sum(grad_n2, axis=(0, 1))
    g_b_out = jnp.sum(grad_resid_low.astype(F32), axis=(0, 1))
    g_b_down = jnp.sum(grad_y_own, axis=(0, 1))
    g_w_out = two_stage(lambda d: across_rows(mixed_heads, columns(flat_resid, d)), 1)
    grad_mixed = times_transposed(flat_resid, w_out).astype(BF16)
    grad_mixed = grad_mixed.reshape(n_rows, seq_len, num_heads, head_size)
    again_probs = jnp.exp(scores_of(queries) - log_total)
    grad_probs = jnp.einsum("rshd,rld->rhsl", grad_mixed, value_rows, preferred_element_type=F32)
    inner_sum = jnp.sum(again_probs * grad_probs, -1, keepdims=True)
    grad_scores = (again_probs * (grad_probs - inner_sum)).astype(BF16)
    grad_query = jnp.einsum("rhsl,rld->rshd", grad_scores, key_rows, preferred_element_type=F32).astype(BF16)
    grad_keys = jnp.einsum("rhsl,rshd->rld", grad_scores, queries, preferred_element_type=F32)
    grad_values = jnp.einsum(
        "rhsl,rshd->rld", again_probs.astype(BF16), grad_mixed, preferred_element_type=F32
    )
    grad_kv = jnp.concatenate([grad_keys, grad_values], -1)
    grad_kv_own = lax.psum_scatter(
        grad_kv.astype(BF16), "seq", scatter_dimension=1, tiled=True
    )
    grad_kv_own = lax.psum_scatter(grad_kv_own, "tensor", scatter_dimension=1, tiled=True)
    flat_query = grad_query.reshape(n_tok, num_heads * head_size)
    g_b_query = jnp.sum(flat_query.astype(F32), axis=0) * q_scale
    grad_n1 = scatter_own(times_transposed(flat_query, w_query) * q_scale)
    g_w_query = two_stage(lambda d: across_rows(columns(flat_one, d), flat_query) * q_scale, 0)
    flat_kv = grad_kv_own.reshape(n_own, 2 * head_size)
    grad_n1 = grad_n1 + times_transposed(flat_kv, w_kv).reshape(n_rows, share_len, model_width)
    one_own = own_rows(normed_one).reshape(n_own, model_width)
    g_w_kv = across_rows(one_own, flat_kv)
    g_b_value = jnp.sum(flat_kv[:, head_size:].astype(F32), axis=0)
    normed_x1_own = own_rows(normed_x1)
    x_grad_own = grad_resid + norm_back(grad_n1, normed_x1_own, own_rows(inv_one), ln1_gain)
    g_ln1_gain = jnp.sum(grad_n1 * normed_x1_own, axis=(0, 1))
    g_ln1_bias = jnp.sum(grad_n1, axis=(0, 1))
    owners = n_dp * n_seq
    small = jnp.stack([g_ln1_gain, g_ln1_bias, g_ln2_gain, g_ln2_bias, g_b_out, g_b_down])
    kv_piece = g_w_kv.reshape(owners, n_tensor, -1)
    small_width = model_width // (owners * n_tensor)
    small_piece = jnp.moveaxis(small.reshape(6, owners, n_tensor, small_width), 0, 2).reshape(owners, n_tensor, -1)
    value_piece = g_b_value.reshape(owners, n_tensor, -1)
    packed = jnp.concatenate([kv_piece, small_piece, value_piece], -1)
    packed = lax.psum_scatter(packed.astype(BF16), "tensor", scatter_dimension=1, tiled=True).astype(F32)[:, 0]
    query_table = jnp.moveaxis(g_b_query.reshape(num_heads, owners, -1), 1, 0).reshape(owners, -1)
    up_table = jnp.moveaxis(g_b_up.reshape(-1, owners, 128 // owners), 1, 0).reshape(owners, -1)
    packed = jnp.concatenate([packed, query_table, up_table], -1)
    packed = lax.psum_scatter(packed.astype(BF16), ("dp", "seq"), scatter_dimension=0, tiled=True).astype(F32)[0]
    sizes = [kv_piece.shape[-1], small_piece.shape[-1], value_piece.shape[-1], query_table.shape[-1], up_table.shape[-1]]
    ends = [sum(sizes[: i + 1]) for i in range(len(sizes))]
    kv_out, small_out, value_out, query_out, up_out = [packed[e - s : e] for s, e in zip(sizes, ends)]
    return (
        y_own,
        x_grad_own,
        g_w_query,
        query_out.reshape(num_heads, -1),
        kv_out.reshape(-1, 2 * head_size),
        value_out,
        g_w_out,
        g_w_up,
        up_out.reshape(-1, 128 // owners),
        g_w_down,
        small_out.reshape(6, -1),
    )


def solution(mesh):
    placed = (
        P("dp", "seq", None),
        P("dp"),
        P("dp", ("seq", "tensor"), None),
        P(),
        P(),
        P(None, "tensor"),
        P("tensor"),
        P(),
        P(),
        P("tensor", None),
        P(),
        P(),
        P(),
        P(None, "tensor"),
        P("tensor"),
        P("tensor", None),
        P(),
    )
    return jax.shard_map(
        shards,
        mesh=mesh,
        in_specs=placed,
        out_specs=(
            P("dp", ("seq", "tensor"), None),
            P("dp", ("seq", "tensor"), None),
            P(("dp", "seq"), "tensor"),
            P("tensor", ("dp", "seq")),
            P(("dp", "seq", "tensor"), None),
            P(("dp", "seq", "tensor")),
            P("tensor", ("dp", "seq")),
            P(("dp", "seq"), "tensor"),
            P("tensor", ("dp", "seq")),
            P("tensor", ("dp", "seq")),
            P(None, ("dp", "seq", "tensor")),
        ),
        check_vma=False,
    )
```

time: 1650 us -> 812 us (0.49)
  waiting for transfers between devices: 1240 us -> 548 us
  blocking collectives: 139 us -> 0 us
    reduce_scatter x7 -> x10, waiting for transfers between devices: 883 us -> 236 us  [the longest x4 138 us: scatter_own(): lax.psum_scatter(values_in.astype(BF16).reshape(n_rows, seq_len, model_wi...]
    psum x2 -> x0, waiting for transfers between devices: 224 us -> none  [the longest x1 118 us: shards(): residual = x_float + (lax.psum(attn_part, 'tensor') + b_out)]
    unnamed x2 -> x0, blocking collectives: 139 us -> none
    ppermute x0 -> x4, waiting for transfers between devices: none -> 135 us  [dp_exchange(): arrived.append(lax.ppermute(part_for(target).astype(BF16), 'dp', pairs))]
    all_gather x1 -> x3, waiting for transfers between devices: 1.47 us -> 70.7 us  [gather_own(): return lax.all_gather(values_in, 'tensor', axis=1, tiled=True)]
    unnamed x17 -> x18, waiting for transfers between devices: 100 us -> 75.7 us
    unnamed x79 -> x84, local copies, waits for them, and re-layouts: 22.3 us -> 5.28 us
    dot_general x5 -> x9, matrix products: 41.1 us -> 38.9 us  [across_rows(): lax.dot_general(left_in, right_in, (((0,), (0,)), ((), ())), preferred_el...]
  transfers between devices with their start and end apart: 14 -> 20, of which waited for: 10 -> 17; matrix products, arithmetic and copies ran while one was open for 11% -> 15% of each run, Pallas kernels for 0% -> 0%
where the time goes in v1:
time: 812 us; the launch traced here: 808 us
  waiting for transfers between devices  548 us (67%)
  matrix products  152 us (19%)
  other arithmetic  57.5 us (7%)
  local copies, waits for them, and re-layouts  27.2 us (3%)
  between operations  15.4 us (2%)
  starting transfers between devices  8.14 us (1%)
    reduce_scatter x4, waiting for transfers between devices, scatter_own(): lax.psum_scatter(values_in.astype(BF16).reshape(n_rows, seq_len, model_wi...  138 us
    ppermute x4, waiting for transfers between devices, dp_exchange(): arrived.append(lax.ppermute(part_for(target).astype(BF16), 'dp', pairs))  135 us
    unnamed x18, waiting for transfers between devices  75.7 us
    all_gather x3, waiting for transfers between devices, gather_own(): return lax.all_gather(values_in, 'tensor', axis=1, tiled=True)  70.7 us
    reduce_scatter x4, waiting for transfers between devices, two_stage(): lax.psum_scatter(total.astype(BF16), 'seq', scatter_dimension=dim, tiled=...  67.2 us
    dot_general x5, matrix products, times_transposed(): lax.dot_general(left_in, right_in, (((1,), (1,)), ((), ())), preferred_el...  39.6 us
    dot_general x9, matrix products, across_rows(): lax.dot_general(left_in, right_in, (((0,), (0,)), ((), ())), preferred_el...  38.9 us
    reduce_scatter x1, waiting for transfers between devices, shards(): lax.psum_scatter(grad_kv.astype(BF16), 'seq', scatter_dimension=1, tiled=...  30.9 us
  transfers between devices with their start and end apart: 20, of which 17 were waited for; matrix products, arithmetic and copies ran while one was open for 15% of the time, Pallas kernels for 0%

profile of v1, /device:TPU:0, one launch (start us, length us, event | category | flops | bytes accessed | tf_op | source)
XLA Modules:
  0.0 807.9 jit_solution(13666337548137846042)
XLA Ops:
  7.3 2.5 convert_reduce_fusion
  11.3 3.4 subtract_multiply_fusion
  16.8 5.2 multiply_convert_fusion.4
  25.8 30.6 %all-gather.5.cloned.1.call-done = bf16[3,1024,256]{2,1,0:T(8,128)(2,1)} async-done(((bf16[3,256,256]{2,1,0:T(8,128)(2,1)}), bf16[3,1024,256]{2,1,0:T(8,128)(2,1)}) %all-gather.5.cloned.1.call-update) | async-done | bytes 1572880 | tf_op jit(solution)/shard_map/all_gather | solution.py:113
  56.4 7.7 fusion.4
  64.1 7.0 fusion.3
  71.1 7.3 fusion.55
  80.6 4.6 convolution_convert_fusion.4
  85.3 5.4 convert_element_type.180
  90.7 31.3 %reduce-scatter.11.cloned.1.call-done = bf16[3,64,2048]{2,1,0:T(8,128)(2,1)} async-done(((bf16[3,256,2048]{2,1,0:T(8,128)(2,1)}), bf16[3,64,2048]{2,1,0:T(8,128)(2,1)}) %reduce-scatter.11.cloned.1.call-update) | async-done | bytes 786448 | tf_op jit(solution)/shard_map/reduce_scatter | solution.py:95
  129.3 25.8 %all-gather.7.cloned.1.call-done = bf16[3,256,2048]{2,1,0:T(8,128)(2,1)} async-done(((bf16[3,64,2048]{2,1,0:T(8,128)(2,1)}), bf16[3,256,2048]{2,1,0:T(8,128)(2,1)}) %all-gather.7.cloned.1.call-update) | async-done | bytes 3145744 | tf_op jit(solution)/shard_map/all_gather | solution.py:92
  155.0 14.2 %multiply_convert_fusion.1 = (bf16[768,2048]{1,0:T(8,128)(2,1)}, f32[768,2048]{1,0:T(8,128)}) fusion(f32[2048]{0:T(1024)S(1)} %convert_element_type.196, bf16[768,2048]{1,0:T(8,128)(2,1)} %bitcast.168, bf16[2048,2048]{1,0:T(8,128)(2,1)} %param.30), kind=kOutput, calls=%fused_computation.26 | convolution fusion | flops 6458179584 | bytes 20979712 | tf_op jit(solution)/shard_map/dot_general | solution.py:141
  169.2 16.3 %all-gather.9.cloned.1.call-done = bf16[3,256,2048]{2,1,0:T(8,128)(2,1)} async-done(((bf16[3,64,2048]{2,1,0:T(8,128)(2,1)}), bf16[3,256,2048]{2,1,0:T(8,128)(2,1)}) %all-gather.9.cloned.1.call-update) | async-done | bytes 3145744 | tf_op jit(solution)/shard_map/all_gather | solution.py:92
  185.5 14.7 %fusion.85 = (bf16[2048]{0:T(1024)(128)(2,1)S(1)}, bf16[768,2048]{1,0:T(8,128)(2,1)S(1)}) fusion(f32[768,2048]{1,0:T(8,128)} %get-tuple-element.36, f32[2048]{0:T(1024)S(1)} %convert_element_type.196, bf16[768,2048]{1,0:T(8,128)(2,1)} %bitcast.165, bf16[2048,2048]{1,0:T(8,128)(2,1)} %param.32), kind=kOutput, calls=%fused_computation.154 | convolution fusion | flops 6477051904 | bytes 20983808 | tf_op jit(solution)/shard_map/dot_general | solution.py:33
  200.2 11.5 %convolution_convert_fusion.2 = bf16[768,2048]{1,0:T(8,128)(2,1)} fusion(bf16[768,2048]{1,0:T(8,128)(2,1)S(1)} %get-tuple-element.19, bf16[2048,2048]{1,0:T(8,128)(2,1)} %param.30), kind=kOutput, calls=%fused_computation.36 | convolution fusion | flops 6444023808 | bytes 14680064 | tf_op jit(solution)/shard_map/dot_general | solution.py:33
  211.9 37.7 %reduce-scatter.15.cloned.1.call-done = bf16[3,64,2048]{2,1,0:T(8,128)(2,1)} async-done(((bf16[3,256,2048]{2,1,0:T(8,128)(2,1)}), bf16[3,64,2048]{2,1,0:T(8,128)(2,1)}) %reduce-scatter.15.cloned.1.call-update) | async-done | bytes 786448 | tf_op jit(solution)/shard_map/reduce_scatter | solution.py:95
  249.6 2.5 fusion.27
  252.1 3.3 fusion.87
  255.4 28.6 %all-gather.11.cloned.1.call-done = bf16[3,256,2048]{2,1,0:T(8,128)(2,1)} async-done(((bf16[3,64,2048]{2,1,0:T(8,128)(2,1)}), bf16[3,256,2048]{2,1,0:T(8,128)(2,1)}) %all-gather.11.cloned.1.call-update) | async-done | bytes 3145744 | tf_op jit(solution)/shard_map/all_gather | solution.py:92
  284.0 4.6 convolution_convert_fusion.5
  291.6 8.0 bitcast_convert_fusion
  299.6 6.4 fusion
  306.0 6.6 fusion.2
  316.6 3.9 convert_reduce_fusion.1
  321.2 30.9 %reduce-scatter.19.cloned.1.call-done = bf16[3,256,256]{1,2,0:T(8,128)(2,1)} async-done(((bf16[3,1024,256]{1,2,0:T(8,128)(2,1)}), bf16[3,256,256]{1,2,0:T(8,128)(2,1)}) %reduce-scatter.19.cloned.1.call-update) | async-done | bytes 393232 | tf_op jit(solution)/shard_map/reduce_scatter | solution.py:178
  354.2 5.1 multiply_convert_fusion
  359.4 11.9 %convolution_convert_fusion.3 = bf16[768,2048]{1,0:T(8,128)(2,1)} fusion(bf16[768,2048]{1,0:T(8,128)(2,1)} %get-tuple-element.35, bf16[2048,2048]{1,0:T(8,128)(2,1)} %param.32), kind=kOutput, calls=%fused_computation.37 | convolution fusion | flops 6444023808 | bytes 14680064 | tf_op jit(solution)/shard_map/dot_general | solution.py:156
  373.3 7.8 convolution_convert_fusion.1
  382.8 4.5 all-reduce.6.cloned.1.call-done
  391.6 2.9 copy.97
  394.7 33.1 %reduce-scatter.17.cloned.1.call-done = bf16[3,64,2048]{2,1,0:T(8,128)(2,1)} async-done(((bf16[3,256,2048]{2,1,0:T(8,128)(2,1)}), bf16[3,64,2048]{2,1,0:T(8,128)(2,1)}) %reduce-scatter.17.cloned.1.call-update) | async-done | bytes 786448 | tf_op jit(solution)/shard_map/reduce_scatter | solution.py:95
  427.8 3.8 multiply_reduce_fusion.1
  431.8 36.2 %reduce-scatter.13.cloned.1.call-done = bf16[3,64,2048]{2,1,0:T(8,128)(2,1)} async-done(((bf16[3,256,2048]{2,1,0:T(8,128)(2,1)}), bf16[3,64,2048]{2,1,0:T(8,128)(2,1)}) %reduce-scatter.13.cloned.1.call-update) | async-done | bytes 786448 | tf_op jit(solution)/shard_map/reduce_scatter | solution.py:95
  467.9 4.8 multiply_add_fusion
  475.5 9.1 %add_convert_fusion.1 = bf16[1024,2048]{1,0:T(8,128)(2,1)} fusion(bf16[1024,2048]{1,0:T(8,128)(2,1)} %collective-permute-done.2, bf16[768,2048]{1,0:T(8,128)(2,1)} %copy-done.36, bf16[768,2048]{1,0:T(8,128)(2,1)} %bitcast.170, s32[]{:T(128)S(6)} %select_n.13), kind=kOutput, calls=%fused_computation.14 | convolution fusion | flops 3227516928 | bytes 13107204 | tf_op jit(solution)/shard_map/dot_general | solution.py:29
  484.8 6.0 convolution_convert_fusion
  492.3 90.7 %collective-permute-done.3 = bf16[2048,1024]{1,0:T(8,128)(2,1)S(1)} collective-permute-done((bf16[2048,1024]{1,0:T(8,128)(2,1)S(1)}, bf16[2048,1024]{1,0:T(8,128)(2,1)S(1)}, u32[]{:S(2)}, u32[]{:S(2)}) %collective-permute-start.3) | collective-permute-done | bytes 4194336 | tf_op jit(solution)/shard_map/ppermute | solution.py:43
  583.0 5.2 add_convert_fusion
  589.4 2.6 fusion.50
  593.5 22.4 %collective-permute-done.1 = bf16[512,1024]{1,0:T(8,128)(2,1)S(1)} collective-permute-done((bf16[512,1024]{1,0:T(8,128)(2,1)S(1)}, bf16[512,1024]{1,0:T(8,128)(2,1)S(1)}, u32[]{:S(2)}, u32[]{:S(2)}) %collective-permute-start.1) | collective-permute-done | bytes 1048608 | tf_op jit(solution)/shard_map/ppermute | solution.py:43
  618.0 2.6 multiply_convert_fusion.2
  622.1 21.6 %collective-permute-done = bf16[1024,512]{1,0:T(8,128)(2,1)S(1)} collective-permute-done((bf16[1024,512]{1,0:T(8,128)(2,1)S(1)}, bf16[1024,512]{1,0:T(8,128)(2,1)S(1)}, u32[]{:S(2)}, u32[]{:S(2)}) %collective-permute-start) | collective-permute-done | bytes 1048608 | tf_op jit(solution)/shard_map/ppermute | solution.py:43
  648.6 2.9 convert_element_type.231
  651.6 13.7 %reduce-scatter.29.cloned.1.call-done = bf16[2048,256]{1,0:T(8,128)(2,1)} async-done(((bf16[2048,1024]{1,0:T(8,128)(2,1)}), bf16[2048,256]{1,0:T(8,128)(2,1)}) %reduce-scatter.29.cloned.1.call-update) | async-done | bytes 1048592 | tf_op jit(solution)/shard_map/reduce_scatter | solution.py:52
  665.3 2.7 convert_element_type.235
  668.0 27.3 %reduce-scatter.25.cloned.1.call-done = bf16[512,256]{1,0:T(8,128)(2,1)} async-done(((bf16[512,1024]{1,0:T(8,128)(2,1)}), bf16[512,256]{1,0:T(8,128)(2,1)}) %reduce-scatter.25.cloned.1.call-update) | async-done | bytes 262160 | tf_op jit(solution)/shard_map/reduce_scatter | solution.py:52
  697.0 26.2 %reduce-scatter.21.cloned.1.call-done = bf16[256,512]{1,0:T(8,128)(2,1)} async-done(((bf16[1024,512]{1,0:T(8,128)(2,1)}), bf16[256,512]{1,0:T(8,128)(2,1)}) %reduce-scatter.21.cloned.1.call-update) | async-done | bytes 262160 | tf_op jit(solution)/shard_map/reduce_scatter | solution.py:52
  725.0 70.9 %all-reduce.8.cloned.1.call-done = bf16[8,17092]{1,0:T(8,128)(2,1)} async-done(((bf16[8,17092]{1,0:T(8,128)(2,1)}), bf16[8,17092]{1,0:T(8,128)(2,1)}) %all-reduce.8.cloned.1.call-update) | async-done | bytes 273488
  (200 shorter events, 58.7 us)
Async XLA Ops:
  7.2 73.4 %copy-start = (bf16[512,2048]{1,0:T(8,128)(2,1)S(1)}, bf16[512,2048]{1,0:T(8,128)(2,1)}, u32[]{:S(2)}) copy-start(bf16[512,2048]{1,0:T(8,128)(2,1)} %param.26) | copy-start | bytes 6291460
  7.2 4.0 copy-start.23
  7.2 4.0 copy-start.24
  7.2 4.1 copy-start.33
  7.2 49.2 %all-gather.5.cloned.1.call-start = ((), (), s32[]{:S(2)}) async-start(), calls=%async_computation.10 | async-start | bytes 1966080 | tf_op jit(solution)/shard_map/all_gather | solution.py:113
  7.3 3.0 copy-start.6
  11.2 3.5 copy-start.21
  11.3 3.4 copy-start.19
  11.3 3.4 copy-start.15
  16.5 105.5 %reduce-scatter.11.cloned.1.call-start = ((), (), s32[]{:S(2)}) async-start(), calls=%async_computation.11 | async-start | bytes 3932160 | tf_op jit(solution)/shard_map/reduce_scatter | solution.py:95
  64.1 7.0 copy-start.9
  85.2 69.8 %all-gather.7.cloned.1.call-start = ((), (), s32[]{:S(2)}) async-start(), calls=%async_computation.12 | async-start | bytes 3932160 | tf_op jit(solution)/shard_map/all_gather | solution.py:92
  85.2 5.4 copy-start.25
  85.3 5.4 copy-start.26
  85.3 5.4 copy-start.27
  124.2 5.0 copy-start.28
  126.3 59.2 %all-gather.9.cloned.1.call-start = ((), (), s32[]{:S(2)}) async-start(), calls=%async_computation.14 | async-start | bytes 3932160 | tf_op jit(solution)/shard_map/all_gather | solution.py:92
  128.8 120.8 %reduce-scatter.15.cloned.1.call-start = ((), (), s32[]{:S(2)}) async-start(), calls=%async_computation.15 | async-start | bytes 3932160 | tf_op jit(solution)/shard_map/reduce_scatter | solution.py:95
  200.2 11.5 %copy-start.36 = (bf16[768,2048]{1,0:T(8,128)(2,1)}, bf16[768,2048]{1,0:T(8,128)(2,1)S(1)}, u32[]{:S(2)}) copy-start(bf16[768,2048]{1,0:T(8,128)(2,1)S(1)} %get-tuple-element.19) | copy-start | bytes 9437188
  211.7 72.3 %all-gather.11.cloned.1.call-start = ((), (), s32[]{:S(2)}) async-start(), calls=%async_computation.16 | async-start | bytes 3932160 | tf_op jit(solution)/shard_map/all_gather | solution.py:92
  255.4 96.7 %reduce-scatter.19.cloned.1.call-start = ((), (), s32[]{:S(2)}) async-start(), calls=%async_computation.18 | async-start | bytes 1966080 | tf_op jit(solution)/shard_map/reduce_scatter | solution.py:178
  291.6 8.0 copy-start.10
  291.6 8.0 copy-start.11
  306.0 6.6 copy-start.8
  316.5 70.8 %all-reduce.6.cloned.1.call-start = ((), (), s32[]{:S(2)}) async-start(), calls=%async_computation.24 | async-start | bytes 1048576
  321.2 38.1 %copy-start.17 = (bf16[3,256,4,128]{3,2,1,0:T(4,128)(2,1)}, bf16[3,256,4,128]{3,2,1,0:T(4,128)(2,1)S(1)}, u32[]{:S(2)}) copy-start(bf16[3,256,4,128]{3,2,1,0:T(4,128)(2,1)S(1)} %copy.87) | copy-start | bytes 2359300
  354.2 73.6 %reduce-scatter.17.cloned.1.call-start = ((), (), s32[]{:S(2)}) async-start(), calls=%async_computation.17 | async-start | bytes 3932160 | tf_op jit(solution)/shard_map/reduce_scatter | solution.py:95
  359.3 108.6 %reduce-scatter.13.cloned.1.call-start = ((), (), s32[]{:S(2)}) async-start(), calls=%async_computation.13 | async-start | bytes 3932160 | tf_op jit(solution)/shard_map/reduce_scatter | solution.py:95
  371.3 274.9 %reduce-scatter.23.cloned.1.call-start = ((), (), s32[]{:S(2)}) async-start(), calls=%async_computation.20 | async-start | bytes 1351680 | tf_op jit(solution)/shard_map/reduce_scatter | solution.py:202
  381.1 94.3 %collective-permute-start.2 = (bf16[1024,2048]{1,0:T(8,128)(2,1)}, bf16[1024,2048]{1,0:T(8,128)(2,1)}, u32[]{:S(2)}, u32[]{:S(2)}) collective-permute-start(bf16[1024,2048]{1,0:T(8,128)(2,1)} %convolution_convert_fusion.1), channel_id=1, source_target_pairs={{0,16},{16,0},{1,17},{17,1},{2,18},{18,2},{3,19},{19,3},{4,20},{20... | collective-permute-start | bytes 12582920 | tf_op jit(solution)/shard_map/ppermute | solution.py:43
  388.3 39.5 %copy-start.20 = (f32[2048]{0:T(1024)S(1)}, f32[2048]{0:T(1024)}, u32[]{:S(2)}) copy-start(f32[2048]{0:T(1024)} %copy-done.19) | copy-start | bytes 24580
  391.6 76.4 %copy-start.4 = (f32[3,64,2048]{2,1,0:T(8,128)S(1)}, f32[3,64,2048]{2,1,0:T(8,128)}, u32[]{:S(2)}) copy-start(f32[3,64,2048]{2,1,0:T(8,128)} %copy-done.2) | copy-start | bytes 4718596
  391.6 76.4 %copy-start.7 = (bf16[3,64,2048]{2,1,0:T(8,128)(2,1)S(1)}, bf16[3,64,2048]{2,1,0:T(8,128)(2,1)}, u32[]{:S(2)}) copy-start(bf16[3,64,2048]{2,1,0:T(8,128)(2,1)} %param.19) | copy-start | bytes 2359300
  475.4 173.2 %reduce-scatter.27.cloned.1.call-start = ((), (), s32[]{:S(2)}) async-start(), calls=%async_computation.22 | async-start | bytes 5242880 | tf_op jit(solution)/shard_map/reduce_scatter | solution.py:52
  484.5 180.7 %reduce-scatter.29.cloned.1.call-start = ((), (), s32[]{:S(2)}) async-start(), calls=%async_computation.23 | async-start | bytes 5242880 | tf_op jit(solution)/shard_map/reduce_scatter | solution.py:52
  484.8 98.2 %copy-start.32 = (bf16[3,256,2048]{2,1,0:T(8,128)(2,1)S(1)}, bf16[3,256,2048]{2,1,0:T(8,128)(2,1)}, u32[]{:S(2)}) copy-start(bf16[3,256,2048]{2,1,0:T(8,128)(2,1)} %all-gather.9.cloned.1.call-done) | copy-start | bytes 9437188
  484.8 98.2 %copy-start.37 = (bf16[768,2048]{1,0:T(8,128)(2,1)S(1)}, bf16[768,2048]{1,0:T(8,128)(2,1)}, u32[]{:S(2)}) copy-start(bf16[768,2048]{1,0:T(8,128)(2,1)} %get-tuple-element.35) | copy-start | bytes 9437188
  490.8 92.2 %collective-permute-start.3 = (bf16[2048,1024]{1,0:T(8,128)(2,1)S(1)}, bf16[2048,1024]{1,0:T(8,128)(2,1)S(1)}, u32[]{:S(2)}, u32[]{:S(2)}) collective-permute-start(bf16[2048,1024]{1,0:T(8,128)(2,1)S(1)} %convolution_convert_fusion), channel_id=1, source_target_pairs={{0,16},{16,0},{1,17},{17,1},{2,18},{18,2},{3,19},{19,3},{4,20},{20... | collective-permute-start | bytes 12582920 | tf_op jit(solution)/shard_map/ppermute | solution.py:43
  588.3 107.0 %reduce-scatter.25.cloned.1.call-start = ((), (), s32[]{:S(2)}) async-start(), calls=%async_computation.21 | async-start | bytes 1310720 | tf_op jit(solution)/shard_map/reduce_scatter | solution.py:52
  589.4 26.5 %copy-start.16 = (bf16[3,256,2048]{2,1,0:T(8,128)(2,1)S(1)}, bf16[3,256,2048]{2,1,0:T(8,128)(2,1)}, u32[]{:S(2)}) copy-start(bf16[3,256,2048]{2,1,0:T(8,128)(2,1)} %all-gather.11.cloned.1.call-done) | copy-start | bytes 9437188
  591.9 26.0 %copy-start.18 = (bf16[3,256,4,128]{3,2,1,0:T(4,128)(2,1)S(1)}, bf16[3,256,4,128]{3,2,1,0:T(4,128)(2,1)}, u32[]{:S(2)}) copy-start(bf16[3,256,4,128]{3,2,1,0:T(4,128)(2,1)} %copy-done.17) | copy-start | bytes 2359300
  591.9 23.9 %collective-permute-start.1 = (bf16[512,1024]{1,0:T(8,128)(2,1)S(1)}, bf16[512,1024]{1,0:T(8,128)(2,1)S(1)}, u32[]{:S(2)}, u32[]{:S(2)}) collective-permute-start(bf16[512,1024]{1,0:T(8,128)(2,1)S(1)} %fusion.50), channel_id=1, source_target_pairs={{0,16},{16,0},{1,17},{17,1},{2,18},{18,2},{3,19},{19,3},{4,20},{20... | collective-permute-start | bytes 3145736 | tf_op jit(solution)/shard_map/ppermute | solution.py:43
  617.9 105.3 %reduce-scatter.21.cloned.1.call-start = ((), (), s32[]{:S(2)}) async-start(), calls=%async_computation.19 | async-start | bytes 1310720 | tf_op jit(solution)/shard_map/reduce_scatter | solution.py:52
  618.0 25.8 %copy-start.14 = (bf16[3,256,2048]{2,1,0:T(8,128)(2,1)S(1)}, bf16[3,256,2048]{2,1,0:T(8,128)(2,1)}, u32[]{:S(2)}) copy-start(bf16[3,256,2048]{2,1,0:T(8,128)(2,1)} %copy-done.13) | copy-start | bytes 9437188
  620.6 27.5 %copy-start.34 = (u32[32]{0:T(128)S(1)}, u32[32]{0:T(128)}, u32[]{:S(2)}) copy-start(u32[32]{0:T(128)} %constant.83) | copy-start | bytes 388
  620.6 23.2 %collective-permute-start = (bf16[1024,512]{1,0:T(8,128)(2,1)S(1)}, bf16[1024,512]{1,0:T(8,128)(2,1)S(1)}, u32[]{:S(2)}, u32[]{:S(2)}) collective-permute-start(bf16[1024,512]{1,0:T(8,128)(2,1)S(1)} %multiply_convert_fusion.2), channel_id=1, source_target_pairs={{0,16},{16,0},{1,17},{17,1},{2,18},{18,2},{3,19},{19,3},{4,20},{20... | collective-permute-start | bytes 3145736 | tf_op jit(solution)/shard_map/ppermute | solution.py:43
  645.8 150.2 %all-reduce.8.cloned.1.call-start = ((), (), s32[]{:S(2)}) async-start(), calls=%async_computation.25 | async-start | bytes 548864
  648.6 152.6 %copy-start.1 = (bf16[512,2048]{1,0:T(8,128)(2,1)S(1)}, bf16[512,2048]{1,0:T(8,128)(2,1)}, u32[]{:S(2)}) copy-start(bf16[512,2048]{1,0:T(8,128)(2,1)} %param.26) | copy-start | bytes 6291460
  (10 other events, 17.5 us)
Sparse Core Ops, SparseCore 0:
  16.6 39.7 all-gather.4
  85.3 36.6 reduce-scatter.10
  126.5 28.5 all-gather.6
  157.0 28.4 all-gather.8
  211.8 37.7 reduce-scatter.14
  255.5 28.4 all-gather.10
  316.7 35.4 reduce-scatter.18
  355.0 32.2 all-reduce.5
  389.9 37.8 reduce-scatter.16
  430.2 37.7 reduce-scatter.12
  475.5 25.0 reduce-scatter.22
  502.7 76.7 reduce-scatter.26
  588.4 76.8 reduce-scatter.28
  667.4 27.8 reduce-scatter.24
  697.4 25.7 reduce-scatter.20
  726.4 69.5 all-reduce.7

commit v2 on v1

v2 whole, which is shorter than its diff:
```python
import functools
import math

import jax
import jax.numpy as jnp
from jax import lax
from jax.experimental import pallas as pl
from jax.experimental.pallas import tpu as pltpu
from jax.sharding import PartitionSpec as P

NORM_EPS = 1e-05
BF16 = jnp.bfloat16
F32 = jnp.float32
MESH = pl.DeviceIdType.MESH


def normalize(values_in):
    row_mean = jnp.mean(values_in, -1, keepdims=True)
    centered = values_in - row_mean
    variance = jnp.mean(centered * centered, -1, keepdims=True)
    inv_std = lax.rsqrt(variance + NORM_EPS)
    return (centered * inv_std, inv_std)


def norm_back(grad_in, normed, inv_std, norm_gain):
    scaled = grad_in * norm_gain
    mean_scaled = jnp.mean(scaled, -1, keepdims=True)
    mean_mixed = jnp.mean(scaled * normed, -1, keepdims=True)
    return inv_std * (scaled - mean_scaled - normed * mean_mixed)


def across_rows(left_in, right_in):
    return lax.dot_general(left_in, right_in, (((0,), (0,)), ((), ())), preferred_element_type=F32)


def times_transposed(left_in, right_in):
    return lax.dot_general(left_in, right_in, (((1,), (1,)), ((), ())), preferred_element_type=F32)


def dp_exchange(part_for):
    n_dp = lax.axis_size("dp")
    me = lax.axis_index("dp")
    arrived = []
    for k in range(1, n_dp):
        target = lax.rem(me + k, n_dp)
        pairs = [(i, (i + k) % n_dp) for i in range(n_dp)]
        arrived.append(lax.ppermute(part_for(target).astype(BF16), "dp", pairs))
    total = part_for(me)
    for piece in arrived:
        total = total + piece.astype(F32)
    return total


def two_stage(part_for, dim):
    total = dp_exchange(part_for)
    return lax.psum_scatter(total.astype(BF16), "seq", scatter_dimension=dim, tiled=True).astype(F32)


def from_all_dp(values_in):
    n_dp = lax.axis_size("dp")
    pieces = [values_in]
    for k in range(1, n_dp):
        pieces.append(lax.ppermute(values_in, "dp", [(i, (i + k) % n_dp) for i in range(n_dp)]))
    return pieces


def columns_from_all_dp(values_in):
    n_dp = lax.axis_size("dp")
    me = lax.axis_index("dp")
    width = values_in.shape[1] // n_dp
    pieces = [lax.dynamic_slice_in_dim(values_in, me * width, width, 1)]
    for k in range(1, n_dp):
        sent = lax.dynamic_slice_in_dim(values_in, lax.rem(me + k, n_dp) * width, width, 1)
        pieces.append(lax.ppermute(sent, "dp", [(i, (i + k) % n_dp) for i in range(n_dp)]))
    return pieces


def tensor_partners():
    here = lax.axis_index("tensor")
    core = lax.rem(here, 2)
    chip = here // 2
    return here, chip, core, 2 * chip + 1 - core, 2 * (1 - chip) + core


def greet(*targets):
    barrier = pltpu.get_barrier_semaphore()
    for target in targets:
        pl.semaphore_signal(barrier, inc=1, device_id={"tensor": target}, device_id_type=MESH)
    pl.semaphore_wait(barrier, len(targets))


def send(source, landing, send_sem, recv_sem, target):
    return pltpu.make_async_remote_copy(
        src_ref=source,
        dst_ref=landing,
        send_sem=send_sem,
        recv_sem=recv_sem,
        device_id={"tensor": target},
        device_id_type=MESH,
    )


def reduce_kernel(
    transposed, a_ref, w_ref, o_ref, w_here, part, core_out, core_in, over_out, over_in, w_sem, cs, cr, xs, xr
):
    n_blocks, width = core_out.shape[0], core_out.shape[-1]
    share = o_ref.shape[0]
    _, chip, core, partner, across = tensor_partners()

    def load(n):
        where = pl.ds(n * width, width)
        block = w_ref.at[where, :] if transposed else w_ref.at[:, where]
        return pltpu.make_async_copy(block, w_here.at[n], w_sem.at[n])

    def to_partner(n):
        return send(core_out.at[n], core_in.at[n], cs.at[n], cr.at[n], partner)

    def to_across(n):
        return send(over_out.at[n], over_in.at[n], xs.at[n], xr.at[n], across)

    for n in range(n_blocks):
        load(n).start()
    greet(partner, across)

    def multiply(n):
        load(n).wait()
        slot = lax.rem(n, 2)
        dims = (((1,), (1,)), ((), ())) if transposed else (((1,), (0,)), ((), ()))
        product = lax.dot_general(a_ref[...], w_here[n], dims, preferred_element_type=F32)
        part[slot] = product.reshape(4, share, width)
        core_out[n, 0] = part[slot, 1 - core].astype(BF16)
        core_out[n, 1] = part[slot, 3 - core].astype(BF16)
        to_partner(n).start()

    def pass_on(n):
        slot = lax.rem(n, 2)
        to_partner(n).wait_recv()
        over_out[n] = (part[slot, 2 * (1 - chip) + core] + core_in[n, 1 - chip].astype(F32)).astype(BF16)
        to_across(n).start()
        columns = pl.ds(pl.multiple_of(n * width, width), width)
        o_ref[:, columns] = part[slot, 2 * chip + core] + core_in[n, chip].astype(F32)

    def step(n, carry):
        multiply(n)

        @pl.when(n > 0)
        def _():
            pass_on(n - 1)

        return carry

    lax.fori_loop(0, n_blocks, step, 0)
    pass_on(n_blocks - 1)

    def finish(n, carry):
        to_across(n).wait_recv()
        columns = pl.ds(pl.multiple_of(n * width, width), width)
        o_ref[:, columns] += over_in[n].astype(F32)
        to_across(n).wait_send()
        to_partner(n).wait_send()
        return carry

    lax.fori_loop(0, n_blocks, finish, 0)


def product_to_owners(name, number, a, w, transposed):
    tokens, depth = a.shape
    model_width = w.shape[0] if transposed else w.shape[1]
    share = tokens // 4
    width = model_width // 4
    n_blocks = 4
    w_block = (n_blocks, width, depth) if transposed else (n_blocks, depth, width)
    dma = pltpu.SemaphoreType.DMA((n_blocks,))
    return pl.pallas_call(
        functools.partial(reduce_kernel, transposed),
        out_shape=jax.ShapeDtypeStruct((share, model_width), F32),
        in_specs=[pl.BlockSpec(memory_space=pltpu.VMEM), pl.BlockSpec(memory_space=pl.ANY)],
        out_specs=pl.BlockSpec(memory_space=pltpu.VMEM),
        scratch_shapes=[
            pltpu.VMEM(w_block, BF16),
            pltpu.VMEM((2, 4, share, width), F32),
            pltpu.VMEM((n_blocks, 2, share, width), BF16),
            pltpu.VMEM((n_blocks, 2, share, width), BF16),
            pltpu.VMEM((n_blocks, share, width), BF16),
            pltpu.VMEM((n_blocks, share, width), BF16),
            dma,
            dma,
            dma,
            dma,
            dma,
        ],
        compiler_params=pltpu.CompilerParams(
            collective_id=number, has_side_effects=True, vmem_limit_bytes=40 * 1024 * 1024
        ),
        cost_estimate=estimate(25),
        name=name,
    )(a, w)


def gather_kernel(own_ref, o_ref, cs, cr, xs, xr, fs, fr):
    n_chunks = cs.shape[0]
    share = own_ref.shape[0]
    rows = share // n_chunks
    here, _, _, partner, across = tensor_partners()

    def copy(source, owner, n, sems, target):
        where = pl.ds(n * rows, rows)
        return send(source.at[where], o_ref.at[owner, where], sems[0].at[n], sems[1].at[n], target)

    greet(partner, across)
    for n in range(n_chunks):
        copy(own_ref, here, n, (xs, xr), across).start()
    for n in range(n_chunks):
        copy(own_ref, here, n, (cs, cr), partner).start()
    o_ref[here] = own_ref[...]
    for n in range(n_chunks):
        copy(own_ref, here, n, (xs, xr), across).wait_recv()
        copy(o_ref.at[across], across, n, (fs, fr), partner).start()
    for n in range(n_chunks):
        copy(own_ref, here, n, (xs, xr), across).wait_send()
        copy(own_ref, here, n, (cs, cr), partner).wait()
        copy(o_ref.at[across], across, n, (fs, fr), partner).wait()


def gather_shares(name, number, own):
    share, width = own.shape
    dma = pltpu.SemaphoreType.DMA((4,))
    return pl.pallas_call(
        gather_kernel,
        out_shape=jax.ShapeDtypeStruct((4, share, width), own.dtype),
        in_specs=[pl.BlockSpec(memory_space=pltpu.VMEM)],
        out_specs=pl.BlockSpec(memory_space=pltpu.VMEM),
        scratch_shapes=[dma] * 6,
        compiler_params=pltpu.CompilerParams(
            collective_id=number, has_side_effects=True, vmem_limit_bytes=16 * 1024 * 1024
        ),
        cost_estimate=estimate(20),
        name=name,
    )(own).reshape(4 * share, width)


def remote(source, landing, send_sem, recv_sem, target):
    return pltpu.make_async_remote_copy(
        src_ref=source,
        dst_ref=landing,
        send_sem=send_sem,
        recv_sem=recv_sem,
        device_id=target,
        device_id_type=MESH,
    )


def greet_all(targets):
    barrier = pltpu.get_barrier_semaphore()
    for target in targets:
        pl.semaphore_signal(barrier, inc=1, device_id=target, device_id_type=MESH)
    pl.semaphore_wait(barrier, len(targets))


def others_along(axis):
    size = lax.axis_size(axis)
    me = lax.axis_index(axis)
    return me, [lax.rem(me + k, size) for k in range(1, size)]


def small_kernel(in_ref, o_ref, core_in, over_out, over_in, dp_out, dp_in, seq_out, seq_in, cs, cr, xs, xr, ys, yr, zs, zr):
    _, chip, core, partner, across = tensor_partners()
    dp_me, dp_others = others_along("dp")
    seq_me, seq_others = others_along("seq")
    greet_all(
        [{"tensor": partner}, {"tensor": across}]
        + [{"dp": other} for other in dp_others]
        + [{"seq": other} for other in seq_others]
    )

    def to_partner(j):
        return remote(in_ref.at[j, 1 - core], core_in.at[j], cs.at[j], cr.at[j], {"tensor": partner})

    to_partner(0).start()
    to_partner(1).start()
    to_partner(0).wait()
    to_partner(1).wait()
    over_out[...] = in_ref[1 - chip, core] + core_in[1 - chip]
    to_across = remote(over_out, over_in, xs.at[0], xr.at[0], {"tensor": across})
    to_across.start()
    to_across.wait()
    dp_out[...] = in_ref[chip, core] + core_in[chip] + over_in[...]

    def fold(outgoing, incoming, send_sems, recv_sems, axis, me, others):
        def copy(target):
            return remote(outgoing.at[target], incoming.at[me], send_sems.at[target], recv_sems.at[me], {axis: target})

        for other in others:
            copy(other).start()
        total = outgoing[me]
        for other in others:
            remote(
                outgoing.at[other], incoming.at[other], send_sems.at[other], recv_sems.at[other], {axis: other}
            ).wait_recv()
            total = total + incoming[other]
        for other in others:
            copy(other).wait_send()
        return total

    seq_out[...] = fold(dp_out, dp_in, ys, yr, "dp", dp_me, dp_others)
    o_ref[...] = fold(seq_out, seq_in, zs, zr, "seq", seq_me, seq_others)


def sum_small(number, packed):
    n_dp, n_seq, rows, lanes = packed.shape[2:]
    dma = pltpu.SemaphoreType.DMA
    return pl.pallas_call(
        small_kernel,
        out_shape=jax.ShapeDtypeStruct((rows, lanes), F32),
        in_specs=[pl.BlockSpec(memory_space=pltpu.VMEM)],
        out_specs=pl.BlockSpec(memory_space=pltpu.VMEM),
        scratch_shapes=[
            pltpu.VMEM((2, n_dp, n_seq, rows, lanes), F32),
            pltpu.VMEM((n_dp, n_seq, rows, lanes), F32),
            pltpu.VMEM((n_dp, n_seq, rows, lanes), F32),
            pltpu.VMEM((n_dp, n_seq, rows, lanes), F32),
            pltpu.VMEM((n_dp, n_seq, rows, lanes), F32),
            pltpu.VMEM((n_seq, rows, lanes), F32),
            pltpu.VMEM((n_seq, rows, lanes), F32),
            dma((2,)),
            dma((2,)),
            dma((1,)),
            dma((1,)),
            dma((n_dp,)),
            dma((n_dp,)),
            dma((n_seq,)),
            dma((n_seq,)),
        ],
        compiler_params=pltpu.CompilerParams(collective_id=number, has_side_effects=True),
        cost_estimate=estimate(12),
        name="sum_small",
    )(packed)


def kv_kernel(
    g_ref, o_ref, core_in, over_out, over_in, seq_out, seq_in, own, cs, cr, xs, xr, zs, zr, gs, gr
):
    here, chip, core, partner, across = tensor_partners()
    seq_me, seq_others = others_along("seq")
    greet_all(
        [{"tensor": partner}, {"tensor": across}] + [{"seq": other} for other in seq_others]
    )

    def to_partner(j):
        return remote(g_ref.at[2 * j + 1 - core], core_in.at[j], cs.at[j], cr.at[j], {"tensor": partner})

    to_partner(1 - chip).start()
    to_partner(chip).start()
    to_partner(1 - chip).wait()
    over_out[...] = (g_ref[2 * (1 - chip) + core].astype(F32) + core_in[1 - chip].astype(F32)).astype(BF16)
    to_across = remote(over_out, over_in, xs.at[0], xr.at[0], {"tensor": across})
    to_across.start()
    to_partner(chip).wait()
    to_across.wait()
    seq_out[...] = (
        g_ref[2 * chip + core].astype(F32) + core_in[chip].astype(F32) + over_in[...].astype(F32)
    ).astype(BF16)

    def to_seq(target):
        return remote(seq_out.at[target], seq_in.at[seq_me], zs.at[target], zr.at[seq_me], {"seq": target})

    for other in seq_others:
        to_seq(other).start()
    total = seq_out[seq_me].astype(F32)
    for other in seq_others:
        remote(seq_out.at[other], seq_in.at[other], zs.at[other], zr.at[other], {"seq": other}).wait_recv()
        total = total + seq_in[other].astype(F32)
    own[...] = total.astype(BF16)
    o_ref[here] = own[...]
    x_copy = remote(own, o_ref.at[here], gs.at[0], gr.at[0], {"tensor": across})
    c_copy = remote(own, o_ref.at[here], gs.at[1], gr.at[1], {"tensor": partner})
    x_copy.start()
    c_copy.start()
    x_copy.wait_recv()
    f_copy = remote(o_ref.at[across], o_ref.at[across], gs.at[2], gr.at[2], {"tensor": partner})
    f_copy.start()
    x_copy.wait_send()
    c_copy.wait()
    f_copy.wait()
    for other in seq_others:
        to_seq(other).wait_send()


def sum_grad_kv(number, parts):
    _, n_seq, share, width = parts.shape
    dma = pltpu.SemaphoreType.DMA
    return pl.pallas_call(
        kv_kernel,
        out_shape=jax.ShapeDtypeStruct((4, share, width), BF16),
        in_specs=[pl.BlockSpec(memory_space=pltpu.VMEM)],
        out_specs=pl.BlockSpec(memory_space=pltpu.VMEM),
        scratch_shapes=[
            pltpu.VMEM((2, n_seq, share, width), BF16),
            pltpu.VMEM((n_seq, share, width), BF16),
            pltpu.VMEM((n_seq, share, width), BF16),
            pltpu.VMEM((n_seq, share, width), BF16),
            pltpu.VMEM((n_seq, share, width), BF16),
            pltpu.VMEM((share, width), BF16),
            dma((2,)),
            dma((2,)),
            dma((1,)),
            dma((1,)),
            dma((n_seq,)),
            dma((n_seq,)),
            dma((3,)),
            dma((3,)),
        ],
        compiler_params=pltpu.CompilerParams(collective_id=number, has_side_effects=True),
        cost_estimate=estimate(30),
        name="sum_grad_kv",
    )(parts).reshape(4 * share, width)


def estimate(microseconds):
    return pl.CostEstimate(flops=int(microseconds * 1e9), bytes_accessed=0, transcendentals=0)


def together(values, *earlier):
    return lax.optimization_barrier(tuple(values) + earlier)[: len(values)]


def after(value, *earlier):
    return lax.optimization_barrier((value,) + earlier)[0]


def shards(
    layer_input,
    lengths,
    cotangent,
    ln1_gain,
    ln1_bias,
    w_query,
    b_query,
    w_kv,
    b_value,
    w_out,
    b_out,
    ln2_gain,
    ln2_bias,
    w_up,
    b_up,
    w_down,
    b_down,
):
    n_rows, seq_len, model_width = layer_input.shape
    n_tensor = lax.axis_size("tensor")
    n_dp = lax.axis_size("dp")
    n_seq = lax.axis_size("seq")
    share_len = seq_len // n_tensor
    tensor_index = lax.axis_index("tensor")
    seq_index = lax.axis_index("seq")
    full_len = seq_len * n_seq
    head_size = w_kv.shape[1] // 2
    num_heads = w_query.shape[1] // head_size
    q_scale = 1.0 / math.sqrt(head_size)
    n_tok = n_rows * seq_len
    n_own = n_rows * share_len

    def by_share(values_in):
        return jnp.moveaxis(values_in.reshape((n_rows, n_tensor, share_len) + values_in.shape[2:]), 1, 0)

    def by_row(values_in):
        return jnp.moveaxis(
            values_in.reshape((n_tensor, n_rows, share_len) + values_in.shape[1:]), 0, 1
        ).reshape((n_rows, seq_len) + values_in.shape[1:])

    def own_share(values_in):
        return lax.dynamic_index_in_dim(values_in.reshape((n_tensor, n_own) + values_in.shape[1:]), tensor_index, 0, False)

    positions = seq_index * seq_len + jnp.arange(seq_len, dtype=jnp.int32)
    key_places = jnp.arange(full_len, dtype=jnp.int32)
    is_valid = (positions[None, :] < lengths[:, None]).astype(F32)
    allowed_keys = (key_places[None, None, :] <= positions[None, :, None]) & (
        key_places[None, None, :] < lengths[:, None, None]
    )
    valid_own = own_share(by_share(is_valid).reshape(n_tok))[:, None]
    grad_y_own = cotangent.reshape(n_own, model_width).astype(F32) * valid_own
    x_float = by_share(layer_input).reshape(n_tok, model_width).astype(F32)
    normed_x1, inv_one = normalize(x_float)
    flat_one = (normed_x1 * ln1_gain + ln1_bias).astype(BF16)
    kv_bias = jnp.concatenate([jnp.zeros((head_size,), F32), b_value.astype(F32)])
    kv_local = (jnp.dot(flat_one, w_kv, preferred_element_type=F32) + kv_bias).astype(BF16)
    kv_all = lax.all_gather(by_row(kv_local), "seq", axis=1, tiled=True)
    queries = ((jnp.dot(flat_one, w_query, preferred_element_type=F32) + b_query) * q_scale).astype(BF16)
    queries = by_row(queries).reshape(n_rows, seq_len, num_heads, head_size)
    key_rows = kv_all[..., :head_size]
    value_rows = kv_all[..., head_size:]
    grad_y_low = gather_shares("gather_grad_y", 0, grad_y_own.astype(BF16))
    grad_y_columns = columns_from_all_dp(grad_y_low)

    def scores_of(query_rows):
        raw_scores = jnp.einsum("rshd,rld->rhsl", query_rows, key_rows, preferred_element_type=F32)
        return jnp.where(allowed_keys[:, None], raw_scores, -1e30)

    scores = scores_of(queries)
    row_max = jnp.max(scores, -1, keepdims=True)
    exp_scores = jnp.exp(scores - row_max)
    exp_total = jnp.sum(exp_scores, -1, keepdims=True)
    soft_probs = exp_scores / exp_total
    log_total = row_max + jnp.log(exp_total)
    mixed_heads = jnp.einsum(
        "rhsl,rld->rshd", soft_probs.astype(BF16), value_rows, preferred_element_type=F32
    ).astype(BF16)
    mixed_heads = by_share(mixed_heads).reshape(n_tok, num_heads * head_size)
    attn_own = product_to_owners("attn_out", 1, mixed_heads, w_out, False)
    x_own = own_share(x_float)
    resid_own = x_own + (attn_own + b_out)
    normed_x2, inv_two = normalize(resid_own)
    normed_two = (normed_x2 * ln2_gain + ln2_bias).astype(BF16)
    flat_two = gather_shares("gather_norm_two", 2, normed_two)
    two_columns = columns_from_all_dp(flat_two)
    pre_act = jnp.dot(flat_two, w_up, preferred_element_type=F32) + b_up
    activated, gelu_pull = jax.vjp(lambda inner_in: jax.nn.gelu(inner_in, approximate=True), pre_act)
    act_low = activated.astype(BF16)
    grad_act = times_transposed(grad_y_low, w_down)
    grad_pre = gelu_pull(grad_act)[0].astype(BF16)
    grad_pre, act_low = lax.optimization_barrier((grad_pre, act_low))

    half_width = model_width // n_dp
    half_hidden = act_low.shape[1] // 2

    def columns(values_in, d):
        return lax.dynamic_slice_in_dim(values_in, d * half_width, half_width, 1)

    def summed_products(lefts, rights, dim):
        total = across_rows(lefts[0], rights[0])
        for left_in, right_in in zip(lefts[1:], rights[1:]):
            total = total + across_rows(left_in, right_in)
        return total.astype(BF16)

    def over_seq(values_in, dim):
        return lax.psum_scatter(values_in, "seq", scatter_dimension=dim, tiled=True)

    act_a = from_all_dp(act_low[:, :half_hidden])
    grad_n2 = product_to_owners("grad_norm_two", 3, grad_pre, w_up, True)
    grad_resid = grad_y_own + norm_back(grad_n2, normed_x2, inv_two, ln2_gain)
    grad_resid_low = grad_resid.astype(BF16)
    act_b = from_all_dp(after(act_low[:, half_hidden:], grad_resid_low))
    act_a = together(act_a, grad_resid_low, *two_columns)
    part_a = summed_products(act_a, grad_y_columns, 1)
    g_w_down_a = over_seq(part_a, 1)
    flat_resid = gather_shares("gather_grad_resid", 4, after(grad_resid_low, part_a))
    pre_a = from_all_dp(after(grad_pre[:, :half_hidden], flat_resid))
    mlp_own = product_to_owners("mlp_out", 5, after(act_low, flat_resid), w_down, False) + b_down
    part_b = summed_products(together(act_b, mlp_own, g_w_down_a), grad_y_columns, 1)
    g_w_down_b = over_seq(part_b, 1)
    pre_b = from_all_dp(after(grad_pre[:, half_hidden:], part_b))
    flat_resid = after(flat_resid, part_b)
    grad_mixed = times_transposed(flat_resid, w_out).astype(BF16)
    grad_mixed = by_row(grad_mixed).reshape(n_rows, seq_len, num_heads, head_size)
    again_probs = jnp.exp(scores_of(queries) - log_total)
    grad_probs = jnp.einsum("rshd,rld->rhsl", grad_mixed, value_rows, preferred_element_type=F32)
    inner_sum = jnp.sum(again_probs * grad_probs, -1, keepdims=True)
    grad_scores = (again_probs * (grad_probs - inner_sum)).astype(BF16)
    grad_query = jnp.einsum("rhsl,rld->rshd", grad_scores, key_rows, preferred_element_type=F32).astype(BF16)
    grad_keys = jnp.einsum("rhsl,rshd->rld", grad_scores, queries, preferred_element_type=F32)
    grad_values = jnp.einsum(
        "rhsl,rshd->rld", again_probs.astype(BF16), grad_mixed, preferred_element_type=F32
    )
    grad_kv = jnp.concatenate([grad_keys, grad_values], -1).astype(BF16)
    flat_query = by_share(grad_query).reshape(n_tok, num_heads * head_size)
    up_a = summed_products(two_columns, together(pre_a, flat_query, grad_kv, g_w_down_b), 0)
    g_w_up_a = over_seq(up_a, 0)
    flat_query, grad_kv, _ = lax.optimization_barrier((flat_query, grad_kv, up_a))
    grad_kv = jnp.transpose(
        grad_kv.reshape(n_rows, n_seq, n_tensor, share_len, 2 * head_size), (2, 1, 0, 3, 4)
    ).reshape(n_tensor, n_seq, n_own, 2 * head_size)
    flat_kv = sum_grad_kv(7, grad_kv)
    kv_columns = lax.dynamic_index_in_dim(
        flat_one.reshape(n_tok, n_dp * n_seq, n_tensor, model_width // (n_dp * n_seq * n_tensor)), tensor_index, 2, False
    )

    def first_part(d):
        query_part = across_rows(columns(flat_one, d), flat_query) * q_scale
        kv_side = lax.dynamic_slice_in_dim(kv_columns, d * n_seq, n_seq, 1).reshape(n_tok, -1)
        kv_part = across_rows(kv_side, flat_kv)
        out_part = across_rows(columns(flat_resid, d), mixed_heads)
        pieces = [p.reshape(n_seq, -1, query_part.shape[1]) for p in (query_part, kv_part, out_part)]
        return jnp.concatenate(pieces, 1)

    last_part = dp_exchange(first_part)
    grad_n1 = product_to_owners("grad_norm_one", 6, after(flat_query, flat_kv), w_query, True) * q_scale
    up_b = summed_products(two_columns, together(pre_b, grad_n1, g_w_up_a), 0)
    g_w_up_b = over_seq(up_b, 0)
    last_part = after(last_part, up_b).astype(BF16)
    last_sum = lax.psum_scatter(last_part, "seq", scatter_dimension=0, tiled=True)[0].astype(F32)
    last_rows = model_width // (n_dp * n_seq)
    g_w_query = last_sum[:last_rows]
    g_w_out = jnp.transpose(last_sum[-last_rows:])
    g_w_kv = last_sum[last_rows:-last_rows].reshape(-1, 2 * head_size)
    g_w_down = jnp.concatenate([g_w_down_a, g_w_down_b], 0).astype(F32)
    g_w_up = jnp.concatenate([g_w_up_a, g_w_up_b], 1).astype(F32)
    y_own = (valid_own * (resid_own + mlp_own)).astype(BF16).reshape(n_rows, share_len, model_width)

    own_kv = own_share(flat_kv)
    grad_n1 = grad_n1 + times_transposed(own_kv, w_kv)
    normed_x1_own = own_share(normed_x1)
    x_grad_own = grad_resid + norm_back(grad_n1, normed_x1_own, own_share(inv_one), ln1_gain)
    x_grad_own = x_grad_own.reshape(n_rows, share_len, model_width)
    g_ln2_gain = jnp.sum(grad_n2 * normed_x2, axis=0)
    g_ln2_bias = jnp.sum(grad_n2, axis=0)
    g_b_out = jnp.sum(grad_resid_low.astype(F32), axis=0)
    g_b_down = jnp.sum(grad_y_own, axis=0)
    g_ln1_gain = jnp.sum(grad_n1 * normed_x1_own, axis=0)
    g_ln1_bias = jnp.sum(grad_n1, axis=0)
    g_b_up = jnp.sum(grad_pre.astype(F32), axis=0)
    g_b_query = jnp.sum(flat_query.astype(F32), axis=0) * q_scale
    g_b_value = jnp.sum(own_kv[:, head_size:].astype(F32), axis=0)
    owners = n_dp * n_seq
    small = jnp.stack([g_ln1_gain, g_ln1_bias, g_ln2_gain, g_ln2_bias, g_b_out, g_b_down])
    mine = (lax.iota(jnp.int32, n_tensor) == tensor_index).astype(F32)[:, None, None]
    query_piece = mine * jnp.moveaxis(g_b_query.reshape(num_heads, owners, -1), 1, 0).reshape(1, owners, -1)
    up_piece = mine * jnp.moveaxis(g_b_up.reshape(-1, owners, 128 // owners), 1, 0).reshape(1, owners, -1)
    small_piece = jnp.transpose(small.reshape(6, owners, n_tensor, -1), (2, 1, 0, 3)).reshape(n_tensor, owners, -1)
    value_piece = jnp.moveaxis(g_b_value.reshape(owners, n_tensor, -1), 1, 0)
    pieces = [query_piece, up_piece, small_piece, value_piece]
    sizes = [p.shape[-1] for p in pieces]
    room = -(-sum(sizes) // 1024) * 1024
    pieces.append(jnp.zeros((n_tensor, owners, room - sum(sizes)), F32))
    packed = jnp.concatenate(pieces, -1).reshape(2, 2, n_dp, n_seq, room // 128, 128)
    packed = sum_small(8, packed).reshape(-1)
    ends = [sum(sizes[: i + 1]) for i in range(len(sizes))]
    query_out, up_out, small_out, value_out = [packed[e - s : e] for s, e in zip(sizes, ends)]
    return (
        y_own,
        x_grad_own,
        g_w_query,
        query_out.reshape(num_heads, -1),
        g_w_kv,
        value_out,
        g_w_out,
        g_w_up,
        up_out.reshape(-1, 128 // owners),
        g_w_down,
        small_out.reshape(6, -1),
    )


def solution(mesh):
    placed = (
        P("dp", "seq", None),
        P("dp"),
        P("dp", ("seq", "tensor"), None),
        P(),
        P(),
        P(None, "tensor"),
        P("tensor"),
        P(),
        P(),
        P("tensor", None),
        P(),
        P(),
        P(),
        P(None, "tensor"),
        P("tensor"),
        P("tensor", None),
        P(),
    )
    return jax.shard_map(
        shards,
        mesh=mesh,
        in_specs=placed,
        out_specs=(
            P("dp", ("seq", "tensor"), None),
            P("dp", ("seq", "tensor"), None),
            P(("dp", "seq"), "tensor"),
            P("tensor", ("dp", "seq")),
            P(("dp", "seq", "tensor"), None),
            P(("dp", "seq", "tensor")),
            P("tensor", ("dp", "seq")),
            P(("dp", "seq"), "tensor"),
            P("tensor", ("dp", "seq")),
            P("tensor", ("dp", "seq")),
            P(None, ("dp", "seq", "tensor")),
        ),
        check_vma=False,
    )
```

time: 812 us -> 584 us (0.72)
  waiting for transfers between devices: 548 us -> 80.9 us
  Pallas kernels: 0 us -> 216 us
  local copies, waits for them, and re-layouts: 27.2 us -> 91.8 us
  matrix products: 152 us -> 111 us
    reduce_scatter x10 -> x5, waiting for transfers between devices: 236 us -> 14.8 us  [the longest x1 11.4 us: shards(): lax.psum_scatter(last_part, 'seq', scatter_dimension=0, tiled=True)[0]]
    pallas_call x0 -> x9, Pallas kernels: none -> 216 us  [the longest x4 94.9 us: product_to_owners(): pl.pallas_call(functools.partial(reduce_kernel, transposed), out_shape=ja...]
    ppermute x4 -> x1, waiting for transfers between devices: 135 us -> 25.3 us  [dp_exchange(): arrived.append(lax.ppermute(part_for(target).astype(BF16), 'dp', pairs))]
    all_gather x4 -> x1, waiting for transfers between devices: 101 us -> 0.01 us  [shards(): kv_all = lax.all_gather(by_row(kv_local), 'seq', axis=1, tiled=True)]
    unnamed x18 -> x6, waiting for transfers between devices: 75.7 us -> 0.1 us
    ppermute x0 -> x6, waiting for transfers between devices: none -> 40.7 us  [the longest x2 33.7 us: columns_from_all_dp(): lax.ppermute(sent, 'dp', [(i, (i + k) % n_dp) for i in range(n_dp)])]
    dot_general x5 -> x3, matrix products: 39.6 us -> 19.3 us  [times_transposed(): lax.dot_general(left_in, right_in, (((1,), (1,)), ((), ())), preferred_el...]
    dynamic_slice x1 -> x7, local copies, waits for them, and re-layouts: 0.08 us -> 18.3 us  [the longest x3 14 us: first_part(): lax.dynamic_slice_in_dim(kv_columns, d * n_seq, n_seq, 1).reshape(n_tok, -1)]
  transfers between devices with their start and end apart: 20 -> 13, of which waited for: 17 -> 6; matrix products, arithmetic and copies ran while one was open for 15% -> 36% of each run, Pallas kernels for 0% -> 38%
where the time goes in v2:
time: 584 us; the launch traced here: 577 us
  Pallas kernels  216 us (37%)
  matrix products  111 us (19%)
  local copies, waits for them, and re-layouts  91.8 us (16%)
  waiting for transfers between devices  80.9 us (14%)
  other arithmetic  52.8 us (9%)
  between operations  15.7 us (3%)
  starting transfers between devices  7.88 us (1%)
    pallas_call x4, Pallas kernels, product_to_owners(): pl.pallas_call(functools.partial(reduce_kernel, transposed), out_shape=ja...  94.9 us
    pallas_call x3, Pallas kernels, gather_shares(): pl.pallas_call(gather_kernel, out_shape=jax.ShapeDtypeStruct((4, share, w...  64 us
    dot_general x14, matrix products, across_rows(): lax.dot_general(left_in, right_in, (((0,), (0,)), ((), ())), preferred_el...  44.4 us
    pallas_call x1, Pallas kernels, sum_grad_kv(): pl.pallas_call(kv_kernel, out_shape=jax.ShapeDtypeStruct((4, share, width...  35.4 us
    ppermute x2, waiting for transfers between devices, columns_from_all_dp(): lax.ppermute(sent, 'dp', [(i, (i + k) % n_dp) for i in range(n_dp)])  33.7 us
    ppermute x1, waiting for transfers between devices, dp_exchange(): arrived.append(lax.ppermute(part_for(target).astype(BF16), 'dp', pairs))  25.3 us
    pallas_call x1, Pallas kernels, sum_small(): pl.pallas_call(small_kernel, out_shape=jax.ShapeDtypeStruct((rows, lanes)...  22.1 us
    dot_general x3, matrix products, times_transposed(): lax.dot_general(left_in, right_in, (((1,), (1,)), ((), ())), preferred_el...  19.3 us
  transfers between devices with their start and end apart: 13, of which 6 were waited for; matrix products, arithmetic and copies ran while one was open for 36% of the time, Pallas kernels for 38%

profile of v2, /device:TPU:0, one launch (start us, length us, event | category | flops | bytes accessed | tf_op | source)
XLA Modules:
  0.0 576.7 jit_solution(8630383389087065559)
XLA Ops:
  7.2 2.9 convert_bitcast_fusion
  11.7 3.0 copy.138
  15.5 3.9 fusion.18
  24.7 22.5 %gather_grad_y.1 = bf16[4,192,2048]{2,1,0:T(8,128)(2,1)S(1)} custom-call(bf16[192,2048]{1,0:T(8,128)(2,1)S(1)} %fusion.33.own_ref), custom_call_target="tpu_custom_call" | custom-call | flops 20000000000 | tf_op jit(solution)/shard_map/gather_grad_y/pallas_call | solution.py:228
  48.9 2.8 constant_dynamic-slice_fusion.5
  54.1 3.7 multiply_convert_fusion.3
  61.8 12.2 %fusion.52 = f32[768,2048]{1,0:T(8,128)} fusion(bf16[768,2048]{1,0:T(8,128)(2,1)} %bitcast.236, bf16[2048,2048]{1,0:T(8,128)(2,1)} %w_ref.6), kind=kOutput, calls=%fused_computation.151 | convolution fusion | flops 6442450944 | bytes 17825792 | tf_op jit(solution)/shard_map/dot_general | solution.py:37
  73.9 3.2 fusion.4
  81.6 5.0 fusion.38
  91.0 22.6 %attn_out.1 = f32[192,2048]{1,0:T(8,128)S(1)} custom-call(bf16[768,512]{1,0:T(8,128)(2,1)S(1)} %bitcast.234, bf16[512,2048]{1,0:T(8,128)(2,1)S(1)} %copy-done.9), custom_call_target="tpu_custom_call" | custom-call | flops 24999999488 | tf_op jit(solution)/shard_map/attn_out/pallas_call | solution.py:174
  116.2 20.9 %gather_norm_two.1 = bf16[4,192,2048]{2,1,0:T(8,128)(2,1)S(1)} custom-call(bf16[192,2048]{1,0:T(8,128)(2,1)S(1)} %add_convert_fusion.5.own_ref), custom_call_target="tpu_custom_call" | custom-call | flops 20000000000 | tf_op jit(solution)/shard_map/gather_norm_two/pallas_call | solution.py:228
  137.1 13.1 %multiply_convert_fusion = (bf16[768,2048]{1,0:T(8,128)(2,1)S(1)}, bf16[768,2048]{1,0:T(8,128)(2,1)S(1)}) fusion(f32[2048]{0:T(1024)S(1)} %convert_element_type.204, f32[768,2048]{1,0:T(8,128)} %fusion.52, bf16[768,2048]{1,0:T(8,128)(2,1)S(1)} %bitcast.232, bf16[2048,2048]{1,0:T(8,128)(2,1)S(1)} %bitcast.240), kind=kOutput, calls=%fused_computation.31 | convolution fusion | flops 6478626816 | bytes 24125440 | tf_op jit(solution)/shard_map/dot_general | solution.py:517
  156.0 24.1 %grad_norm_two.1 = f32[192,2048]{1,0:T(8,128)S(1)} custom-call(bf16[768,2048]{1,0:T(8,128)(2,1)S(1)} %get-tuple-element.32.a_ref, bf16[2048,2048]{1,0:T(8,128)(2,1)S(1)} %bitcast.240), custom_call_target="tpu_custom_call" | custom-call | flops 24999999488 | tf_op jit(solution)/shard_map/grad_norm_two/pallas_call | solution.py:174
  185.7 4.0 collective-permute-done
  189.7 33.7 %collective-permute-done.1 = bf16[768,1024]{1,0:T(8,128)(2,1)S(1)} collective-permute-done((bf16[768,1024]{1,0:T(8,128)(2,1)S(1)}, bf16[768,1024]{1,0:T(8,128)(2,1)S(1)}, u32[]{:S(2)}, u32[]{:S(2)}) %collective-permute-start.1) | collective-permute-done | bytes 1572896 | tf_op jit(solution)/shard_map/ppermute | solution.py:74
  223.4 3.9 fusion.53
  227.3 3.3 add_convert_fusion.4
  230.7 20.6 %gather_grad_resid.1 = bf16[4,192,2048]{2,1,0:T(8,128)(2,1)S(1)} custom-call(bf16[192,2048]{1,0:T(8,128)(2,1)S(1)} %get-tuple-element.35.own_ref), custom_call_target="tpu_custom_call" | custom-call | flops 20000000000 | tf_op jit(solution)/shard_map/gather_grad_resid/pallas_call | solution.py:228
  253.0 3.4 copy-done.8
  256.4 25.4 %mlp_out.1 = f32[192,2048]{1,0:T(8,128)S(1)} custom-call(bf16[768,2048]{1,0:T(8,128)(2,1)S(1)} %copy-done.3, bf16[2048,2048]{1,0:T(8,128)(2,1)S(1)} %copy-done.8), custom_call_target="tpu_custom_call" | custom-call | flops 24999999488 | tf_op jit(solution)/shard_map/mlp_out/pallas_call | solution.py:174
  283.6 3.9 fusion.54
  287.5 4.7 add_convert_fusion.3
  293.8 3.7 convolution_convert_fusion.1
  298.6 6.6 %fusion = (f32[3,4,256]{2,1,0:T(4,128)S(1)}, f32[3,1024,256,4]{2,1,3,0:T(8,128)S(1)}) fusion(f32[3,1024,256,4]{2,1,3,0:T(8,128)} %copy-done.13, f32[3,4,256]{2,1,0:T(4,128)S(1)} %log_add_fusion, pred[3,256,1024]{1,2,0:T(8,128)(4,1)S(1)} %copy-done.17, bf16[3,256,4,128]{1,3,2,0:T(8,128)(2,1)S(1)} %copy.159, bf16[3,1024,256]{2,1,0:T(8,128)(2,1)} %all-gather.2.cloned.1.call-done), kind=kOutput, calls=%fused_computation.2 | convolution fusion | flops 817886208 | bytes 27549696 | tf_op jit(solution)/shard_map/rshd,rld->rhsl/dot_general | solution.py:557
  305.3 6.9 %fusion.2 = bf16[3,4,256,1024]{2,3,1,0:T(8,128)(2,1)S(1)} fusion(f32[3,1024,256,4]{2,1,3,0:T(8,128)S(1)} %get-tuple-element.140, f32[3,1024,256,4]{2,1,3,0:T(8,128)} %copy-done.13, f32[3,4,256]{2,1,0:T(4,128)S(1)} %get-tuple-element.139, f32[3,4,256]{2,1,0:T(4,128)S(1)} %log_add_fusion, pred[3,256,1024]{1,2,0:T(8,128)(4,1)S(1)} %copy-done.17), kind=kLoop, calls=%fused_computation.4 | loop fusion | flops 15728640 | bytes 32268288 | tf_op jit(solution)/shard_map/convert_element_type | solution.py:559
  319.1 5.0 bitcast_convert_fusion.1
  324.2 7.8 %bitcast_convert_fusion = bf16[3,1024,128]{1,2,0:T(8,128)(2,1)S(1)} fusion(bf16[3,256,4,128]{1,3,2,0:T(8,128)(2,1)S(1)} %copy-done.29, f32[3,1024,256,4]{2,1,3,0:T(8,128)} %copy-done.13, f32[3,4,256]{2,1,0:T(4,128)S(1)} %log_add_fusion, pred[3,256,1024]{1,2,0:T(8,128)(4,1)S(1)} %copy-done.17), kind=kOutput, calls=%fused_computation.55 | convolution fusion | flops 815136768 | bytes 14954496 | tf_op jit(solution)/shard_map/rhsl,rshd->rld/dot_general | solution.py:562
  333.3 3.4 reduce-scatter.8.cloned.1.call-done
  336.7 3.4 fusion.55
  340.1 4.7 add_convert_fusion.2
  345.0 13.6 %reshape.427 = f32[768,8,4,64]{3,2,1,0:T(4,128)} reshape(f32[4,3,64,2048]{3,2,1,0:T(8,128)} %copy.138) | data formatting | bytes 12582912 | tf_op jit(solution)/shard_map/convert_element_type | solution.py:483
  359.1 8.6 %add_convert_fusion = bf16[768,8,4,64]{3,2,1,0:T(4,128)(2,1)S(1)} fusion(f32[768,8,4,64]{3,2,1,0:T(4,128)} %reshape.427, f32[8,4,64]{2,1,0:T(4,128)S(1)} %add.253, f32[8,4,64]{2,1,0:T(4,128)S(1)} %mul.322, f32[768]{0:T(1024)S(1)} %copy-done.50, f32[768]{0:T(1024)S(1)} %copy-done.52), kind=kLoop, calls=%fused_computation.6 | loop fusion | flops 7864320 | bytes 9459712 | tf_op jit(solution)/shard_map/convert_element_type | solution.py:485
  367.8 5.0 constant_dynamic-slice_fusion.1
  374.5 4.5 copy.165
  379.0 4.5 copy.167
  387.7 3.3 dynamic-slice_bitcast_fusion
  395.2 3.7 convolution_convert_fusion
  403.0 2.8 copy.161
  405.8 3.0 collective-permute-done.6
  408.8 3.7 fusion.58
  412.6 4.7 add_convert_fusion.1
  417.4 35.4 %sum_grad_kv.1 = bf16[4,192,256]{2,1,0:T(8,128)(2,1)} custom-call(bf16[4,4,192,256]{3,2,1,0:T(8,128)(2,1)} %bitcast.256), custom_call_target="tpu_custom_call" | custom-call | flops 30000001024 | tf_op jit(solution)/shard_map/sum_grad_kv/pallas_call | solution.py:392
  461.6 22.7 %grad_norm_one.1 = f32[192,2048]{1,0:T(8,128)S(1)} custom-call(bf16[768,512]{1,0:T(8,128)(2,1)S(1)} %bitcast.228, bf16[2048,512]{1,0:T(8,128)(2,1)S(1)} %copy-done.12), custom_call_target="tpu_custom_call" | custom-call | flops 24999999488 | tf_op jit(solution)/shard_map/grad_norm_one/pallas_call | solution.py:174
  484.4 25.3 %collective-permute-done.5 = bf16[4,544,512]{2,1,0:T(8,128)(2,1)S(1)} collective-permute-done((bf16[4,544,512]{2,1,0:T(8,128)(2,1)S(1)}, bf16[4,544,512]{2,1,0:T(8,128)(2,1)S(1)}, u32[]{:S(2)}, u32[]{:S(2)}) %collective-permute-start.5) | collective-permute-done | bytes 2228256 | tf_op jit(solution)/shard_map/ppermute | solution.py:47
  512.5 3.5 fusion.28
  518.3 22.1 %sum_small.1 = f32[8,128]{1,0:T(8,128)} custom-call(f32[2,2,2,4,8,128]{5,4,3,2,1,0:T(8,128)} %bitcast.271), custom_call_target="tpu_custom_call" | custom-call | flops 12000000000 | tf_op jit(solution)/shard_map/sum_small/pallas_call | solution.py:312
  547.8 3.2 fusion.27
  553.6 11.4 %reduce-scatter.12.cloned.1.call-done = bf16[1,544,512]{2,1,0:T(8,128)(2,1)} async-done(((bf16[4,544,512]{2,1,0:T(8,128)(2,1)}), bf16[1,544,512]{2,1,0:T(8,128)(2,1)}) %reduce-scatter.12.cloned.1.call-update) | async-done | bytes 557072 | tf_op jit(solution)/shard_map/reduce_scatter | solution.py:591
  (301 shorter events, 95.6 us)
Async XLA Ops:
  7.2 12.2 %copy-start = (bf16[2048,256]{1,0:T(8,128)(2,1)S(1)}, bf16[2048,256]{1,0:T(8,128)(2,1)}, u32[]{:S(2)}) copy-start(bf16[2048,256]{1,0:T(8,128)(2,1)} %param.24) | copy-start | bytes 3145732
  7.2 66.7 %all-gather.2.cloned.1.call-start = ((), (), s32[]{:S(2)}) async-start(), calls=%async_computation.5 | async-start | bytes 1966080 | tf_op jit(solution)/shard_map/all_gather | solution.py:488
  19.4 5.1 copy-start.18
  21.9 261.7 %reduce-scatter.6.cloned.1.call-start = ((), (), s32[]{:S(2)}) async-start(), calls=%async_computation.6 | async-start | bytes 2621440 | tf_op jit(solution)/shard_map/reduce_scatter | solution.py:537
  48.9 5.2 copy-start.67
  48.9 5.2 copy-start.11
  51.7 171.7 %collective-permute-start.2 = (bf16[768,1024]{1,0:T(8,128)(2,1)}, bf16[768,1024]{1,0:T(8,128)(2,1)}, u32[]{:S(2)}, u32[]{:S(2)}) collective-permute-start(bf16[768,1024]{1,0:T(8,128)(2,1)} %constant_dynamic-slice_fusion.5), channel_id=1, source_target_pairs={{0,16},{16,0},{1,17},{17,1},{2,18},{18,2},{3,19},{19,3},{4,20},{20... | collective-permute-start | bytes 4718600 | tf_op jit(solution)/shard_map/ppermute | solution.py:74
  61.8 17.7 %copy-start.16 = (pred[3,256,1024]{1,2,0:T(8,128)(4,1)}, pred[3,256,1024]{1,2,0:T(8,128)(4,1)S(1)}, u32[]{:S(2)}) copy-start(pred[3,256,1024]{1,2,0:T(8,128)(4,1)S(1)} %broadcast_and_fusion) | copy-start | bytes 2359300
  77.1 4.5 copy-start.13
  86.6 4.3 copy-start.9
  90.8 22.8 %copy-start.21 = (bf16[4,3,64,4,128]{4,3,2,1,0:T(4,128)(2,1)}, bf16[4,3,64,4,128]{4,3,2,1,0:T(4,128)(2,1)S(1)}, u32[]{:S(2)}) copy-start(bf16[4,3,64,4,128]{4,3,2,1,0:T(4,128)(2,1)S(1)} %copy.148) | copy-start | bytes 2359300
  113.6 23.5 %slice-start = ((s8[8388608]{0:T(1024)(128)(4,1)}), s8[4194304]{0:T(1024)(128)(4,1)S(1)}, s32[]{:S(2)}) async-start(s8[8388608]{0:T(1024)(128)(4,1)} %bitcast.239), calls=%async_computation.11 | async-start | bytes 8388608
  116.2 20.9 %slice-start.1 = ((s8[8388608]{0:T(1024)(128)(4,1)}), s8[4194304]{0:T(1024)(128)(4,1)S(1)}, s32[]{:S(2)}) async-start(s8[8388608]{0:T(1024)(128)(4,1)} %bitcast.239), calls=%async_computation.12 | async-start | bytes 8388608
  150.3 33.4 %copy-start.1 = (bf16[768,2048]{1,0:T(8,128)(2,1)}, bf16[768,2048]{1,0:T(8,128)(2,1)S(1)}, u32[]{:S(2)}) copy-start(bf16[768,2048]{1,0:T(8,128)(2,1)S(1)} %get-tuple-element.32.a_ref) | copy-start | bytes 9437188
  152.5 37.3 %collective-permute-start = (bf16[768,1024]{1,0:T(8,128)(2,1)S(1)}, bf16[768,1024]{1,0:T(8,128)(2,1)S(1)}, u32[]{:S(2)}, u32[]{:S(2)}) collective-permute-start(bf16[768,1024]{1,0:T(8,128)(2,1)S(1)} %get-tuple-element.33), channel_id=1, source_target_pairs={{0,16},{16,0},{1,17},{17,1},{2,18},{18,2},{3,19},{19,3},{4,20},{20... | collective-permute-start | bytes 4718600 | tf_op jit(solution)/shard_map/ppermute | solution.py:63
  154.5 69.0 %collective-permute-start.1 = (bf16[768,1024]{1,0:T(8,128)(2,1)S(1)}, bf16[768,1024]{1,0:T(8,128)(2,1)S(1)}, u32[]{:S(2)}, u32[]{:S(2)}) collective-permute-start(bf16[768,1024]{1,0:T(8,128)(2,1)S(1)} %get-tuple-element.133), channel_id=1, source_target_pairs={{0,16},{16,0},{1,17},{17,1},{2,18},{18,2},{3,19},{19,3},{4,20},{20... | collective-permute-start | bytes 4718600 | tf_op jit(solution)/shard_map/ppermute | solution.py:74
  183.2 100.4 %collective-permute-start.3 = (bf16[768,1024]{1,0:T(8,128)(2,1)}, bf16[768,1024]{1,0:T(8,128)(2,1)}, u32[]{:S(2)}, u32[]{:S(2)}) collective-permute-start(bf16[768,1024]{1,0:T(8,128)(2,1)} %get-tuple-element.38), channel_id=1, source_target_pairs={{0,16},{16,0},{1,17},{17,1},{2,18},{18,2},{3,19},{19,3},{4,20},{20... | collective-permute-start | bytes 4718600 | tf_op jit(solution)/shard_map/ppermute | solution.py:63
  223.4 3.9 copy-start.6
  230.7 106.1 %reduce-scatter.8.cloned.1.call-start = ((), (), s32[]{:S(2)}) async-start(), calls=%async_computation.7 | async-start | bytes 2621440 | tf_op jit(solution)/shard_map/reduce_scatter | solution.py:537
  230.7 22.3 %copy-start.3 = (bf16[768,2048]{1,0:T(8,128)(2,1)S(1)}, bf16[768,2048]{1,0:T(8,128)(2,1)}, u32[]{:S(2)}) copy-start(bf16[768,2048]{1,0:T(8,128)(2,1)} %copy-done.2) | copy-start | bytes 9437188
  256.4 26.1 %copy-start.53 = (f32[2048]{0:T(1024)S(1)}, f32[2048]{0:T(1024)}, u32[]{:S(2)}) copy-start(f32[2048]{0:T(1024)} %convert_element_type.209) | copy-start | bytes 24580
  281.9 51.5 %collective-permute-start.4 = (bf16[768,1024]{1,0:T(8,128)(2,1)}, bf16[768,1024]{1,0:T(8,128)(2,1)}, u32[]{:S(2)}, u32[]{:S(2)}) collective-permute-start(bf16[768,1024]{1,0:T(8,128)(2,1)} %get-tuple-element.42), channel_id=1, source_target_pairs={{0,16},{16,0},{1,17},{17,1},{2,18},{18,2},{3,19},{19,3},{4,20},{20... | collective-permute-start | bytes 4718600 | tf_op jit(solution)/shard_map/ppermute | solution.py:63
  292.2 116.6 %reduce-scatter.10.cloned.1.call-start = ((), (), s32[]{:S(2)}) async-start(), calls=%async_computation.8 | async-start | bytes 2621440 | tf_op jit(solution)/shard_map/reduce_scatter | solution.py:537
  298.6 6.6 %copy-start.28 = (bf16[3,256,4,128]{1,3,2,0:T(8,128)(2,1)}, bf16[3,256,4,128]{1,3,2,0:T(8,128)(2,1)S(1)}, u32[]{:S(2)}) copy-start(bf16[3,256,4,128]{1,3,2,0:T(8,128)(2,1)S(1)} %copy.159) | copy-start | bytes 2359300
  305.3 9.5 %copy-start.27 = (bf16[3,1024,256]{2,1,0:T(8,128)(2,1)S(1)}, bf16[3,1024,256]{2,1,0:T(8,128)(2,1)}, u32[]{:S(2)}) copy-start(bf16[3,1024,256]{2,1,0:T(8,128)(2,1)} %all-gather.2.cloned.1.call-done) | copy-start | bytes 4718596
  319.1 5.1 copy-start.29
  332.0 4.8 copy-start.69
  344.9 13.7 %copy-start.55 = (bf16[2048]{0:T(1024)(128)(2,1)S(1)}, bf16[2048]{0:T(1024)(128)(2,1)}, u32[]{:S(2)}) copy-start(bf16[2048]{0:T(1024)(128)(2,1)} %param.21) | copy-start | bytes 12292
  344.9 13.8 %copy-start.57 = (bf16[2048]{0:T(1024)(128)(2,1)S(1)}, bf16[2048]{0:T(1024)(128)(2,1)}, u32[]{:S(2)}) copy-start(bf16[2048]{0:T(1024)(128)(2,1)} %param.20) | copy-start | bytes 12292
  344.9 13.9 %copy-start.65 = (f32[192]{0:T(256)S(1)}, f32[192]{0:T(256)}, u32[]{:S(2)}) copy-start(f32[192]{0:T(256)} %get-tuple-element.114) | copy-start | bytes 2308
  344.9 13.9 %copy-start.20 = (bf16[3,64,2048]{2,1,0:T(8,128)(2,1)S(1)}, bf16[3,64,2048]{2,1,0:T(8,128)(2,1)}, u32[]{:S(2)}) copy-start(bf16[3,64,2048]{2,1,0:T(8,128)(2,1)} %param.19) | copy-start | bytes 2359300
  344.9 14.2 %copy-start.50 = (f32[768]{0:T(1024)S(1)}, f32[768]{0:T(1024)}, u32[]{:S(2)}) copy-start(f32[768]{0:T(1024)} %copy-done.49) | copy-start | bytes 9220
  345.0 14.2 %copy-start.52 = (f32[768]{0:T(1024)S(1)}, f32[768]{0:T(1024)}, u32[]{:S(2)}) copy-start(f32[768]{0:T(1024)} %copy-done.51) | copy-start | bytes 9220
  345.0 206.0 %reduce-scatter.14.cloned.1.call-start = ((), (), s32[]{:S(2)}) async-start(), calls=%async_computation.10 | async-start | bytes 2621440 | tf_op jit(solution)/shard_map/reduce_scatter | solution.py:537
  367.8 6.5 %copy-start.48 = (f32[4,3,64]{2,1,0:T(4,128)S(1)}, f32[4,3,64]{2,1,0:T(4,128)}, u32[]{:S(2)}) copy-start(f32[4,3,64]{2,1,0:T(4,128)} %copy-done.47) | copy-start | bytes 9220
  367.8 6.5 %copy-start.44 = (f32[4,3,64]{2,1,0:T(4,128)S(1)}, f32[4,3,64]{2,1,0:T(4,128)}, u32[]{:S(2)}) copy-start(f32[4,3,64]{2,1,0:T(4,128)} %copy-done.43) | copy-start | bytes 9220
  372.7 10.9 %copy-start.22 = (bf16[4,3,64,4,128]{4,3,2,1,0:T(4,128)(2,1)S(1)}, bf16[4,3,64,4,128]{4,3,2,1,0:T(4,128)(2,1)}, u32[]{:S(2)}) copy-start(bf16[4,3,64,4,128]{4,3,2,1,0:T(4,128)(2,1)} %copy-done.21) | copy-start | bytes 2359300
  372.7 36.1 %collective-permute-start.6 = (bf16[768,1024]{1,0:T(8,128)(2,1)}, bf16[768,1024]{1,0:T(8,128)(2,1)}, u32[]{:S(2)}, u32[]{:S(2)}) collective-permute-start(bf16[768,1024]{1,0:T(8,128)(2,1)} %get-tuple-element.48), channel_id=1, source_target_pairs={{0,16},{16,0},{1,17},{17,1},{2,18},{18,2},{3,19},{19,3},{4,20},{20... | collective-permute-start | bytes 4718600 | tf_op jit(solution)/shard_map/ppermute | solution.py:63
  405.8 6.8 %copy-start.37 = (bf16[768,1024]{1,0:T(8,128)(2,1)S(1)}, bf16[768,1024]{1,0:T(8,128)(2,1)}, u32[]{:S(2)}) copy-start(bf16[768,1024]{1,0:T(8,128)(2,1)} %get-tuple-element.134) | copy-start | bytes 4718596
  417.3 147.7 %reduce-scatter.12.cloned.1.call-start = ((), (), s32[]{:S(2)}) async-start(), calls=%async_computation.9 | async-start | bytes 2785280 | tf_op jit(solution)/shard_map/reduce_scatter | solution.py:591
  417.3 35.4 %copy-start.35 = (bf16[768,4,1,64]{0,3,1,2:T(8,128)(2,1)S(1)}, bf16[768,4,1,64]{0,3,1,2:T(8,128)(2,1)}, u32[]{:S(2)}) copy-start(bf16[768,4,1,64]{0,3,1,2:T(8,128)(2,1)} %copy.165) | copy-start | bytes 1179652
  417.4 37.5 %copy-start.34 = (bf16[768,4,1,64]{0,3,1,2:T(8,128)(2,1)S(1)}, bf16[768,4,1,64]{0,3,1,2:T(8,128)(2,1)}, u32[]{:S(2)}) copy-start(bf16[768,4,1,64]{0,3,1,2:T(8,128)(2,1)} %copy.167) | copy-start | bytes 1179652
  458.9 50.8 %collective-permute-start.5 = (bf16[4,544,512]{2,1,0:T(8,128)(2,1)S(1)}, bf16[4,544,512]{2,1,0:T(8,128)(2,1)S(1)}, u32[]{:S(2)}, u32[]{:S(2)}) collective-permute-start(bf16[4,544,512]{2,1,0:T(8,128)(2,1)S(1)} %pad_maximum_fusion), channel_id=1, source_target_pairs={{0,16},{16,0},{1,17},{17,1},{2,18},{18,2},{3,19},{19,3},{4,20},{20... | collective-permute-start | bytes 6684680 | tf_op jit(solution)/shard_map/ppermute | solution.py:47
  461.6 48.0 %copy-start.32 = (f32[4,256,512]{2,1,0:T(8,128)S(1)}, f32[4,256,512]{2,1,0:T(8,128)}, u32[]{:S(2)}) copy-start(f32[4,256,512]{2,1,0:T(8,128)} %fusion.57) | copy-start | bytes 6291460
  461.6 48.0 %copy-start.39 = (f32[4,32,512]{2,1,0:T(8,128)S(1)}, f32[4,32,512]{2,1,0:T(8,128)}, u32[]{:S(2)}) copy-start(f32[4,32,512]{2,1,0:T(8,128)} %reshape.414) | copy-start | bytes 786436
  518.3 27.0 %copy-start.41 = (bf16[1024,256]{1,0:T(8,128)(2,1)S(1)}, bf16[1024,256]{1,0:T(8,128)(2,1)}, u32[]{:S(2)}) copy-start(bf16[1024,256]{1,0:T(8,128)(2,1)} %reduce-scatter.6.cloned.1.call-done) | copy-start | bytes 1572868
  540.5 7.3 %copy-start.25 = (f32[192,2048]{1,0:T(8,128)S(1)}, f32[192,2048]{1,0:T(8,128)}, u32[]{:S(2)}) copy-start(f32[192,2048]{1,0:T(8,128)} %get-tuple-element.118) | copy-start | bytes 4718596
  543.3 4.5 copy-start.26
  (38 other events, 82.1 us)
Sparse Core Ops, SparseCore 0:
  22.0 39.7 all-gather.1
  230.8 43.5 reduce-scatter.5
  292.3 44.3 reduce-scatter.7
  345.0 42.8 reduce-scatter.9
  417.4 49.4 reduce-scatter.13
  511.9 52.9 reduce-scatter.11

commit v3 on v2

--- a/solution.py
+++ b/solution.py
@@ -37,56 +37,11 @@
     return lax.dot_general(left_in, right_in, (((1,), (1,)), ((), ())), preferred_element_type=F32)
 
 
-def dp_exchange(part_for):
-    n_dp = lax.axis_size("dp")
-    me = lax.axis_index("dp")
-    arrived = []
-    for k in range(1, n_dp):
-        target = lax.rem(me + k, n_dp)
-        pairs = [(i, (i + k) % n_dp) for i in range(n_dp)]
-        arrived.append(lax.ppermute(part_for(target).astype(BF16), "dp", pairs))
-    total = part_for(me)
-    for piece in arrived:
-        total = total + piece.astype(F32)
-    return total
-
-
-def two_stage(part_for, dim):
-    total = dp_exchange(part_for)
-    return lax.psum_scatter(total.astype(BF16), "seq", scatter_dimension=dim, tiled=True).astype(F32)
-
-
-def from_all_dp(values_in):
-    n_dp = lax.axis_size("dp")
-    pieces = [values_in]
-    for k in range(1, n_dp):
-        pieces.append(lax.ppermute(values_in, "dp", [(i, (i + k) % n_dp) for i in range(n_dp)]))
-    return pieces
-
-
-def columns_from_all_dp(values_in):
-    n_dp = lax.axis_size("dp")
-    me = lax.axis_index("dp")
-    width = values_in.shape[1] // n_dp
-    pieces = [lax.dynamic_slice_in_dim(values_in, me * width, width, 1)]
-    for k in range(1, n_dp):
-        sent = lax.dynamic_slice_in_dim(values_in, lax.rem(me + k, n_dp) * width, width, 1)
-        pieces.append(lax.ppermute(sent, "dp", [(i, (i + k) % n_dp) for i in range(n_dp)]))
-    return pieces
-
-
 def tensor_partners():
     here = lax.axis_index("tensor")
     core = lax.rem(here, 2)
     chip = here // 2
     return here, chip, core, 2 * chip + 1 - core, 2 * (1 - chip) + core
-
-
-def greet(*targets):
-    barrier = pltpu.get_barrier_semaphore()
-    for target in targets:
-        pl.semaphore_signal(barrier, inc=1, device_id={"tensor": target}, device_id_type=MESH)
-    pl.semaphore_wait(barrier, len(targets))
 
 
 def send(source, landing, send_sem, recv_sem, target):
@@ -100,9 +55,38 @@
     )
 
 
-def reduce_kernel(
-    transposed, a_ref, w_ref, o_ref, w_here, part, core_out, core_in, over_out, over_in, w_sem, cs, cr, xs, xr
-):
+def side_copies(plan, sources, landings, send_sems, recv_sems):
+    _, dp_others = others_along("dp")
+    copies = []
+    for i, (source, row, rows, column, width) in enumerate(plan):
+        for k, target in enumerate(dp_others):
+            first = pl.multiple_of(target * width, width) if column is None else column
+            window = sources[source].at[pl.ds(row, rows), pl.ds(first, width)]
+            copies.append(remote(window, landings[i].at[k], send_sems.at[i, k], recv_sems.at[i, k], {"dp": target}))
+    return copies
+
+
+def greet_tensor_and_dp(with_dp):
+    _, _, _, partner, across = tensor_partners()
+    targets = [{"tensor": partner}, {"tensor": across}]
+    if with_dp:
+        targets += [{"dp": other} for other in others_along("dp")[1]]
+    greet_all(targets)
+
+
+def side_shapes(plan, sources):
+    n_far = lax.axis_size("dp") - 1
+    return [jax.ShapeDtypeStruct((n_far, rows, width), sources[i].dtype) for i, _, rows, _, width in plan]
+
+
+def side_sems(plan):
+    return [pltpu.SemaphoreType.DMA((max(len(plan), 1), max(lax.axis_size("dp") - 1, 1)))] * 2
+
+
+def reduce_kernel(transposed, plan, n_sources, a_ref, w_ref, *refs):
+    sources, o_ref, refs = refs[:n_sources], refs[n_sources], refs[n_sources + 1 :]
+    landings, refs = refs[: len(plan)], refs[len(plan) :]
+    w_here, part, core_out, core_in, over_out, over_in, w_sem, cs, cr, xs, xr, side_s, side_r = refs
     n_blocks, width = core_out.shape[0], core_out.shape[-1]
     share = o_ref.shape[0]
     _, chip, core, partner, across = tensor_partners()
@@ -120,7 +104,10 @@
 
     for n in range(n_blocks):
         load(n).start()
-    greet(partner, across)
+    greet_tensor_and_dp(len(plan) > 0)
+    beside = side_copies(plan, sources, landings, side_s, side_r)
+    for copy in beside:
+        copy.start()
 
     def multiply(n):
         load(n).wait()
@@ -161,9 +148,11 @@
         return carry
 
     lax.fori_loop(0, n_blocks, finish, 0)
-
-
-def product_to_owners(name, number, a, w, transposed):
+    for copy in beside:
+        copy.wait()
+
+
+def product_to_owners(name, number, a, w, transposed, sources=(), plan=()):
     tokens, depth = a.shape
     model_width = w.shape[0] if transposed else w.shape[1]
     share = tokens // 4
@@ -171,11 +160,11 @@
     n_blocks = 4
     w_block = (n_blocks, width, depth) if transposed else (n_blocks, depth, width)
     dma = pltpu.SemaphoreType.DMA((n_blocks,))
-    return pl.pallas_call(
-        functools.partial(reduce_kernel, transposed),
-        out_shape=jax.ShapeDtypeStruct((share, model_width), F32),
-        in_specs=[pl.BlockSpec(memory_space=pltpu.VMEM), pl.BlockSpec(memory_space=pl.ANY)],
-        out_specs=pl.BlockSpec(memory_space=pltpu.VMEM),
+    results = pl.pallas_call(
+        functools.partial(reduce_kernel, transposed, plan, len(sources)),
+        out_shape=[jax.ShapeDtypeStruct((share, model_width), F32)] + side_shapes(plan, sources),
+        in_specs=[pl.BlockSpec(memory_space=pltpu.VMEM)] + [pl.BlockSpec(memory_space=pl.ANY)] * (1 + len(sources)),
+        out_specs=[pl.BlockSpec(memory_space=pltpu.VMEM)] + [pl.BlockSpec(memory_space=pltpu.HBM)] * len(plan),
         scratch_shapes=[
             pltpu.VMEM(w_block, BF16),
             pltpu.VMEM((2, 4, share, width), F32),
@@ -188,16 +177,21 @@
             dma,
             dma,
             dma,
-        ],
+        ]
+        + side_sems(plan),
         compiler_params=pltpu.CompilerParams(
             collective_id=number, has_side_effects=True, vmem_limit_bytes=40 * 1024 * 1024
         ),
         cost_estimate=estimate(25),
         name=name,
-    )(a, w)
-
-
-def gather_kernel(own_ref, o_ref, cs, cr, xs, xr, fs, fr):
+    )(a, w, *sources)
+    return results[0] if not plan else results
+
+
+def gather_kernel(plan, n_sources, own_ref, *refs):
+    sources, o_ref, refs = refs[:n_sources], refs[n_sources], refs[n_sources + 1 :]
+    landings, refs = refs[: len(plan)], refs[len(plan) :]
+    cs, cr, xs, xr, fs, fr, side_s, side_r = refs
     n_chunks = cs.shape[0]
     share = own_ref.shape[0]
     rows = share // n_chunks
@@ -207,9 +201,12 @@
         where = pl.ds(n * rows, rows)
         return send(source.at[where], o_ref.at[owner, where], sems[0].at[n], sems[1].at[n], target)
 
-    greet(partner, across)
+    greet_tensor_and_dp(len(plan) > 0)
+    beside = side_copies(plan, sources, landings, side_s, side_r)
     for n in range(n_chunks):
         copy(own_ref, here, n, (xs, xr), across).start()
+    for side in beside:
+        side.start()
     for n in range(n_chunks):
         copy(own_ref, here, n, (cs, cr), partner).start()
     o_ref[here] = own_ref[...]
@@ -220,23 +217,102 @@
         copy(own_ref, here, n, (xs, xr), across).wait_send()
         copy(own_ref, here, n, (cs, cr), partner).wait()
         copy(o_ref.at[across], across, n, (fs, fr), partner).wait()
-
-
-def gather_shares(name, number, own):
+    for side in beside:
+        side.wait()
+
+
+def gather_shares(name, number, own, sources=(), plan=()):
     share, width = own.shape
     dma = pltpu.SemaphoreType.DMA((4,))
-    return pl.pallas_call(
-        gather_kernel,
-        out_shape=jax.ShapeDtypeStruct((4, share, width), own.dtype),
-        in_specs=[pl.BlockSpec(memory_space=pltpu.VMEM)],
-        out_specs=pl.BlockSpec(memory_space=pltpu.VMEM),
-        scratch_shapes=[dma] * 6,
+    results = pl.pallas_call(
+        functools.partial(gather_kernel, plan, len(sources)),
+        out_shape=[jax.ShapeDtypeStruct((4, share, width), own.dtype)] + side_shapes(plan, sources),
+        in_specs=[pl.BlockSpec(memory_space=pltpu.VMEM)] + [pl.BlockSpec(memory_space=pl.ANY)] * len(sources),
+        out_specs=[pl.BlockSpec(memory_space=pltpu.VMEM)] + [pl.BlockSpec(memory_space=pltpu.HBM)] * len(plan),
+        scratch_shapes=[dma] * 6 + side_sems(plan),
         compiler_params=pltpu.CompilerParams(
             collective_id=number, has_side_effects=True, vmem_limit_bytes=16 * 1024 * 1024
         ),
         cost_estimate=estimate(20),
         name=name,
-    )(own).reshape(4 * share, width)
+    )(own, *sources)
+    return (results[0].reshape(4 * share, width), *results[1:])
+
+
+def front_kernel(
+    grad_ref, kv_ref, o_ref, all_ref, cs, cr, xs, xr, fs, fr, zs, zr, kcs, kcr, kxs, kxr, kfs, kfr
+):
+    n_chunks = cs.shape[0]
+    rows = grad_ref.shape[0] // n_chunks
+    here, _, _, partner, across = tensor_partners()
+    seq_me, seq_others = others_along("seq")
+    greet_all([{"tensor": partner}, {"tensor": across}] + [{"seq": other} for other in seq_others])
+
+    def copy(source, owner, n, sems, target):
+        where = pl.ds(n * rows, rows)
+        return send(source.at[where], o_ref.at[owner, where], sems[0].at[n], sems[1].at[n], target)
+
+    def to_seq(source, owner, target):
+        return remote(source, all_ref.at[owner, here], zs.at[target], zr.at[owner], {"seq": target})
+
+    def keys(source, seq, owner, sems, target):
+        return send(source, all_ref.at[seq, owner], sems[0].at[seq], sems[1].at[seq], target)
+
+    for other in seq_others:
+        to_seq(kv_ref, seq_me, other).start()
+    keys(kv_ref, seq_me, here, (kxs, kxr), across).start()
+    keys(kv_ref, seq_me, here, (kcs, kcr), partner).start()
+    for n in range(n_chunks):
+        copy(grad_ref, here, n, (xs, xr), across).start()
+    for n in range(n_chunks):
+        copy(grad_ref, here, n, (cs, cr), partner).start()
+    all_ref[seq_me, here] = kv_ref[...]
+    o_ref[here] = grad_ref[...]
+    for other in seq_others:
+        remote(kv_ref, all_ref.at[other, here], zs.at[other], zr.at[other], {"seq": other}).wait_recv()
+        keys(all_ref.at[other, here], other, here, (kxs, kxr), across).start()
+        keys(all_ref.at[other, here], other, here, (kcs, kcr), partner).start()
+    keys(kv_ref, seq_me, across, (kxs, kxr), across).wait_recv()
+    keys(all_ref.at[seq_me, across], seq_me, across, (kfs, kfr), partner).start()
+    for n in range(n_chunks):
+        copy(grad_ref, here, n, (xs, xr), across).wait_recv()
+        copy(o_ref.at[across], across, n, (fs, fr), partner).start()
+    for other in seq_others:
+        keys(kv_ref, other, across, (kxs, kxr), across).wait_recv()
+        keys(all_ref.at[other, across], other, across, (kfs, kfr), partner).start()
+    for n in range(n_chunks):
+        copy(grad_ref, here, n, (xs, xr), across).wait_send()
+        copy(grad_ref, here, n, (cs, cr), partner).wait()
+        copy(o_ref.at[across], across, n, (fs, fr), partner).wait()
+    for other in seq_others:
+        to_seq(kv_ref, seq_me, other).wait_send()
+    for seq in [seq_me] + seq_others:
+        keys(kv_ref, seq, here, (kxs, kxr), across).wait_send()
+        keys(kv_ref, seq, here, (kcs, kcr), partner).wait()
+        keys(all_ref.at[seq, across], seq, across, (kfs, kfr), partner).wait()
+
+
+def front(number, grad_own, kv_own):
+    n_seq = lax.axis_size("seq")
+    share, width = grad_own.shape
+    dma = pltpu.SemaphoreType.DMA
+    vmem = pl.BlockSpec(memory_space=pltpu.VMEM)
+    grads, kv_all = pl.pallas_call(
+        front_kernel,
+        out_shape=(
+            jax.ShapeDtypeStruct((4, share, width), BF16),
+            jax.ShapeDtypeStruct((n_seq, 4) + kv_own.shape, BF16),
+        ),
+        in_specs=[vmem] * 2,
+        out_specs=(vmem,) * 2,
+        scratch_shapes=[dma((4,))] * 6 + [dma((n_seq,))] * 8,
+        compiler_params=pltpu.CompilerParams(
+            collective_id=number, has_side_effects=True, vmem_limit_bytes=16 * 1024 * 1024
+        ),
+        cost_estimate=estimate(30),
+        name="front",
+    )(grad_own, kv_own)
+    return grads.reshape(4 * share, width), kv_all
 
 
 def remote(source, landing, send_sem, recv_sem, target):
@@ -337,14 +413,24 @@
     )(packed)
 
 
-def kv_kernel(
-    g_ref, o_ref, core_in, over_out, over_in, seq_out, seq_in, own, cs, cr, xs, xr, zs, zr, gs, gr
-):
+def kv_kernel(plan, n_sources, g_ref, two_ref, *refs):
+    sources, o_ref, two_all, refs = refs[:n_sources], refs[n_sources], refs[n_sources + 1], refs[n_sources + 2 :]
+    landings, refs = refs[: len(plan)], refs[len(plan) :]
+    core_in, over_out, over_in, seq_out, seq_in, own = refs[:6]
+    cs, cr, xs, xr, zs, zr, gs, gr, ts, tr, side_s, side_r = refs[6:]
     here, chip, core, partner, across = tensor_partners()
     seq_me, seq_others = others_along("seq")
     greet_all(
-        [{"tensor": partner}, {"tensor": across}] + [{"seq": other} for other in seq_others]
+        [{"tensor": partner}, {"tensor": across}]
+        + [{"seq": other} for other in seq_others]
+        + [{"dp": other} for other in others_along("dp")[1]]
     )
+    beside = side_copies(plan, sources, landings, side_s, side_r)
+    for copy in beside:
+        copy.start()
+
+    def two_copy(source, owner, i, target):
+        return remote(source, two_all.at[owner], ts.at[i], tr.at[i], {"tensor": target})
 
     def to_partner(j):
         return remote(g_ref.at[2 * j + 1 - core], core_in.at[j], cs.at[j], cr.at[j], {"tensor": partner})
@@ -355,6 +441,9 @@
     over_out[...] = (g_ref[2 * (1 - chip) + core].astype(F32) + core_in[1 - chip].astype(F32)).astype(BF16)
     to_across = remote(over_out, over_in, xs.at[0], xr.at[0], {"tensor": across})
     to_across.start()
+    two_copy(two_ref, here, 0, across).start()
+    two_copy(two_ref, here, 1, partner).start()
+    two_all[here] = two_ref[...]
     to_partner(chip).wait()
     to_across.wait()
     seq_out[...] = (
@@ -366,6 +455,8 @@
 
     for other in seq_others:
         to_seq(other).start()
+    two_copy(two_ref, across, 0, across).wait_recv()
+    two_copy(two_all.at[across], across, 2, partner).start()
     total = seq_out[seq_me].astype(F32)
     for other in seq_others:
         remote(seq_out.at[other], seq_in.at[other], zs.at[other], zr.at[other], {"seq": other}).wait_recv()
@@ -384,16 +475,26 @@
     f_copy.wait()
     for other in seq_others:
         to_seq(other).wait_send()
-
-
-def sum_grad_kv(number, parts):
+    two_copy(two_ref, here, 0, across).wait_send()
+    two_copy(two_ref, here, 1, partner).wait()
+    two_copy(two_all.at[across], across, 2, partner).wait()
+    for copy in beside:
+        copy.wait()
+
+
+def sum_grad_kv(number, parts, two_own, sources, plan):
     _, n_seq, share, width = parts.shape
     dma = pltpu.SemaphoreType.DMA
-    return pl.pallas_call(
-        kv_kernel,
-        out_shape=jax.ShapeDtypeStruct((4, share, width), BF16),
-        in_specs=[pl.BlockSpec(memory_space=pltpu.VMEM)],
-        out_specs=pl.BlockSpec(memory_space=pltpu.VMEM),
+    vmem = pl.BlockSpec(memory_space=pltpu.VMEM)
+    results = pl.pallas_call(
+        functools.partial(kv_kernel, plan, len(sources)),
+        out_shape=[
+            jax.ShapeDtypeStruct((4, share, width), BF16),
+            jax.ShapeDtypeStruct((4,) + two_own.shape, BF16),
+        ]
+        + side_shapes(plan, sources),
+        in_specs=[vmem] * 2 + [pl.BlockSpec(memory_space=pl.ANY)] * len(sources),
+        out_specs=[vmem] * 2 + [pl.BlockSpec(memory_space=pltpu.HBM)] * len(plan),
         scratch_shapes=[
             pltpu.VMEM((2, n_seq, share, width), BF16),
             pltpu.VMEM((n_seq, share, width), BF16),
@@ -409,23 +510,319 @@
             dma((n_seq,)),
             dma((3,)),
             dma((3,)),
-        ],
-        compiler_params=pltpu.CompilerParams(collective_id=number, has_side_effects=True),
+            dma((3,)),
+            dma((3,)),
+        ]
+        + side_sems(plan),
+        compiler_params=pltpu.CompilerParams(
+            collective_id=number, has_side_effects=True, vmem_limit_bytes=32 * 1024 * 1024
+        ),
         cost_estimate=estimate(30),
         name="sum_grad_kv",
-    )(parts).reshape(4 * share, width)
+    )(parts, two_own, *sources)
+    return (results[0].reshape(4 * share, width), *results[1:])
 
 
 def estimate(microseconds):
-    return pl.CostEstimate(flops=int(microseconds * 1e9), bytes_accessed=0, transcendentals=0)
-
-
-def together(values, *earlier):
-    return lax.optimization_barrier(tuple(values) + earlier)[: len(values)]
-
-
-def after(value, *earlier):
-    return lax.optimization_barrier((value,) + earlier)[0]
+    return pl.CostEstimate(flops=int(microseconds * 1e6), bytes_accessed=0, transcendentals=0)
+
+
+def attention_kernel(len_ref, q_ref, kv_ref, o_ref, lse_ref, scores):
+    share = o_ref.shape[0] // 4
+    n_rows = len_ref.shape[0]
+    tile = share // n_rows
+    block = 4 * tile
+    head = kv_ref.shape[-1] // 2
+    heads = q_ref.shape[1] // head
+    lanes = heads * tile
+    seq_me = lax.axis_index("seq")
+
+    def one_tile(t, carry):
+        quarter = t // n_rows
+        row = t - quarter * n_rows
+        length = len_ref[row]
+        first = seq_me * block + quarter * tile
+        where = pl.ds(pl.multiple_of(t * tile, tile), tile)
+        own_rows = pl.ds(pl.multiple_of(row * tile, tile), tile)
+
+        @pl.when(first >= length)
+        def _():
+            o_ref[where, :] = jnp.zeros((tile, heads * head), BF16)
+            lse_ref[t] = jnp.zeros((1, lanes), F32)
+
+        @pl.when(first < length)
+        def _():
+            queries = q_ref[where, :]
+            stacked = jnp.concatenate([queries[:, h * head : (h + 1) * head] for h in range(heads)], 0)
+            n_blocks = jnp.minimum(seq_me + 1, (length + block - 1) // block)
+            place = first + lax.rem(lax.broadcasted_iota(jnp.int32, (1, lanes), 1), tile)
+            limit = jnp.minimum(place + 1, length)
+            key_index = lax.broadcasted_iota(jnp.int32, (block, lanes), 0)
+
+            def score(b, highest):
+                keys = kv_ref[b, :, own_rows, :head].reshape(block, head)
+                s = lax.dot_general(keys, stacked, (((1,), (1,)), ((), ())), preferred_element_type=F32)
+                s = jnp.where(key_index < limit - b * block, s, -1e30)
+                scores[b] = s
+                return jnp.maximum(highest, jnp.max(s, 0, keepdims=True))
+
+            highest = lax.fori_loop(0, n_blocks, score, jnp.full((1, lanes), -1e30, F32))
+
+            def mix(b, both):
+                total, mixed = both
+                values = kv_ref[b, :, own_rows, head:].reshape(block, head)
+                p = jnp.exp(scores[b] - highest)
+                total = total + jnp.sum(p, 0, keepdims=True)
+                mixed = mixed + lax.dot_general(
+                    values, p.astype(BF16), (((0,), (0,)), ((), ())), preferred_element_type=F32
+                )
+                return total, mixed
+
+            total, mixed = lax.fori_loop(
+                0, n_blocks, mix, (jnp.zeros((1, lanes), F32), jnp.zeros((head, lanes), F32))
+            )
+            lse_ref[t] = highest + jnp.log(total)
+            back = jnp.transpose(mixed / total)
+            o_ref[where, :] = jnp.concatenate(
+                [back[h * tile : (h + 1) * tile] for h in range(heads)], 1
+            ).astype(BF16)
+
+        return carry
+
+    lax.fori_loop(0, 4 * n_rows, one_tile, 0)
+
+
+def attention(lengths, queries, kv_all):
+    tokens, width = queries.shape
+    n_rows = lengths.shape[0]
+    n_seq, kv_width = kv_all.shape[0], kv_all.shape[-1]
+    tile = tokens // (4 * n_rows)
+    lanes = width // (kv_width // 2) * tile
+    return pl.pallas_call(
+        attention_kernel,
+        out_shape=(
+            jax.ShapeDtypeStruct((tokens, width), BF16),
+            jax.ShapeDtypeStruct((4 * n_rows, 1, lanes), F32),
+        ),
+        in_specs=[pl.BlockSpec(memory_space=pltpu.SMEM)] + [pl.BlockSpec(memory_space=pltpu.VMEM)] * 2,
+        out_specs=(pl.BlockSpec(memory_space=pltpu.VMEM),) * 2,
+        scratch_shapes=[pltpu.VMEM((n_seq, 4 * tile, lanes), F32)],
+        compiler_params=pltpu.CompilerParams(vmem_limit_bytes=24 * 1024 * 1024),
+        cost_estimate=estimate(10),
+        name="attention",
+    )(lengths, queries, kv_all)
+
+
+def attention_back_kernel(len_ref, q_ref, do_ref, kv_ref, lse_ref, dq_ref, dkv_ref, probs, grads, total, keys_t):
+    share = dq_ref.shape[0] // 4
+    n_rows = len_ref.shape[0]
+    tile = share // n_rows
+    block = 4 * tile
+    head = kv_ref.shape[-1] // 2
+    heads = q_ref.shape[1] // head
+    lanes = heads * tile
+    n_seq = total.shape[0]
+    seq_me = lax.axis_index("seq")
+
+    def one_row(row, carry):
+        length = len_ref[row]
+        n_blocks = jnp.minimum(seq_me + 1, (length + block - 1) // block)
+        total[...] = jnp.zeros_like(total)
+        own_rows = pl.ds(pl.multiple_of(row * tile, tile), tile)
+        for b in range(n_seq):
+            keys_t[b] = jnp.transpose(kv_ref[b, :, own_rows, :head].reshape(block, head).astype(F32)).astype(BF16)
+
+        def one_tile(quarter, carry):
+            t = quarter * n_rows + row
+            first = seq_me * block + quarter * tile
+            where = pl.ds(pl.multiple_of(t * tile, tile), tile)
+
+            @pl.when(first >= length)
+            def _():
+                dq_ref[where, :] = jnp.zeros((tile, heads * head), BF16)
+
+            @pl.when(first < length)
+            def _():
+                def stack(ref):
+                    rows = ref[where, :]
+                    return jnp.concatenate([rows[:, h * head : (h + 1) * head] for h in range(heads)], 0)
+
+                stacked = stack(q_ref)
+                outer = stack(do_ref)
+                lse = lse_ref[t]
+                place = first + lax.rem(lax.broadcasted_iota(jnp.int32, (1, lanes), 1), tile)
+                limit = jnp.minimum(place + 1, length)
+                key_index = lax.broadcasted_iota(jnp.int32, (block, lanes), 0)
+
+                def score(b, inner):
+                    keys = kv_ref[b, :, own_rows, :head].reshape(block, head)
+                    values = kv_ref[b, :, own_rows, head:].reshape(block, head)
+                    s = lax.dot_general(keys, stacked, (((1,), (1,)), ((), ())), preferred_element_type=F32)
+                    p = jnp.where(key_index < limit - b * block, jnp.exp(s - lse), 0.0)
+                    g = lax.dot_general(values, outer, (((1,), (1,)), ((), ())), preferred_element_type=F32)
+                    probs[b] = p
+                    grads[b] = g
+                    total[b, :, head:] += jnp.dot(p.astype(BF16), outer, preferred_element_type=F32)
+                    return inner + jnp.sum(p * g, 0, keepdims=True)
+
+                inner = lax.fori_loop(0, n_blocks, score, jnp.zeros((1, lanes), F32))
+
+                def back(b, dq):
+                    ds = (probs[b] * (grads[b] - inner)).astype(BF16)
+                    total[b, :, :head] += jnp.dot(ds, stacked, preferred_element_type=F32)
+                    return dq + jnp.dot(keys_t[b], ds, preferred_element_type=F32)
+
+                dq = jnp.transpose(lax.fori_loop(0, n_blocks, back, jnp.zeros((head, lanes), F32)))
+                dq_ref[where, :] = jnp.concatenate(
+                    [dq[h * tile : (h + 1) * tile] for h in range(heads)], 1
+                ).astype(BF16)
+
+            return carry
+
+        lax.fori_loop(0, 4, one_tile, 0)
+        for quarter in range(4):
+            for b in range(n_seq):
+                dkv_ref[quarter, b, own_rows, :] = total[b, quarter * tile : (quarter + 1) * tile, :].astype(BF16)
+        return carry
+
+    lax.fori_loop(0, n_rows, one_row, 0)
+
+
+def attention_back(lengths, queries, grad_mixed, kv_all, lse):
+    tokens, width = queries.shape
+    n_rows = lengths.shape[0]
+    n_seq, kv_width = kv_all.shape[0], kv_all.shape[-1]
+    tile = tokens // (4 * n_rows)
+    lanes = width // (kv_width // 2) * tile
+    block = 4 * tile
+    return pl.pallas_call(
+        attention_back_kernel,
+        out_shape=(
+            jax.ShapeDtypeStruct((tokens, width), BF16),
+            jax.ShapeDtypeStruct((4, n_seq, tokens // 4, kv_width), BF16),
+        ),
+        in_specs=[pl.BlockSpec(memory_space=pltpu.SMEM)] + [pl.BlockSpec(memory_space=pltpu.VMEM)] * 4,
+        out_specs=(pl.BlockSpec(memory_space=pltpu.VMEM),) * 2,
+        scratch_shapes=[
+            pltpu.VMEM((n_seq, block, lanes), F32),
+            pltpu.VMEM((n_seq, block, lanes), F32),
+            pltpu.VMEM((n_seq, block, kv_width), F32),
+            pltpu.VMEM((n_seq, kv_width // 2, block), BF16),
+        ],
+        compiler_params=pltpu.CompilerParams(vmem_limit_bytes=32 * 1024 * 1024),
+        cost_estimate=estimate(25),
+        name="attention_back",
+    )(lengths, queries, grad_mixed, kv_all, lse)
+
+
+def last_kernel(
+    q_ref, kv_ref, out_ref, q_sum, kv_sum, out_sum,
+    packed, dp_in, near_out, near_in, far_out, far_in, total, ys, yr, ns, nr, fs, fr,
+):
+    rows = q_ref.shape[2]
+    kv_rows, kv_width = kv_ref.shape[3:]
+    per_line = q_ref.shape[3] // kv_width
+    lines = kv_rows // per_line
+    here = lax.axis_index("tensor")
+    dp_me, dp_others = others_along("dp")
+    seq_me = lax.axis_index("seq")
+    beside = seq_me + 1 - 2 * lax.rem(seq_me, 2)
+    far = seq_me + 2 - 4 * (seq_me // 2)
+    opposite = 3 - seq_me
+    greet_all([{"dp": other} for other in dp_others] + [{"seq": beside}, {"seq": far}])
+
+    def to_dp(k, b):
+        return remote(packed.at[dp_others[k], b], dp_in.at[k, b], ys.at[k, b], yr.at[k, b], {"dp": dp_others[k]})
+
+    def pack(d, b):
+        packed[d, b, :rows] = q_ref[d, b]
+        packed[d, b, rows : 2 * rows] = out_ref[d, b]
+        for i in range(per_line):
+            packed[d, b, 2 * rows :, i * kv_width : (i + 1) * kv_width] = kv_ref[
+                d, b, here, i * lines : (i + 1) * lines
+            ]
+
+    order = (beside, opposite, far, seq_me)
+    for b in order:
+        for k, d in enumerate(dp_others):
+            pack(d, b)
+            to_dp(k, b).start()
+    for b in order:
+        pack(dp_me, b)
+
+    def summed(b):
+        value = packed[dp_me, b].astype(F32)
+        for k in range(len(dp_others)):
+            to_dp(k, b).wait_recv()
+            value = value + dp_in[k, b].astype(F32)
+        return value
+
+    def to_beside(i):
+        return remote(near_out.at[i], near_in.at[i], ns.at[i], nr.at[i], {"seq": beside})
+
+    near_out[0] = summed(beside).astype(BF16)
+    near_out[1] = summed(opposite).astype(BF16)
+    to_beside(1).start()
+    to_beside(0).start()
+    total[...] = summed(far)
+    to_beside(1).wait_recv()
+    far_out[...] = (total[...] + near_in[1].astype(F32)).astype(BF16)
+    to_far = remote(far_out, far_in, fs.at[0], fr.at[0], {"seq": far})
+    to_far.start()
+    total[...] = summed(seq_me)
+    to_beside(0).wait_recv()
+    total[...] += near_in[0].astype(F32)
+    to_far.wait_recv()
+    total[...] += far_in[...].astype(F32)
+    q_sum[...] = total[:rows]
+    out_sum[...] = jnp.transpose(total[rows : 2 * rows])
+    for i in range(per_line):
+        kv_sum[i * lines : (i + 1) * lines] = total[2 * rows :, i * kv_width : (i + 1) * kv_width]
+    for b in order:
+        for k in range(len(dp_others)):
+            to_dp(k, b).wait_send()
+    to_beside(0).wait_send()
+    to_beside(1).wait_send()
+    to_far.wait_send()
+
+
+def sum_last(number, q_part, kv_part, out_part):
+    n_dp, n_seq, rows, width = q_part.shape
+    kv_rows, kv_width = kv_part.shape[3:]
+    block = (2 * rows + kv_rows * kv_width // width, width)
+    n_far = n_dp - 1
+    dma = pltpu.SemaphoreType.DMA
+    vmem = pl.BlockSpec(memory_space=pltpu.VMEM)
+    return pl.pallas_call(
+        last_kernel,
+        out_shape=(
+            jax.ShapeDtypeStruct((rows, width), F32),
+            jax.ShapeDtypeStruct((kv_rows, kv_width), F32),
+            jax.ShapeDtypeStruct((width, rows), F32),
+        ),
+        in_specs=[vmem] * 3,
+        out_specs=(vmem,) * 3,
+        scratch_shapes=[
+            pltpu.VMEM((n_dp, n_seq) + block, BF16),
+            pltpu.VMEM((n_far, n_seq) + block, BF16),
+            pltpu.VMEM((2,) + block, BF16),
+            pltpu.VMEM((2,) + block, BF16),
+            pltpu.VMEM(block, BF16),
+            pltpu.VMEM(block, BF16),
+            pltpu.VMEM(block, F32),
+            dma((n_far, n_seq)),
+            dma((n_far, n_seq)),
+            dma((2,)),
+            dma((2,)),
+            dma((1,)),
+            dma((1,)),
+        ],
+        compiler_params=pltpu.CompilerParams(
+            collective_id=number, has_side_effects=True, vmem_limit_bytes=48 * 1024 * 1024
+        ),
+        cost_estimate=estimate(70),
+        name="sum_last",
+    )(q_part, kv_part, out_part)
 
 
 def shards(
@@ -454,7 +851,6 @@
     share_len = seq_len // n_tensor
     tensor_index = lax.axis_index("tensor")
     seq_index = lax.axis_index("seq")
-    full_len = seq_len * n_seq
     head_size = w_kv.shape[1] // 2
     num_heads = w_query.shape[1] // head_size
     q_scale = 1.0 / math.sqrt(head_size)
@@ -464,137 +860,96 @@
     def by_share(values_in):
         return jnp.moveaxis(values_in.reshape((n_rows, n_tensor, share_len) + values_in.shape[2:]), 1, 0)
 
-    def by_row(values_in):
-        return jnp.moveaxis(
-            values_in.reshape((n_tensor, n_rows, share_len) + values_in.shape[1:]), 0, 1
-        ).reshape((n_rows, seq_len) + values_in.shape[1:])
-
     def own_share(values_in):
         return lax.dynamic_index_in_dim(values_in.reshape((n_tensor, n_own) + values_in.shape[1:]), tensor_index, 0, False)
 
     positions = seq_index * seq_len + jnp.arange(seq_len, dtype=jnp.int32)
-    key_places = jnp.arange(full_len, dtype=jnp.int32)
     is_valid = (positions[None, :] < lengths[:, None]).astype(F32)
-    allowed_keys = (key_places[None, None, :] <= positions[None, :, None]) & (
-        key_places[None, None, :] < lengths[:, None, None]
-    )
     valid_own = own_share(by_share(is_valid).reshape(n_tok))[:, None]
     grad_y_own = cotangent.reshape(n_own, model_width).astype(F32) * valid_own
     x_float = by_share(layer_input).reshape(n_tok, model_width).astype(F32)
     normed_x1, inv_one = normalize(x_float)
     flat_one = (normed_x1 * ln1_gain + ln1_bias).astype(BF16)
     kv_bias = jnp.concatenate([jnp.zeros((head_size,), F32), b_value.astype(F32)])
-    kv_local = (jnp.dot(flat_one, w_kv, preferred_element_type=F32) + kv_bias).astype(BF16)
-    kv_all = lax.all_gather(by_row(kv_local), "seq", axis=1, tiled=True)
+    kv_own = (jnp.dot(own_share(flat_one), w_kv, preferred_element_type=F32) + kv_bias).astype(BF16)
     queries = ((jnp.dot(flat_one, w_query, preferred_element_type=F32) + b_query) * q_scale).astype(BF16)
-    queries = by_row(queries).reshape(n_rows, seq_len, num_heads, head_size)
-    key_rows = kv_all[..., :head_size]
-    value_rows = kv_all[..., head_size:]
-    grad_y_low = gather_shares("gather_grad_y", 0, grad_y_own.astype(BF16))
-    grad_y_columns = columns_from_all_dp(grad_y_low)
-
-    def scores_of(query_rows):
-        raw_scores = jnp.einsum("rshd,rld->rhsl", query_rows, key_rows, preferred_element_type=F32)
-        return jnp.where(allowed_keys[:, None], raw_scores, -1e30)
-
-    scores = scores_of(queries)
-    row_max = jnp.max(scores, -1, keepdims=True)
-    exp_scores = jnp.exp(scores - row_max)
-    exp_total = jnp.sum(exp_scores, -1, keepdims=True)
-    soft_probs = exp_scores / exp_total
-    log_total = row_max + jnp.log(exp_total)
-    mixed_heads = jnp.einsum(
-        "rhsl,rld->rshd", soft_probs.astype(BF16), value_rows, preferred_element_type=F32
-    ).astype(BF16)
-    mixed_heads = by_share(mixed_heads).reshape(n_tok, num_heads * head_size)
-    attn_own = product_to_owners("attn_out", 1, mixed_heads, w_out, False)
+    grad_y_low, kv_all = front(0, grad_y_own.astype(BF16), kv_own)
+
+    half_width = model_width // n_dp
+    hidden = w_up.shape[1]
+    chunk = hidden // 8
+    dp_me = lax.axis_index("dp")
+
+    def own_columns(values_in):
+        return lax.dynamic_slice_in_dim(values_in, dp_me * half_width, half_width, 1)
+
+    mixed_heads, log_total = attention(lengths, queries, kv_all)
+    attn_own, grad_y_far_a = product_to_owners(
+        "attn_out", 1, mixed_heads, w_out, False, (grad_y_low,), ((0, 0, n_tok // 2, None, half_width),)
+    )
     x_own = own_share(x_float)
     resid_own = x_own + (attn_own + b_out)
     normed_x2, inv_two = normalize(resid_own)
     normed_two = (normed_x2 * ln2_gain + ln2_bias).astype(BF16)
-    flat_two = gather_shares("gather_norm_two", 2, normed_two)
-    two_columns = columns_from_all_dp(flat_two)
+    flat_two, grad_y_far_b = gather_shares(
+        "gather_norm_two", 2, normed_two, (grad_y_low,), ((0, n_tok // 2, n_tok // 2, None, half_width),)
+    )
     pre_act = jnp.dot(flat_two, w_up, preferred_element_type=F32) + b_up
     activated, gelu_pull = jax.vjp(lambda inner_in: jax.nn.gelu(inner_in, approximate=True), pre_act)
     act_low = activated.astype(BF16)
     grad_act = times_transposed(grad_y_low, w_down)
     grad_pre = gelu_pull(grad_act)[0].astype(BF16)
-    grad_pre, act_low = lax.optimization_barrier((grad_pre, act_low))
-
-    half_width = model_width // n_dp
-    half_hidden = act_low.shape[1] // 2
-
-    def columns(values_in, d):
-        return lax.dynamic_slice_in_dim(values_in, d * half_width, half_width, 1)
-
-    def summed_products(lefts, rights, dim):
-        total = across_rows(lefts[0], rights[0])
-        for left_in, right_in in zip(lefts[1:], rights[1:]):
-            total = total + across_rows(left_in, right_in)
-        return total.astype(BF16)
-
-    def over_seq(values_in, dim):
-        return lax.psum_scatter(values_in, "seq", scatter_dimension=dim, tiled=True)
-
-    act_a = from_all_dp(act_low[:, :half_hidden])
-    grad_n2 = product_to_owners("grad_norm_two", 3, grad_pre, w_up, True)
+
+    def window(source, first, count):
+        return (source, 0, n_tok, first * chunk, count * chunk)
+
+    grad_n2, act_far_a, two_far_own = product_to_owners(
+        "grad_norm_two", 3, grad_pre, w_up, True, (act_low, normed_two), (window(0, 0, 3), (1, 0, n_own, None, half_width))
+    )
     grad_resid = grad_y_own + norm_back(grad_n2, normed_x2, inv_two, ln2_gain)
     grad_resid_low = grad_resid.astype(BF16)
-    act_b = from_all_dp(after(act_low[:, half_hidden:], grad_resid_low))
-    act_a = together(act_a, grad_resid_low, *two_columns)
-    part_a = summed_products(act_a, grad_y_columns, 1)
-    g_w_down_a = over_seq(part_a, 1)
-    flat_resid = gather_shares("gather_grad_resid", 4, after(grad_resid_low, part_a))
-    pre_a = from_all_dp(after(grad_pre[:, :half_hidden], flat_resid))
-    mlp_own = product_to_owners("mlp_out", 5, after(act_low, flat_resid), w_down, False) + b_down
-    part_b = summed_products(together(act_b, mlp_own, g_w_down_a), grad_y_columns, 1)
-    g_w_down_b = over_seq(part_b, 1)
-    pre_b = from_all_dp(after(grad_pre[:, half_hidden:], part_b))
-    flat_resid = after(flat_resid, part_b)
+    flat_resid, act_far_b = gather_shares("gather_grad_resid", 4, grad_resid_low, (act_low,), (window(0, 3, 3),))
     grad_mixed = times_transposed(flat_resid, w_out).astype(BF16)
-    grad_mixed = by_row(grad_mixed).reshape(n_rows, seq_len, num_heads, head_size)
-    again_probs = jnp.exp(scores_of(queries) - log_total)
-    grad_probs = jnp.einsum("rshd,rld->rhsl", grad_mixed, value_rows, preferred_element_type=F32)
-    inner_sum = jnp.sum(again_probs * grad_probs, -1, keepdims=True)
-    grad_scores = (again_probs * (grad_probs - inner_sum)).astype(BF16)
-    grad_query = jnp.einsum("rhsl,rld->rshd", grad_scores, key_rows, preferred_element_type=F32).astype(BF16)
-    grad_keys = jnp.einsum("rhsl,rshd->rld", grad_scores, queries, preferred_element_type=F32)
-    grad_values = jnp.einsum(
-        "rhsl,rshd->rld", again_probs.astype(BF16), grad_mixed, preferred_element_type=F32
+    flat_query, grad_kv = attention_back(lengths, queries, grad_mixed, kv_all, log_total)
+    grad_n1, act_far_c, pre_far_a = product_to_owners(
+        "grad_norm_one", 6, flat_query, w_query, True, (act_low, grad_pre), (window(0, 6, 2), window(1, 0, 1))
     )
-    grad_kv = jnp.concatenate([grad_keys, grad_values], -1).astype(BF16)
-    flat_query = by_share(grad_query).reshape(n_tok, num_heads * head_size)
-    up_a = summed_products(two_columns, together(pre_a, flat_query, grad_kv, g_w_down_b), 0)
-    g_w_up_a = over_seq(up_a, 0)
-    flat_query, grad_kv, _ = lax.optimization_barrier((flat_query, grad_kv, up_a))
-    grad_kv = jnp.transpose(
-        grad_kv.reshape(n_rows, n_seq, n_tensor, share_len, 2 * head_size), (2, 1, 0, 3, 4)
-    ).reshape(n_tensor, n_seq, n_own, 2 * head_size)
-    flat_kv = sum_grad_kv(7, grad_kv)
-    kv_columns = lax.dynamic_index_in_dim(
-        flat_one.reshape(n_tok, n_dp * n_seq, n_tensor, model_width // (n_dp * n_seq * n_tensor)), tensor_index, 2, False
-    )
-
-    def first_part(d):
-        query_part = across_rows(columns(flat_one, d), flat_query) * q_scale
-        kv_side = lax.dynamic_slice_in_dim(kv_columns, d * n_seq, n_seq, 1).reshape(n_tok, -1)
-        kv_part = across_rows(kv_side, flat_kv)
-        out_part = across_rows(columns(flat_resid, d), mixed_heads)
-        pieces = [p.reshape(n_seq, -1, query_part.shape[1]) for p in (query_part, kv_part, out_part)]
-        return jnp.concatenate(pieces, 1)
-
-    last_part = dp_exchange(first_part)
-    grad_n1 = product_to_owners("grad_norm_one", 6, after(flat_query, flat_kv), w_query, True) * q_scale
-    up_b = summed_products(two_columns, together(pre_b, grad_n1, g_w_up_a), 0)
-    g_w_up_b = over_seq(up_b, 0)
-    last_part = after(last_part, up_b).astype(BF16)
-    last_sum = lax.psum_scatter(last_part, "seq", scatter_dimension=0, tiled=True)[0].astype(F32)
-    last_rows = model_width // (n_dp * n_seq)
-    g_w_query = last_sum[:last_rows]
-    g_w_out = jnp.transpose(last_sum[-last_rows:])
-    g_w_kv = last_sum[last_rows:-last_rows].reshape(-1, 2 * head_size)
-    g_w_down = jnp.concatenate([g_w_down_a, g_w_down_b], 0).astype(F32)
-    g_w_up = jnp.concatenate([g_w_up_a, g_w_up_b], 1).astype(F32)
+    grad_n1 = grad_n1 * q_scale
+    two_swapped = jnp.swapaxes(two_far_own, 0, 1).reshape(n_own, -1)
+    flat_kv, two_far, pre_far_b = sum_grad_kv(7, grad_kv, two_swapped, (grad_pre,), (window(0, 1, 4),))
+    mlp_own, pre_far_c = product_to_owners("mlp_out", 5, act_low, w_down, False, (grad_pre, flat_kv), (window(0, 5, 3),))
+    mlp_own = mlp_own + b_down
+
+    grad_y_far = jnp.concatenate([grad_y_far_a, grad_y_far_b], 1)
+    grad_y_here = own_columns(grad_y_low)
+    two_here = own_columns(flat_two)
+    two_far = two_far.reshape(n_tok, n_dp - 1, half_width)
+
+    def part_down(first, count, far):
+        total = across_rows(act_low[:, first * chunk : (first + count) * chunk], grad_y_here)
+        for k in range(n_dp - 1):
+            total = total + across_rows(far[k], grad_y_far[k])
+        return lax.psum_scatter(total.astype(BF16), "seq", scatter_dimension=1, tiled=True)
+
+    def part_up(first, count, fars):
+        total = across_rows(two_here, grad_pre[:, first * chunk : (first + count) * chunk])
+        for k in range(n_dp - 1):
+            far = jnp.concatenate([piece[k] for piece in fars], 1) if len(fars) > 1 else fars[0][k]
+            total = total + across_rows(two_far[:, k], far)
+        return lax.psum_scatter(total.astype(BF16), "seq", scatter_dimension=0, tiled=True)
+
+    g_w_down = jnp.concatenate([part_down(0, 3, act_far_a), part_down(3, 3, act_far_b), part_down(6, 2, act_far_c)], 0)
+    g_w_up = jnp.concatenate([part_up(0, 5, (pre_far_a, pre_far_b)), part_up(5, 3, (pre_far_c,))], 1)
+    g_w_down = g_w_down.astype(F32)
+    g_w_up = g_w_up.astype(F32)
+
+    def by_owner(values_in, *between):
+        return values_in.astype(BF16).reshape((n_dp, n_seq) + between + (-1, values_in.shape[1]))
+
+    q_part = by_owner(across_rows(flat_one, flat_query) * q_scale)
+    kv_part = by_owner(across_rows(flat_one, flat_kv), n_tensor)
+    out_part = by_owner(across_rows(flat_resid, mixed_heads))
+    g_w_query, g_w_kv, g_w_out = sum_last(9, q_part, kv_part, out_part)
     y_own = (valid_own * (resid_own + mlp_own)).astype(BF16).reshape(n_rows, share_len, model_width)
 
     own_kv = own_share(flat_kv)

time: 584 us -> 532 us (0.911); the launches traced: 577 us -> 532 us
  Pallas kernels: 216 us -> 363 us
  waiting for transfers between devices: 80.9 us -> 0.11 us
  local copies, waits for them, and re-layouts: 91.8 us -> 47.9 us
  matrix products: 111 us -> 69.2 us
  other arithmetic: 52.8 us -> 35.7 us
  starting transfers between devices: 7.88 us -> 0.38 us
    pallas_call x8 -> x11, Pallas kernels: 194 us -> 347 us  [the longest x4 114 us: product_to_owners(): pl.pallas_call(functools.partial(reduce_kernel, transposed, plan, len(sou...]
    ppermute x7 -> x0, waiting for transfers between devices: 66 us -> none  [the longest x2 33.7 us: columns_from_all_dp(): lax.ppermute(sent, 'dp', [(i, (i + k) % n_dp) for i in range(n_dp)])]
    dot_general x7 -> x1, matrix products: 30.6 us -> 0.4 us  [shards(): jnp.dot(own_share(flat_one), w_kv, preferred_element_type=F32) + kv_bias]
    dynamic_slice x5 -> x0, local copies, waits for them, and re-layouts: 18.3 us -> none  [the longest x3 14 us: first_part(): lax.dynamic_slice_in_dim(kv_columns, d * n_seq, n_seq, 1).reshape(n_tok, -1)]
    reduce_scatter x5, waiting for transfers between devices: 14.8 us -> 0.03 us  [the longest x3 0.02 us: part_down(): lax.psum_scatter(total.astype(BF16), 'seq', scatter_dimension=1, tiled=True)]
    convert_element_type x2 -> x1, local copies, waits for them, and re-layouts: 16.7 us -> 6.28 us  [shards(): x_float = by_share(layer_input).reshape(n_tok, model_width).astype(F32)]
    dot_general x14 -> x13, matrix products: 44.4 us -> 35.7 us  [across_rows(): lax.dot_general(left_in, right_in, (((0,), (0,)), ((), ())), preferred_el...]
    convert_element_type x4, other arithmetic: 12.5 us -> 4.22 us  [shards(): flat_one = (normed_x1 * ln1_gain + ln1_bias).astype(BF16)]
  transfers between devices with their start and end apart: 13 -> 5, of which waited for: 6 -> 0; matrix products, arithmetic and copies ran while one was open for 36% -> 14% of each run, Pallas kernels for 38% -> 33%
where the time goes in v3:
time: 532 us
  Pallas kernels  363 us (68%)
  matrix products  69.2 us (13%)
  local copies, waits for them, and re-layouts  47.9 us (9%)
  other arithmetic  35.7 us (7%)
  between operations  15.1 us (3%)
    pallas_call x4, Pallas kernels, product_to_owners(): pl.pallas_call(functools.partial(reduce_kernel, transposed, plan, len(sou...  114 us
    pallas_call x1, Pallas kernels, sum_last(): pl.pallas_call(last_kernel, out_shape=(jax.ShapeDtypeStruct((rows, width)...  74.2 us
    pallas_call x1, Pallas kernels, sum_grad_kv(): pl.pallas_call(functools.partial(kv_kernel, plan, len(sources)), out_shap...  58.5 us
    pallas_call x2, Pallas kernels, gather_shares(): pl.pallas_call(functools.partial(gather_kernel, plan, len(sources)), out_...  49 us
    dot_general x13, matrix products, across_rows(): lax.dot_general(left_in, right_in, (((0,), (0,)), ((), ())), preferred_el...  35.7 us
    pallas_call x1, Pallas kernels, front(): pl.pallas_call(front_kernel, out_shape=(jax.ShapeDtypeStruct((4, share, w...  33.8 us
    unnamed x153, local copies, waits for them, and re-layouts  23.1 us
    dot_general x3, matrix products, times_transposed(): lax.dot_general(left_in, right_in, (((1,), (1,)), ((), ())), preferred_el...  20.5 us
  transfers between devices with their start and end apart: 5, of which 0 were waited for; matrix products, arithmetic and copies ran while one was open for 14% of the time, Pallas kernels for 33%

profile of v3, /device:TPU:0, one launch (start us, length us, event | category | flops | bytes accessed | tf_op | source)
XLA Modules:
  0.0 531.7 jit_solution(15837676297297192538)
XLA Ops:
  7.2 5.5 %convert_bitcast_fusion = f32[4,3,64,2048]{3,2,0,1:T(8,128)} fusion(bf16[3,256,2048]{2,1,0:T(8,128)(2,1)} %param.17), kind=kLoop, calls=%fused_computation.14 | loop fusion | flops 1572864 | bytes 9437184 | tf_op jit(solution)/shard_map/convert_element_type | solution.py:870
  14.7 6.3 %copy.51 = f32[4,3,64,2048]{3,2,1,0:T(8,128)} copy(f32[4,3,64,2048]{3,2,0,1:T(8,128)} %convert_bitcast_fusion) | data formatting | bytes 12582912 | tf_op jit(solution)/shard_map/convert_element_type | solution.py:870
  22.8 3.5 subtract_multiply_fusion
  28.4 1.5 copy-done.49
  30.3 33.8 %front.1 = (bf16[4,192,2048]{2,1,0:T(8,128)(2,1)S(1)}, bf16[4,4,192,256]{3,2,1,0:T(8,128)(2,1)S(1)}) custom-call(bf16[192,2048]{1,0:T(8,128)(2,1)S(1)} %fusion.22.grad_ref, bf16[192,256]{1,0:T(8,128)(2,1)S(1)} %fusion.38.kv_ref), custom_call_target="tpu_custom_call" | custom-call | flops 30000000 | tf_op jit(solution)/shard_map/front/pallas_call | solution.py:300
  64.1 1.8 multiply_convert_fusion.3.q_ref
  65.9 7.5 %attention.1 = (bf16[768,512]{1,0:T(8,128)(2,1)S(1)}, f32[12,1,256]{2,1,0:T(1,128)S(1)}) custom-call(s32[3]{0:T(128)S(1)} %copy-done.21, bf16[768,512]{1,0:T(8,128)(2,1)S(1)} %multiply_convert_fusion.3.q_ref, bf16[4,4,192,256]{3,2,1,0:T(8,128)(2,1)S(1)} %get-tuple-element.37.kv_ref), custom_call_target="tpu_custom_call" | custom-call | flops 10000000 | tf_op jit(solution)/shard_map/attention/pallas_call | solution.py:601
  73.4 22.8 %attn_out.1 = (f32[192,2048]{1,0:T(8,128)S(1)}, bf16[1,384,1024]{2,1,0:T(8,128)(2,1)S(1)}) custom-call(bf16[768,512]{1,0:T(8,128)(2,1)S(1)} %get-tuple-element.38.a_ref, bf16[512,2048]{1,0:T(8,128)(2,1)S(1)} %copy-done.7, bf16[768,2048]{1,0:T(8,128)(2,1)S(1)} %bitcast.116), custom_call_target="tpu_custom_call" | custom-call | flops 25000000 | tf_op jit(solution)/shard_map/attn_out/pallas_call | solution.py:163
  97.8 21.0 %gather_norm_two.1 = (bf16[4,192,2048]{2,1,0:T(8,128)(2,1)S(1)}, bf16[1,384,1024]{2,1,0:T(8,128)(2,1)S(1)}) custom-call(bf16[192,2048]{1,0:T(8,128)(2,1)S(1)} %add_convert_fusion.6.own_ref.refs_1_, bf16[768,2048]{1,0:T(8,128)(2,1)S(1)} %bitcast.117), custom_call_target="tpu_custom_call" | custom-call | flops 20000000 | tf_op jit(solution)/shard_map/gather_norm_two/pallas_call | solution.py:227
  118.9 1.6 copy-done.24
  120.5 10.8 %fusion.58 = f32[768,2048]{1,0:T(8,128)} fusion(bf16[768,2048]{1,0:T(8,128)(2,1)S(1)} %bitcast.129, bf16[2048,2048]{1,0:T(8,128)(2,1)} %w_ref.5), kind=kOutput, calls=%fused_computation.124 | convolution fusion | flops 6442450944 | bytes 17825792 | tf_op jit(solution)/shard_map/dot_general | solution.py:897
  131.3 14.3 %convert_reduce_fusion = (f32[2048]{0:T(1024)S(1)}, bf16[768,2048]{1,0:T(8,128)(2,1)S(1)}, bf16[768,2048]{1,0:T(8,128)(2,1)S(1)}) fusion(f32[768,2048]{1,0:T(8,128)} %fusion.58, f32[2048]{0:T(1024)S(1)} %convert_element_type.180, bf16[768,2048]{1,0:T(8,128)(2,1)S(1)} %bitcast.118, bf16[2048,2048]{1,0:T(8,128)(2,1)} %w_ref.6), kind=kOutput, calls=%fused_computation.15 | convolution fusion | flops 6481770496 | bytes 24133632 | tf_op jit(solution)/shard_map/dot_general | solution.py:37
  145.6 36.9 %grad_norm_two.1 = (f32[192,2048]{1,0:T(8,128)S(1)}, bf16[1,768,768]{2,1,0:T(8,128)(2,1)S(1)}, bf16[1,192,1024]{2,1,0:T(8,128)(2,1)S(1)}) custom-call(bf16[768,2048]{1,0:T(8,128)(2,1)S(1)} %get-tuple-element.77.a_ref.refs_0_.refs_1_, bf16[2048,2048]{1,0:T(8,128)(2,1)} %w_ref.5, bf16[768,2048]{1,0:T(8,128)(2,1)S(1)} %get-tuple-element.80.refs_0_.a_ref, ...), custom_call_target="tpu_custom_call" | custom-call | flops 25000000 | tf_op jit(solution)/shard_map/grad_norm_two/pallas_call | solution.py:163
  182.6 1.3 multiply_reduce_fusion.2
  184.3 2.5 convert_reduce_fusion.1
  186.9 28.0 %gather_grad_resid.1 = (bf16[4,192,2048]{2,1,0:T(8,128)(2,1)S(1)}, bf16[1,768,768]{2,1,0:T(8,128)(2,1)S(1)}) custom-call(bf16[192,2048]{1,0:T(8,128)(2,1)S(1)} %get-tuple-element.74.own_ref, bf16[768,2048]{1,0:T(8,128)(2,1)S(1)} %get-tuple-element.80.refs_0_.a_ref), custom_call_target="tpu_custom_call" | custom-call | flops 20000000 | tf_op jit(solution)/shard_map/gather_grad_resid/pallas_call | solution.py:227
  214.9 1.8 convolution_convert_fusion.2.do_ref
  217.0 9.8 %attention_back.1 = (bf16[768,512]{1,0:T(8,128)(2,1)S(1)}, bf16[4,4,192,256]{3,2,1,0:T(8,128)(2,1)S(1)}) custom-call(s32[3]{0:T(128)S(1)} %copy-done.21, bf16[768,512]{1,0:T(8,128)(2,1)S(1)} %multiply_convert_fusion.3.q_ref, bf16[768,512]{1,0:T(8,128)(2,1)S(1)} %convolution_convert_fusion.2.do_ref, bf16[4,4,192,256]{3,2,1,0:T(8,128)(2,1)S(1)} %get-tuple-element.37.kv_ref, ...), custom_call_target="tpu_custom_call" | custom-call | flops 25000000 | tf_op jit(solution)/shard_map/attention_back/pallas_call | solution.py:698
  226.8 28.0 %grad_norm_one.1 = (f32[192,2048]{1,0:T(8,128)S(1)}, bf16[1,768,512]{2,1,0:T(8,128)(2,1)S(1)}, bf16[1,768,256]{2,1,0:T(8,128)(2,1)S(1)}) custom-call(bf16[768,512]{1,0:T(8,128)(2,1)S(1)} %get-tuple-element.49.a_ref, bf16[2048,512]{1,0:T(8,128)(2,1)S(1)} %copy-done.9, bf16[768,2048]{1,0:T(8,128)(2,1)S(1)} %get-tuple-element.80.refs_0_.a_ref, ...), custom_call_target="tpu_custom_call" | custom-call | flops 25000000 | tf_op jit(solution)/shard_map/grad_norm_one/pallas_call | solution.py:163
  254.8 1.1 copy-done.10
  257.6 2.8 fusion.26
  260.4 2.0 add_convert_fusion.5
  262.5 3.3 fusion.28
  265.9 2.7 add_convert_fusion.2
  268.7 3.3 fusion.30
  272.1 2.7 add_convert_fusion.3
  274.8 1.9 copy-done.4
  277.7 58.5 %sum_grad_kv.1 = (bf16[4,192,256]{2,1,0:T(8,128)(2,1)S(1)}, bf16[4,192,1024]{2,1,0:T(8,128)(2,1)S(1)}, bf16[1,768,1024]{2,1,0:T(8,128)(2,1)S(1)}) custom-call(bf16[4,4,192,256]{3,2,1,0:T(8,128)(2,1)S(1)} %get-tuple-element.45.g_ref, bf16[192,1024]{1,0:T(8,128)(2,1)S(1)} %bitcast.126, bf16[768,2048]{1,0:T(8,128)(2,1)S(1)} %copy-done.4), custom_call_target="tpu_custom_call" | custom-call | flops 30000000 | tf_op jit(solution)/shard_map/sum_grad_kv/pallas_call | solution.py:489
  337.4 2.6 copy-done.5
  340.0 26.4 %mlp_out.1 = (f32[192,2048]{1,0:T(8,128)S(1)}, bf16[1,768,768]{2,1,0:T(8,128)(2,1)S(1)}) custom-call(bf16[768,2048]{1,0:T(8,128)(2,1)S(1)} %copy-done.2, bf16[2048,2048]{1,0:T(8,128)(2,1)} %w_ref.6, bf16[768,2048]{1,0:T(8,128)(2,1)S(1)} %copy-done.5, bf16[768,256]{1,0:T(8,128)(2,1)S(1)} %bitcast.124), custom_call_target="tpu_custom_call" | custom-call | flops 25000000 | tf_op jit(solution)/shard_map/mlp_out/pallas_call | solution.py:163
  366.4 1.4 fusion.23
  367.9 2.7 add_convert_fusion.4
  370.8 4.5 fusion.12
  375.4 4.0 add_convert_fusion.1
  379.5 4.4 fusion.21
  384.1 2.0 multiply_reduce_fusion.1
  399.1 1.4 broadcast_multiply_fusion.1
  400.5 1.4 broadcast_multiply_fusion
  404.2 16.6 %sum_small.1 = f32[8,128]{1,0:T(8,128)} custom-call(f32[2,2,2,4,8,128]{5,4,3,2,1,0:T(8,128)} %bitcast.146), custom_call_target="tpu_custom_call" | custom-call | flops 12000000 | tf_op jit(solution)/shard_map/sum_small/pallas_call | solution.py:388
  424.2 3.1 add_convert_fusion
  429.4 1.5 copy-done.23
  430.9 3.2 convolution_convert_fusion
  434.0 2.1 multiply_convert_fusion.1
  436.2 74.2 %sum_last.1 = (f32[256,512]{1,0:T(8,128)S(1)}, f32[64,256]{1,0:T(8,128)S(1)}, f32[512,256]{1,0:T(8,128)S(1)}) custom-call(bf16[2,4,256,512]{3,2,1,0:T(8,128)(2,1)S(1)} %bitcast.122, bf16[2,4,4,64,256]{4,3,2,1,0:T(8,128)(2,1)S(1)} %bitcast.123, bf16[2,4,256,512]{3,2,1,0:T(8,128)(2,1)} %bitcast.142), custom_call_target="tpu_custom_call" | custom-call | flops 70000000 | tf_op jit(solution)/shard_map/sum_last/pallas_call | solution.py:796
  510.4 1.4 slice.40
  514.2 3.0 fusion.20
  517.2 2.7 maximum_convert_fusion.1
  519.9 2.9 maximum_convert_fusion
  (235 shorter events, 38.4 us)
Async XLA Ops:
  7.2 22.7 %copy-start = (bf16[2048,256]{1,0:T(8,128)(2,1)S(1)}, bf16[2048,256]{1,0:T(8,128)(2,1)}, u32[]{:S(2)}) copy-start(bf16[2048,256]{1,0:T(8,128)(2,1)} %param.24) | copy-start | bytes 3145732
  7.2 510.0 %reduce-scatter.14.cloned.1.call-start = ((), (), s32[]{:S(2)}) async-start(), calls=%async_computation.9 | async-start | bytes 1310720 | tf_op jit(solution)/shard_map/reduce_scatter | solution.py:932
  7.2 5.5 %copy-start.48 = (bf16[3,256,2048]{2,1,0:T(8,128)(2,1)S(1)}, bf16[3,256,2048]{2,1,0:T(8,128)(2,1)}, u32[]{:S(2)}) copy-start(bf16[3,256,2048]{2,1,0:T(8,128)(2,1)} %param.17) | copy-start | bytes 9437188
  13.3 7.7 %copy-start.56 = (f32[4,3,64]{2,0,1:T(4,128)}, f32[4,3,64]{2,0,1:T(4,128)S(1)}, u32[]{:S(2)}) copy-start(f32[4,3,64]{2,0,1:T(4,128)S(1)} %broadcast_multiply_fusion.2) | copy-start | bytes 9220
  14.3 6.7 %copy-start.57 = (f32[4,3,64]{2,0,1:T(4,128)}, f32[4,3,64]{2,0,1:T(4,128)S(1)}, u32[]{:S(2)}) copy-start(f32[4,3,64]{2,0,1:T(4,128)S(1)} %add_rsqrt_fusion) | copy-start | bytes 9220
  14.6 6.4 %copy-start.62 = (bf16[2048]{0:T(1024)(128)(2,1)S(1)}, bf16[2048]{0:T(1024)(128)(2,1)}, u32[]{:S(2)}) copy-start(bf16[2048]{0:T(1024)(128)(2,1)} %param.21) | copy-start | bytes 12292
  14.6 6.4 %copy-start.63 = (bf16[2048]{0:T(1024)(128)(2,1)S(1)}, bf16[2048]{0:T(1024)(128)(2,1)}, u32[]{:S(2)}) copy-start(bf16[2048]{0:T(1024)(128)(2,1)} %param.20) | copy-start | bytes 12292
  14.6 6.4 %copy-start.68 = (bf16[512]{0:T(512)(128)(2,1)S(1)}, bf16[512]{0:T(512)(128)(2,1)}, u32[]{:S(2)}) copy-start(bf16[512]{0:T(512)(128)(2,1)} %param.23) | copy-start | bytes 3076
  14.6 6.4 %copy-start.21 = (s32[3]{0:T(128)S(1)}, s32[3]{0:T(128)}, u32[]{:S(2)}) copy-start(s32[3]{0:T(128)} %len_ref.3) | copy-start | bytes 40
  14.6 6.7 %copy-start.69 = (bf16[128]{0:T(256)(128)(2,1)S(1)}, bf16[128]{0:T(256)(128)(2,1)}, u32[]{:S(2)}) copy-start(bf16[128]{0:T(256)(128)(2,1)} %param.25) | copy-start | bytes 772
  14.6 6.7 %copy-start.64 = (bf16[2048]{0:T(1024)(128)(2,1)S(1)}, bf16[2048]{0:T(1024)(128)(2,1)}, u32[]{:S(2)}) copy-start(bf16[2048]{0:T(1024)(128)(2,1)} %param.27) | copy-start | bytes 12292
  14.6 6.7 %copy-start.65 = (bf16[2048]{0:T(1024)(128)(2,1)S(1)}, bf16[2048]{0:T(1024)(128)(2,1)}, u32[]{:S(2)}) copy-start(bf16[2048]{0:T(1024)(128)(2,1)} %param.29) | copy-start | bytes 12292
  14.6 6.7 %copy-start.66 = (bf16[2048]{0:T(1024)(128)(2,1)S(1)}, bf16[2048]{0:T(1024)(128)(2,1)}, u32[]{:S(2)}) copy-start(bf16[2048]{0:T(1024)(128)(2,1)} %param.28) | copy-start | bytes 12292
  14.7 7.9 %copy-start.50 = (bf16[3,64,2048]{2,1,0:T(8,128)(2,1)S(1)}, bf16[3,64,2048]{2,1,0:T(8,128)(2,1)}, u32[]{:S(2)}) copy-start(bf16[3,64,2048]{2,1,0:T(8,128)(2,1)} %param.19) | copy-start | bytes 2359300
  22.5 161.4 %copy-start.58 = (f32[1,192]{1,0:T(1,128)}, f32[1,192]{1,0:T(1,128)S(1)}, u32[]{:S(2)}) copy-start(f32[1,192]{1,0:T(1,128)S(1)} %get-tuple-element.72) | copy-start | bytes 2308
  22.5 4.0 slice-start
  22.8 4.5 slice-start.1
  29.9 36.0 %copy-start.54 = (bf16[768,2048]{1,0:T(8,128)(2,1)}, bf16[768,2048]{1,0:T(8,128)(2,1)S(1)}, u32[]{:S(2)}) copy-start(bf16[768,2048]{1,0:T(8,128)(2,1)S(1)} %fusion.10) | copy-start | bytes 9437188
  29.9 34.2 %copy-start.8 = (bf16[2048,512]{1,0:T(8,128)(2,1)S(1)}, bf16[2048,512]{1,0:T(8,128)(2,1)}, u32[]{:S(2)}) copy-start(bf16[2048,512]{1,0:T(8,128)(2,1)} %w_ref.7) | copy-start | bytes 6291460
  64.1 67.2 %copy-start.6 = (bf16[4,192,2048]{2,1,0:T(8,128)(2,1)}, bf16[4,192,2048]{2,1,0:T(8,128)(2,1)S(1)}, u32[]{:S(2)}) copy-start(bf16[4,192,2048]{2,1,0:T(8,128)(2,1)S(1)} %get-tuple-element.39) | copy-start | bytes 9437188
  65.9 7.5 %copy-start.7 = (bf16[512,2048]{1,0:T(8,128)(2,1)S(1)}, bf16[512,2048]{1,0:T(8,128)(2,1)}, u32[]{:S(2)}) copy-start(bf16[512,2048]{1,0:T(8,128)(2,1)} %w_ref.4) | copy-start | bytes 6291460
  73.4 22.8 %copy-start.13 = (bf16[768,512]{1,0:T(8,128)(2,1)}, bf16[768,512]{1,0:T(8,128)(2,1)S(1)}, u32[]{:S(2)}) copy-start(bf16[768,512]{1,0:T(8,128)(2,1)S(1)} %get-tuple-element.38.a_ref) | copy-start | bytes 2359300
  97.1 86.9 %copy-start.46 = (f32[192,2048]{1,0:T(8,128)}, f32[192,2048]{1,0:T(8,128)S(1)}, u32[]{:S(2)}) copy-start(f32[192,2048]{1,0:T(8,128)S(1)} %get-tuple-element.79) | copy-start | bytes 4718596
  97.8 21.0 %copy-start.67 = (bf16[2048]{0:T(1024)(128)(2,1)S(1)}, bf16[2048]{0:T(1024)(128)(2,1)}, u32[]{:S(2)}) copy-start(bf16[2048]{0:T(1024)(128)(2,1)} %param.31) | copy-start | bytes 12292
  118.9 12.5 %copy-start.38 = (bf16[1,384,1024]{2,1,0:T(8,128)(2,1)}, bf16[1,384,1024]{2,1,0:T(8,128)(2,1)S(1)}, u32[]{:S(2)}) copy-start(bf16[1,384,1024]{2,1,0:T(8,128)(2,1)S(1)} %get-tuple-element.60) | copy-start | bytes 2359300
  145.6 81.2 %copy-start.1 = (bf16[768,2048]{1,0:T(8,128)(2,1)}, bf16[768,2048]{1,0:T(8,128)(2,1)S(1)}, u32[]{:S(2)}) copy-start(bf16[768,2048]{1,0:T(8,128)(2,1)S(1)} %get-tuple-element.80.refs_0_.a_ref) | copy-start | bytes 9437188
  145.6 81.2 %copy-start.3 = (bf16[768,2048]{1,0:T(8,128)(2,1)}, bf16[768,2048]{1,0:T(8,128)(2,1)S(1)}, u32[]{:S(2)}) copy-start(bf16[768,2048]{1,0:T(8,128)(2,1)S(1)} %get-tuple-element.77.a_ref.refs_0_.refs_1_) | copy-start | bytes 9437188
  182.6 4.3 copy-start.19
  182.6 4.3 copy-start.30
  217.0 9.8 %copy-start.9 = (bf16[2048,512]{1,0:T(8,128)(2,1)S(1)}, bf16[2048,512]{1,0:T(8,128)(2,1)}, u32[]{:S(2)}) copy-start(bf16[2048,512]{1,0:T(8,128)(2,1)} %w_ref.7) | copy-start | bytes 6291460
  262.4 254.8 %reduce-scatter.12.cloned.1.call-start = ((), (), s32[]{:S(2)}) async-start(), calls=%async_computation.8 | async-start | bytes 1966080 | tf_op jit(solution)/shard_map/reduce_scatter | solution.py:932
  268.6 248.6 %reduce-scatter.10.cloned.1.call-start = ((), (), s32[]{:S(2)}) async-start(), calls=%async_computation.7 | async-start | bytes 1966080 | tf_op jit(solution)/shard_map/reduce_scatter | solution.py:932
  274.8 245.1 %reduce-scatter.8.cloned.1.call-start = ((), (), s32[]{:S(2)}) async-start(), calls=%async_computation.6 | async-start | bytes 1966080 | tf_op jit(solution)/shard_map/reduce_scatter | solution.py:939
  277.7 59.7 %copy-start.2 = (bf16[768,2048]{1,0:T(8,128)(2,1)S(1)}, bf16[768,2048]{1,0:T(8,128)(2,1)}, u32[]{:S(2)}) copy-start(bf16[768,2048]{1,0:T(8,128)(2,1)} %copy-done.1) | copy-start | bytes 9437188
  337.4 29.0 %copy-start.11 = (bf16[4,192,256]{2,1,0:T(8,128)(2,1)}, bf16[4,192,256]{2,1,0:T(8,128)(2,1)S(1)}, u32[]{:S(2)}) copy-start(bf16[4,192,256]{2,1,0:T(8,128)(2,1)S(1)} %get-tuple-element.47) | copy-start | bytes 1179652
  337.4 30.5 %copy-start.26 = (bf16[4,192,1024]{2,1,0:T(8,128)(2,1)}, bf16[4,192,1024]{2,1,0:T(8,128)(2,1)S(1)}, u32[]{:S(2)}) copy-start(bf16[4,192,1024]{2,1,0:T(8,128)(2,1)S(1)} %get-tuple-element.54) | copy-start | bytes 4718596
  340.0 26.4 %copy-start.25 = (bf16[4,192,2048]{2,1,0:T(8,128)(2,1)S(1)}, bf16[4,192,2048]{2,1,0:T(8,128)(2,1)}, u32[]{:S(2)}) copy-start(bf16[4,192,2048]{2,1,0:T(8,128)(2,1)} %copy-done.24) | copy-start | bytes 9437188
  370.6 149.3 %reduce-scatter.6.cloned.1.call-start = ((), (), s32[]{:S(2)}) async-start(), calls=%async_computation.5 | async-start | bytes 3276800 | tf_op jit(solution)/shard_map/reduce_scatter | solution.py:939
  370.8 4.5 copy-start.27
  370.8 4.5 copy-start.29
  370.8 4.5 copy-start.45
  436.1 76.9 %copy-start.61 = (f32[192]{0:T(256)S(1)}, f32[192]{0:T(256)}, u32[]{:S(2)}) copy-start(f32[192]{0:T(256)} %get-tuple-element.64) | copy-start | bytes 2308
  436.1 76.9 %copy-start.60 = (f32[192]{0:T(256)S(1)}, f32[192]{0:T(256)}, u32[]{:S(2)}) copy-start(f32[192]{0:T(256)} %get-tuple-element.68) | copy-start | bytes 2308
  436.1 76.9 %copy-start.47 = (f32[192,2048]{1,0:T(8,128)S(1)}, f32[192,2048]{1,0:T(8,128)}, u32[]{:S(2)}) copy-start(f32[192,2048]{1,0:T(8,128)} %copy-done.46) | copy-start | bytes 4718596
  436.2 76.9 %copy-start.59 = (f32[1,192]{1,0:T(1,128)S(1)}, f32[1,192]{1,0:T(1,128)}, u32[]{:S(2)}) copy-start(f32[1,192]{1,0:T(1,128)} %copy-done.58) | copy-start | bytes 2308
  510.3 3.9 copy-start.15
  510.3 6.9 %copy-start.17 = (f32[256,512]{1,0:T(8,128)}, f32[256,512]{1,0:T(8,128)S(1)}, u32[]{:S(2)}) copy-start(f32[256,512]{1,0:T(8,128)S(1)} %get-tuple-element.97) | copy-start | bytes 1572868
  519.9 4.3 copy-start.16
  (29 other events, 67.5 us)
Sparse Core Ops, SparseCore 0:
  262.5 47.9 reduce-scatter.13
  312.9 34.9 reduce-scatter.11
  350.2 35.7 reduce-scatter.9
  388.2 34.5 reduce-scatter.7
  424.9 59.5 reduce-scatter.5

commit v4 on v3

--- a/solution.py
+++ b/solution.py
@@ -83,9 +83,92 @@
     return [pltpu.SemaphoreType.DMA((max(len(plan), 1), max(lax.axis_size("dp") - 1, 1)))] * 2
 
 
-def reduce_kernel(transposed, plan, n_sources, a_ref, w_ref, *refs):
-    sources, o_ref, refs = refs[:n_sources], refs[n_sources], refs[n_sources + 1 :]
+class Guest:
+    def __init__(self, arrays, views, left, right, by_columns, far):
+        self.arrays, self.views, self.left, self.right, self.by_columns = tuple(arrays), views, left, right, by_columns
+        self.far_array, self.far_first = far
+        self.far_shape = left if by_columns else right
+        self.n_seq = lax.axis_size("seq")
+        self.lanes = 256
+        self.n_chunks = self.far_shape[1] // self.lanes
+        self.n_far = lax.axis_size("dp") - 1
+        self.tokens = left[0] // (self.n_far + 1)
+
+    def out_shape(self):
+        wide, across = self.left[1], self.right[1]
+        shape = (self.n_seq * wide, across // self.n_seq) if self.by_columns else (wide, across)
+        return jax.ShapeDtypeStruct(shape, BF16)
+
+    def scratch(self):
+        dma = pltpu.SemaphoreType.DMA
+        far_sems = dma((max(self.n_far, 1), self.n_chunks))
+        done = pltpu.VMEM(self.out_shape().shape, BF16)
+        loads = dma((4 * (self.n_far + 1),))
+        return [pltpu.VMEM(self.left, BF16), pltpu.VMEM(self.right, BF16), done, dma, loads, far_sems, far_sems]
+
+    def loads(self, refs, scratch):
+        pairs = self.views(refs, scratch[0], scratch[1])
+        return [pltpu.make_async_copy(source, landing, scratch[4].at[i]) for i, (source, landing) in enumerate(pairs)]
+
+    def far_copy(self, refs, scratch, k, c):
+        _, dp_others = others_along("dp")
+        side = scratch[0] if self.by_columns else scratch[1]
+        source = refs[self.far_array].at[:, pl.ds(self.far_first + c * self.lanes, self.lanes)]
+        landing = side.at[pl.ds((k + 1) * self.tokens, self.tokens), pl.ds(c * self.lanes, self.lanes)]
+        return remote(source, landing, scratch[5].at[k, c], scratch[6].at[k, c], {"dp": dp_others[k]})
+
+    def start(self, refs, scratch):
+        for c in range(self.n_chunks):
+            for k in range(self.n_far):
+                self.far_copy(refs, scratch, k, c).start()
+        for copy in self.loads(refs, scratch):
+            copy.start()
+
+    def run(self, refs, scratch, out_ref):
+        left, right, done, done_sem = scratch[:4]
+        for copy in self.loads(refs, scratch):
+            copy.wait()
+        at_once = 1 if self.by_columns else 2
+        for c in range(0, self.n_chunks, at_once):
+            for i in range(at_once):
+                for k in range(self.n_far):
+                    self.far_copy(refs, scratch, k, c + i).wait_recv()
+            first, step = c * self.lanes, at_once * self.lanes
+            a = left[:, first : first + step] if self.by_columns else left[...]
+            b = right[...] if self.by_columns else right[:, first : first + step]
+            block = lax.dot_general(a, b, (((0,), (0,)), ((), ())), preferred_element_type=F32).astype(BF16)
+            if self.by_columns:
+                piece, wide = block.shape[1] // self.n_seq, self.left[1]
+                for s in range(self.n_seq):
+                    done[s * wide + first : s * wide + first + step] = block[:, s * piece : (s + 1) * piece]
+            else:
+                done[:, first : first + step] = block
+        copy = pltpu.make_async_copy(done, out_ref, done_sem)
+        copy.start()
+        for c in range(self.n_chunks):
+            for k in range(self.n_far):
+                self.far_copy(refs, scratch, k, c).wait_send()
+        copy.wait()
+
+
+def split_refs(refs, plan, n_sources, guest):
+    n_guest = len(guest.arrays) if guest else 0
+    sources, refs = refs[:n_sources], refs[n_sources:]
+    guest_in, refs = refs[:n_guest], refs[n_guest:]
+    o_ref, refs = refs[0], refs[1:]
     landings, refs = refs[: len(plan)], refs[len(plan) :]
+    if not guest:
+        return sources, guest_in, o_ref, landings, None, refs, None
+    return sources, guest_in, o_ref, landings, refs[0], refs[1:-7], refs[-7:]
+
+
+def reduce_kernel(transposed, plan, n_sources, guest, spread, a_ref, w_ref, *refs):
+    if spread:
+        spread_ref, ts, tr = refs[0], refs[-2], refs[-1]
+        n_in = 1 + n_sources + len(guest.arrays)
+        spread_all = refs[n_in + 1 + len(plan)]
+        refs = refs[1 : n_in + 1 + len(plan)] + refs[n_in + 2 + len(plan) : -2]
+    sources, guest_in, o_ref, landings, guest_out, refs, guest_scratch = split_refs(refs, plan, n_sources, guest)
     w_here, part, core_out, core_in, over_out, over_in, w_sem, cs, cr, xs, xr, side_s, side_r = refs
     n_blocks, width = core_out.shape[0], core_out.shape[-1]
     share = o_ref.shape[0]
@@ -104,10 +187,12 @@
 
     for n in range(n_blocks):
         load(n).start()
-    greet_tensor_and_dp(len(plan) > 0)
+    greet_tensor_and_dp(len(plan) > 0 or guest is not None)
     beside = side_copies(plan, sources, landings, side_s, side_r)
     for copy in beside:
         copy.start()
+    if guest:
+        guest.start(guest_in, guest_scratch)
 
     def multiply(n):
         load(n).wait()
@@ -138,6 +223,16 @@
 
     lax.fori_loop(0, n_blocks, step, 0)
     pass_on(n_blocks - 1)
+    here, _, _, _, _ = tensor_partners()
+
+    def spread_copy(source, owner, i, target):
+        return remote(source, spread_all.at[owner], ts.at[i], tr.at[i], {"tensor": target})
+
+    if spread:
+        spread_copy(spread_ref, here, 0, across).start()
+        spread_copy(spread_ref, here, 1, partner).start()
+        own_copy = pltpu.make_async_copy(spread_ref, spread_all.at[here], ts.at[2])
+        own_copy.start()
 
     def finish(n, carry):
         to_across(n).wait_recv()
@@ -148,11 +243,20 @@
         return carry
 
     lax.fori_loop(0, n_blocks, finish, 0)
+    if spread:
+        spread_copy(spread_ref, across, 0, across).wait_recv()
+        spread_copy(spread_all.at[across], across, 3, partner).start()
+        spread_copy(spread_ref, here, 0, across).wait_send()
+        spread_copy(spread_ref, here, 1, partner).wait()
+        spread_copy(spread_all.at[across], across, 3, partner).wait()
+        own_copy.wait()
     for copy in beside:
         copy.wait()
-
-
-def product_to_owners(name, number, a, w, transposed, sources=(), plan=()):
+    if guest:
+        guest.run(guest_in, guest_scratch, guest_out)
+
+
+def product_to_owners(name, number, a, w, transposed, sources=(), plan=(), guest=None, spread=None):
     tokens, depth = a.shape
     model_width = w.shape[0] if transposed else w.shape[1]
     share = tokens // 4
@@ -160,11 +264,17 @@
     n_blocks = 4
     w_block = (n_blocks, width, depth) if transposed else (n_blocks, depth, width)
     dma = pltpu.SemaphoreType.DMA((n_blocks,))
+    extra = [] if spread is None else [spread]
     results = pl.pallas_call(
-        functools.partial(reduce_kernel, transposed, plan, len(sources)),
-        out_shape=[jax.ShapeDtypeStruct((share, model_width), F32)] + side_shapes(plan, sources),
-        in_specs=[pl.BlockSpec(memory_space=pltpu.VMEM)] + [pl.BlockSpec(memory_space=pl.ANY)] * (1 + len(sources)),
-        out_specs=[pl.BlockSpec(memory_space=pltpu.VMEM)] + [pl.BlockSpec(memory_space=pltpu.HBM)] * len(plan),
+        functools.partial(reduce_kernel, transposed, plan, len(sources), guest, spread is not None),
+        out_shape=[jax.ShapeDtypeStruct((share, model_width), F32)]
+        + side_shapes(plan, sources)
+        + [jax.ShapeDtypeStruct((4,) + e.shape, e.dtype) for e in extra]
+        + guest_shape(guest),
+        in_specs=[pl.BlockSpec(memory_space=pltpu.VMEM)] + anywhere(1 + len(extra) + len(sources)) + guest_specs(guest),
+        out_specs=[pl.BlockSpec(memory_space=pltpu.VMEM)]
+        + [pl.BlockSpec(memory_space=pltpu.HBM)] * len(extra)
+        + side_specs(plan, guest),
         scratch_shapes=[
             pltpu.VMEM(w_block, BF16),
             pltpu.VMEM((2, 4, share, width), F32),
@@ -178,19 +288,37 @@
             dma,
             dma,
         ]
-        + side_sems(plan),
+        + side_sems(plan)
+        + (guest.scratch() if guest else [])
+        + [pltpu.SemaphoreType.DMA((4,))] * (2 * len(extra)),
         compiler_params=pltpu.CompilerParams(
-            collective_id=number, has_side_effects=True, vmem_limit_bytes=40 * 1024 * 1024
+            collective_id=number, has_side_effects=True, vmem_limit_bytes=52 * 1024 * 1024
         ),
         cost_estimate=estimate(25),
         name=name,
-    )(a, w, *sources)
-    return results[0] if not plan else results
-
-
-def gather_kernel(plan, n_sources, own_ref, *refs):
-    sources, o_ref, refs = refs[:n_sources], refs[n_sources], refs[n_sources + 1 :]
-    landings, refs = refs[: len(plan)], refs[len(plan) :]
+    )(a, w, *extra, *sources, *(guest.arrays if guest else ()))
+    return results
+
+
+def anywhere(count):
+    return [pl.BlockSpec(memory_space=pl.ANY)] * count
+
+
+def guest_specs(guest):
+    return anywhere(len(guest.arrays)) if guest else []
+
+
+def guest_shape(guest):
+    return [guest.out_shape()] if guest else []
+
+
+def side_specs(plan, guest):
+    specs = [pl.BlockSpec(memory_space=pltpu.HBM)] * len(plan)
+    return specs + ([pl.BlockSpec(memory_space=pltpu.HBM)] if guest else [])
+
+
+def gather_kernel(plan, n_sources, guest, own_ref, *refs):
+    sources, guest_in, o_ref, landings, guest_out, refs, guest_scratch = split_refs(refs, plan, n_sources, guest)
     cs, cr, xs, xr, fs, fr, side_s, side_r = refs
     n_chunks = cs.shape[0]
     share = own_ref.shape[0]
@@ -201,7 +329,7 @@
         where = pl.ds(n * rows, rows)
         return send(source.at[where], o_ref.at[owner, where], sems[0].at[n], sems[1].at[n], target)
 
-    greet_tensor_and_dp(len(plan) > 0)
+    greet_tensor_and_dp(len(plan) > 0 or guest is not None)
     beside = side_copies(plan, sources, landings, side_s, side_r)
     for n in range(n_chunks):
         copy(own_ref, here, n, (xs, xr), across).start()
@@ -209,6 +337,8 @@
         side.start()
     for n in range(n_chunks):
         copy(own_ref, here, n, (cs, cr), partner).start()
+    if guest:
+        guest.start(guest_in, guest_scratch)
     o_ref[here] = own_ref[...]
     for n in range(n_chunks):
         copy(own_ref, here, n, (xs, xr), across).wait_recv()
@@ -219,23 +349,25 @@
         copy(o_ref.at[across], across, n, (fs, fr), partner).wait()
     for side in beside:
         side.wait()
-
-
-def gather_shares(name, number, own, sources=(), plan=()):
+    if guest:
+        guest.run(guest_in, guest_scratch, guest_out)
+
+
+def gather_shares(name, number, own, sources=(), plan=(), guest=None):
     share, width = own.shape
     dma = pltpu.SemaphoreType.DMA((4,))
     results = pl.pallas_call(
-        functools.partial(gather_kernel, plan, len(sources)),
-        out_shape=[jax.ShapeDtypeStruct((4, share, width), own.dtype)] + side_shapes(plan, sources),
-        in_specs=[pl.BlockSpec(memory_space=pltpu.VMEM)] + [pl.BlockSpec(memory_space=pl.ANY)] * len(sources),
-        out_specs=[pl.BlockSpec(memory_space=pltpu.VMEM)] + [pl.BlockSpec(memory_space=pltpu.HBM)] * len(plan),
-        scratch_shapes=[dma] * 6 + side_sems(plan),
+        functools.partial(gather_kernel, plan, len(sources), guest),
+        out_shape=[jax.ShapeDtypeStruct((4, share, width), own.dtype)] + side_shapes(plan, sources) + guest_shape(guest),
+        in_specs=[pl.BlockSpec(memory_space=pltpu.VMEM)] + anywhere(len(sources)) + guest_specs(guest),
+        out_specs=[pl.BlockSpec(memory_space=pltpu.VMEM)] + side_specs(plan, guest),
+        scratch_shapes=[dma] * 6 + side_sems(plan) + (guest.scratch() if guest else []),
         compiler_params=pltpu.CompilerParams(
-            collective_id=number, has_side_effects=True, vmem_limit_bytes=16 * 1024 * 1024
+            collective_id=number, has_side_effects=True, vmem_limit_bytes=32 * 1024 * 1024
         ),
         cost_estimate=estimate(20),
         name=name,
-    )(own, *sources)
+    )(own, *sources, *(guest.arrays if guest else ()))
     return (results[0].reshape(4 * share, width), *results[1:])
 
 
@@ -339,85 +471,10 @@
     return me, [lax.rem(me + k, size) for k in range(1, size)]
 
 
-def small_kernel(in_ref, o_ref, core_in, over_out, over_in, dp_out, dp_in, seq_out, seq_in, cs, cr, xs, xr, ys, yr, zs, zr):
-    _, chip, core, partner, across = tensor_partners()
-    dp_me, dp_others = others_along("dp")
-    seq_me, seq_others = others_along("seq")
-    greet_all(
-        [{"tensor": partner}, {"tensor": across}]
-        + [{"dp": other} for other in dp_others]
-        + [{"seq": other} for other in seq_others]
-    )
-
-    def to_partner(j):
-        return remote(in_ref.at[j, 1 - core], core_in.at[j], cs.at[j], cr.at[j], {"tensor": partner})
-
-    to_partner(0).start()
-    to_partner(1).start()
-    to_partner(0).wait()
-    to_partner(1).wait()
-    over_out[...] = in_ref[1 - chip, core] + core_in[1 - chip]
-    to_across = remote(over_out, over_in, xs.at[0], xr.at[0], {"tensor": across})
-    to_across.start()
-    to_across.wait()
-    dp_out[...] = in_ref[chip, core] + core_in[chip] + over_in[...]
-
-    def fold(outgoing, incoming, send_sems, recv_sems, axis, me, others):
-        def copy(target):
-            return remote(outgoing.at[target], incoming.at[me], send_sems.at[target], recv_sems.at[me], {axis: target})
-
-        for other in others:
-            copy(other).start()
-        total = outgoing[me]
-        for other in others:
-            remote(
-                outgoing.at[other], incoming.at[other], send_sems.at[other], recv_sems.at[other], {axis: other}
-            ).wait_recv()
-            total = total + incoming[other]
-        for other in others:
-            copy(other).wait_send()
-        return total
-
-    seq_out[...] = fold(dp_out, dp_in, ys, yr, "dp", dp_me, dp_others)
-    o_ref[...] = fold(seq_out, seq_in, zs, zr, "seq", seq_me, seq_others)
-
-
-def sum_small(number, packed):
-    n_dp, n_seq, rows, lanes = packed.shape[2:]
-    dma = pltpu.SemaphoreType.DMA
-    return pl.pallas_call(
-        small_kernel,
-        out_shape=jax.ShapeDtypeStruct((rows, lanes), F32),
-        in_specs=[pl.BlockSpec(memory_space=pltpu.VMEM)],
-        out_specs=pl.BlockSpec(memory_space=pltpu.VMEM),
-        scratch_shapes=[
-            pltpu.VMEM((2, n_dp, n_seq, rows, lanes), F32),
-            pltpu.VMEM((n_dp, n_seq, rows, lanes), F32),
-            pltpu.VMEM((n_dp, n_seq, rows, lanes), F32),
-            pltpu.VMEM((n_dp, n_seq, rows, lanes), F32),
-            pltpu.VMEM((n_dp, n_seq, rows, lanes), F32),
-            pltpu.VMEM((n_seq, rows, lanes), F32),
-            pltpu.VMEM((n_seq, rows, lanes), F32),
-            dma((2,)),
-            dma((2,)),
-            dma((1,)),
-            dma((1,)),
-            dma((n_dp,)),
-            dma((n_dp,)),
-            dma((n_seq,)),
-            dma((n_seq,)),
-        ],
-        compiler_params=pltpu.CompilerParams(collective_id=number, has_side_effects=True),
-        cost_estimate=estimate(12),
-        name="sum_small",
-    )(packed)
-
-
-def kv_kernel(plan, n_sources, g_ref, two_ref, *refs):
-    sources, o_ref, two_all, refs = refs[:n_sources], refs[n_sources], refs[n_sources + 1], refs[n_sources + 2 :]
-    landings, refs = refs[: len(plan)], refs[len(plan) :]
+def kv_kernel(plan, n_sources, guest, g_ref, *refs):
+    sources, guest_in, o_ref, landings, guest_out, refs, guest_scratch = split_refs(refs, plan, n_sources, guest)
     core_in, over_out, over_in, seq_out, seq_in, own = refs[:6]
-    cs, cr, xs, xr, zs, zr, gs, gr, ts, tr, side_s, side_r = refs[6:]
+    cs, cr, xs, xr, zs, zr, gs, gr, side_s, side_r = refs[6:]
     here, chip, core, partner, across = tensor_partners()
     seq_me, seq_others = others_along("seq")
     greet_all(
@@ -428,9 +485,7 @@
     beside = side_copies(plan, sources, landings, side_s, side_r)
     for copy in beside:
         copy.start()
-
-    def two_copy(source, owner, i, target):
-        return remote(source, two_all.at[owner], ts.at[i], tr.at[i], {"tensor": target})
+    guest.start(guest_in, guest_scratch)
 
     def to_partner(j):
         return remote(g_ref.at[2 * j + 1 - core], core_in.at[j], cs.at[j], cr.at[j], {"tensor": partner})
@@ -441,9 +496,6 @@
     over_out[...] = (g_ref[2 * (1 - chip) + core].astype(F32) + core_in[1 - chip].astype(F32)).astype(BF16)
     to_across = remote(over_out, over_in, xs.at[0], xr.at[0], {"tensor": across})
     to_across.start()
-    two_copy(two_ref, here, 0, across).start()
-    two_copy(two_ref, here, 1, partner).start()
-    two_all[here] = two_ref[...]
     to_partner(chip).wait()
     to_across.wait()
     seq_out[...] = (
@@ -455,8 +507,6 @@
 
     for other in seq_others:
         to_seq(other).start()
-    two_copy(two_ref, across, 0, across).wait_recv()
-    two_copy(two_all.at[across], across, 2, partner).start()
     total = seq_out[seq_me].astype(F32)
     for other in seq_others:
         remote(seq_out.at[other], seq_in.at[other], zs.at[other], zr.at[other], {"seq": other}).wait_recv()
@@ -475,26 +525,24 @@
     f_copy.wait()
     for other in seq_others:
         to_seq(other).wait_send()
-    two_copy(two_ref, here, 0, across).wait_send()
-    two_copy(two_ref, here, 1, partner).wait()
-    two_copy(two_all.at[across], across, 2, partner).wait()
+    guest.run(guest_in, guest_scratch, guest_out)
     for copy in beside:
         copy.wait()
 
 
-def sum_grad_kv(number, parts, two_own, sources, plan):
+def sum_grad_kv(number, parts, sources, plan, guest):
     _, n_seq, share, width = parts.shape
     dma = pltpu.SemaphoreType.DMA
     vmem = pl.BlockSpec(memory_space=pltpu.VMEM)
     results = pl.pallas_call(
-        functools.partial(kv_kernel, plan, len(sources)),
+        functools.partial(kv_kernel, plan, len(sources), guest),
         out_shape=[
             jax.ShapeDtypeStruct((4, share, width), BF16),
-            jax.ShapeDtypeStruct((4,) + two_own.shape, BF16),
         ]
-        + side_shapes(plan, sources),
-        in_specs=[vmem] * 2 + [pl.BlockSpec(memory_space=pl.ANY)] * len(sources),
-        out_specs=[vmem] * 2 + [pl.BlockSpec(memory_space=pltpu.HBM)] * len(plan),
+        + side_shapes(plan, sources)
+        + guest_shape(guest),
+        in_specs=[vmem] + anywhere(len(sources)) + guest_specs(guest),
+        out_specs=[vmem] + side_specs(plan, guest),
         scratch_shapes=[
             pltpu.VMEM((2, n_seq, share, width), BF16),
             pltpu.VMEM((n_seq, share, width), BF16),
@@ -510,16 +558,15 @@
             dma((n_seq,)),
             dma((3,)),
             dma((3,)),
-            dma((3,)),
-            dma((3,)),
         ]
-        + side_sems(plan),
+        + side_sems(plan)
+        + guest.scratch(),
         compiler_params=pltpu.CompilerParams(
-            collective_id=number, has_side_effects=True, vmem_limit_bytes=32 * 1024 * 1024
+            collective_id=number, has_side_effects=True, vmem_limit_bytes=40 * 1024 * 1024
         ),
         cost_estimate=estimate(30),
         name="sum_grad_kv",
-    )(parts, two_own, *sources)
+    )(parts, *sources, *guest.arrays)
     return (results[0].reshape(4 * share, width), *results[1:])
 
 
@@ -715,10 +762,13 @@
     )(lengths, queries, grad_mixed, kv_all, lse)
 
 
-def last_kernel(
-    q_ref, kv_ref, out_ref, q_sum, kv_sum, out_sum,
-    packed, dp_in, near_out, near_in, far_out, far_in, total, ys, yr, ns, nr, fs, fr,
-):
+def last_kernel(n_all, n_local, q_ref, kv_ref, out_ref, _, *refs):
+    small_refs, refs = refs[: n_all + n_local], refs[n_all + n_local :]
+    q_sum, kv_sum, out_sum, small = refs[:4]
+    packed, dp_in, near_out, near_in, far_out, far_in, total, small_core, small_x, small_dp, small_seq = refs[4:15]
+    ys, yr, ns, nr, fs, fr, ss, sr = refs[15:]
+    shared = small_core.shape[0]
+    _, _, _, partner, across = tensor_partners()
     rows = q_ref.shape[2]
     kv_rows, kv_width = kv_ref.shape[3:]
     per_line = q_ref.shape[3] // kv_width
@@ -729,7 +779,25 @@
     beside = seq_me + 1 - 2 * lax.rem(seq_me, 2)
     far = seq_me + 2 - 4 * (seq_me // 2)
     opposite = 3 - seq_me
-    greet_all([{"dp": other} for other in dp_others] + [{"seq": beside}, {"seq": far}])
+    greet_all(
+        [{"tensor": partner}, {"tensor": across}]
+        + [{"dp": other} for other in dp_others]
+        + [{"seq": beside}, {"seq": far}]
+    )
+    small[...] = jnp.zeros_like(small)
+    for i, ref in enumerate(small_refs):
+        row = i if i < n_all else shared + i - n_all
+        small[row : row + 1, : ref.shape[1]] = ref[...]
+    head_rows = pl.ds(0, shared)
+    small_to_partner = remote(small.at[head_rows], small_core, ss.at[0], sr.at[0], {"tensor": partner})
+    small_to_across = remote(small.at[head_rows], small_x, ss.at[1], sr.at[1], {"tensor": across})
+    small_to_beside = remote(small, small_seq.at[0], ss.at[2], sr.at[2], {"seq": beside})
+    small_to_far = remote(small, small_seq.at[1], ss.at[3], sr.at[3], {"seq": far})
+
+    def small_to_dp(k):
+        return remote(small, small_dp.at[k], ss.at[4 + k], sr.at[4 + k], {"dp": dp_others[k]})
+
+    small_to_partner.start()
 
     def to_dp(k, b):
         return remote(packed.at[dp_others[k], b], dp_in.at[k, b], ys.at[k, b], yr.at[k, b], {"dp": dp_others[k]})
@@ -743,10 +811,18 @@
             ]
 
     order = (beside, opposite, far, seq_me)
-    for b in order:
+    for i, b in enumerate(order):
         for k, d in enumerate(dp_others):
             pack(d, b)
             to_dp(k, b).start()
+        if i == 0:
+            small_to_partner.wait()
+            small[:shared] += small_core[...]
+            small_to_across.start()
+            small_to_across.wait()
+            small[:shared] += small_x[...]
+            for k in range(len(dp_others)):
+                small_to_dp(k).start()
     for b in order:
         pack(dp_me, b)
 
@@ -761,10 +837,18 @@
         return remote(near_out.at[i], near_in.at[i], ns.at[i], nr.at[i], {"seq": beside})
 
     near_out[0] = summed(beside).astype(BF16)
+    to_beside(0).start()
+    for k in range(len(dp_others)):
+        small_to_dp(k).wait()
+    for k in range(len(dp_others)):
+        small[...] += small_dp[k]
+    small_to_beside.start()
     near_out[1] = summed(opposite).astype(BF16)
     to_beside(1).start()
-    to_beside(0).start()
     total[...] = summed(far)
+    small_to_beside.wait()
+    small[...] += small_seq[0]
+    small_to_far.start()
     to_beside(1).wait_recv()
     far_out[...] = (total[...] + near_in[1].astype(F32)).astype(BF16)
     to_far = remote(far_out, far_in, fs.at[0], fr.at[0], {"seq": far})
@@ -774,6 +858,8 @@
     total[...] += near_in[0].astype(F32)
     to_far.wait_recv()
     total[...] += far_in[...].astype(F32)
+    small_to_far.wait()
+    small[...] += small_seq[1]
     q_sum[...] = total[:rows]
     out_sum[...] = jnp.transpose(total[rows : 2 * rows])
     for i in range(per_line):
@@ -786,22 +872,24 @@
     to_far.wait_send()
 
 
-def sum_last(number, q_part, kv_part, out_part):
+def sum_last(number, q_part, kv_part, out_part, earlier, summed_all, summed_local):
     n_dp, n_seq, rows, width = q_part.shape
     kv_rows, kv_width = kv_part.shape[3:]
     block = (2 * rows + kv_rows * kv_width // width, width)
     n_far = n_dp - 1
     dma = pltpu.SemaphoreType.DMA
     vmem = pl.BlockSpec(memory_space=pltpu.VMEM)
+    lanes = summed_all[0].shape[1]
     return pl.pallas_call(
-        last_kernel,
+        functools.partial(last_kernel, len(summed_all), len(summed_local)),
         out_shape=(
             jax.ShapeDtypeStruct((rows, width), F32),
             jax.ShapeDtypeStruct((kv_rows, kv_width), F32),
             jax.ShapeDtypeStruct((width, rows), F32),
+            jax.ShapeDtypeStruct((16, lanes), F32),
         ),
-        in_specs=[vmem] * 3,
-        out_specs=(vmem,) * 3,
+        in_specs=[vmem] * 3 + anywhere(1) + [vmem] * (len(summed_all) + len(summed_local)),
+        out_specs=(vmem,) * 4,
         scratch_shapes=[
             pltpu.VMEM((n_dp, n_seq) + block, BF16),
             pltpu.VMEM((n_far, n_seq) + block, BF16),
@@ -810,19 +898,25 @@
             pltpu.VMEM(block, BF16),
             pltpu.VMEM(block, BF16),
             pltpu.VMEM(block, F32),
+            pltpu.VMEM((8, lanes), F32),
+            pltpu.VMEM((8, lanes), F32),
+            pltpu.VMEM((n_far, 16, lanes), F32),
+            pltpu.VMEM((2, 16, lanes), F32),
             dma((n_far, n_seq)),
             dma((n_far, n_seq)),
             dma((2,)),
             dma((2,)),
             dma((1,)),
             dma((1,)),
+            dma((4 + n_far,)),
+            dma((4 + n_far,)),
         ],
         compiler_params=pltpu.CompilerParams(
             collective_id=number, has_side_effects=True, vmem_limit_bytes=48 * 1024 * 1024
         ),
         cost_estimate=estimate(70),
         name="sum_last",
-    )(q_part, kv_part, out_part)
+    )(q_part, kv_part, out_part, earlier, *summed_all, *summed_local)
 
 
 def shards(
@@ -867,7 +961,7 @@
     is_valid = (positions[None, :] < lengths[:, None]).astype(F32)
     valid_own = own_share(by_share(is_valid).reshape(n_tok))[:, None]
     grad_y_own = cotangent.reshape(n_own, model_width).astype(F32) * valid_own
-    x_float = by_share(layer_input).reshape(n_tok, model_width).astype(F32)
+    x_float = lax.optimization_barrier(by_share(layer_input).reshape(n_tok, model_width)).astype(F32)
     normed_x1, inv_one = normalize(x_float)
     flat_one = (normed_x1 * ln1_gain + ln1_bias).astype(BF16)
     kv_bias = jnp.concatenate([jnp.zeros((head_size,), F32), b_value.astype(F32)])
@@ -877,22 +971,23 @@
 
     half_width = model_width // n_dp
     hidden = w_up.shape[1]
-    chunk = hidden // 8
     dp_me = lax.axis_index("dp")
 
-    def own_columns(values_in):
-        return lax.dynamic_slice_in_dim(values_in, dp_me * half_width, half_width, 1)
-
+    first_rows = n_tok * 5 // 128 * 16
     mixed_heads, log_total = attention(lengths, queries, kv_all)
     attn_own, grad_y_far_a = product_to_owners(
-        "attn_out", 1, mixed_heads, w_out, False, (grad_y_low,), ((0, 0, n_tok // 2, None, half_width),)
+        "attn_out", 1, mixed_heads, w_out, False, (grad_y_low,), ((0, 0, first_rows, None, half_width),)
     )
     x_own = own_share(x_float)
     resid_own = x_own + (attn_own + b_out)
     normed_x2, inv_two = normalize(resid_own)
     normed_two = (normed_x2 * ln2_gain + ln2_bias).astype(BF16)
-    flat_two, grad_y_far_b = gather_shares(
-        "gather_norm_two", 2, normed_two, (grad_y_low,), ((0, n_tok // 2, n_tok // 2, None, half_width),)
+    flat_two, grad_y_far_b, two_far_own = gather_shares(
+        "gather_norm_two",
+        2,
+        normed_two,
+        (grad_y_low, normed_two),
+        ((0, first_rows, n_tok - first_rows, None, half_width), (1, 0, n_own, None, half_width)),
     )
     pre_act = jnp.dot(flat_two, w_up, preferred_element_type=F32) + b_up
     activated, gelu_pull = jax.vjp(lambda inner_in: jax.nn.gelu(inner_in, approximate=True), pre_act)
@@ -900,48 +995,72 @@
     grad_act = times_transposed(grad_y_low, w_down)
     grad_pre = gelu_pull(grad_act)[0].astype(BF16)
 
-    def window(source, first, count):
-        return (source, 0, n_tok, first * chunk, count * chunk)
-
-    grad_n2, act_far_a, two_far_own = product_to_owners(
-        "grad_norm_two", 3, grad_pre, w_up, True, (act_low, normed_two), (window(0, 0, 3), (1, 0, n_own, None, half_width))
-    )
+    def mine(ref):
+        return ref.at[:, pl.ds(pl.multiple_of(lax.axis_index("dp") * half_width, half_width), half_width)]
+
+    def tokens_of(ref, k, first=0, rows=n_tok):
+        return ref.at[pl.ds((k + 1) * n_tok + first, rows)]
+
+    group = hidden * 3 // 8
+    half_hidden = hidden // 2
+
+    def part_down(first, width):
+        def views(refs, left, right):
+            act, grads, grads_far_a, grads_far_b = refs
+            pairs = [(act.at[:, pl.ds(first, width)], tokens_of(left, -1)), (mine(grads), tokens_of(right, -1))]
+            for k in range(n_dp - 1):
+                pairs.append((grads_far_a.at[k], tokens_of(right, k, 0, first_rows)))
+                pairs.append((grads_far_b.at[k], tokens_of(right, k, first_rows, n_tok - first_rows)))
+            return pairs
+
+        arrays = (act_low, grad_y_low, grad_y_far_a, grad_y_far_b)
+        return Guest(arrays, views, (n_dp * n_tok, width), (n_dp * n_tok, half_width), True, (0, first))
+
+    def part_up(first, width):
+        def views(refs, left, right):
+            two, far_two, pre = refs
+            pairs = [(mine(two), tokens_of(left, -1)), (pre.at[:, pl.ds(first, width)], tokens_of(right, -1))]
+            for k in range(n_dp - 1):
+                pairs.append((far_two.at[:, pl.ds(k * half_width, half_width)], tokens_of(left, k)))
+            return pairs
+
+        arrays = (flat_two, two_far, grad_pre)
+        return Guest(arrays, views, (n_dp * n_tok, half_width), (n_dp * n_tok, width), False, (2, first))
+
+    def over_seq(values_in):
+        return lax.psum_scatter(values_in, "seq", scatter_dimension=0, tiled=True)
+
+    grad_n2, down_a = product_to_owners("grad_norm_two", 3, grad_pre, w_up, True, guest=part_down(0, group))
+    down_a = over_seq(down_a)
     grad_resid = grad_y_own + norm_back(grad_n2, normed_x2, inv_two, ln2_gain)
     grad_resid_low = grad_resid.astype(BF16)
-    flat_resid, act_far_b = gather_shares("gather_grad_resid", 4, grad_resid_low, (act_low,), (window(0, 3, 3),))
+    flat_resid, down_b = gather_shares("gather_grad_resid", 4, grad_resid_low, guest=part_down(group, group))
+    down_b = over_seq(down_b)
     grad_mixed = times_transposed(flat_resid, w_out).astype(BF16)
     flat_query, grad_kv = attention_back(lengths, queries, grad_mixed, kv_all, log_total)
-    grad_n1, act_far_c, pre_far_a = product_to_owners(
-        "grad_norm_one", 6, flat_query, w_query, True, (act_low, grad_pre), (window(0, 6, 2), window(1, 0, 1))
+    two_swapped = jnp.swapaxes(two_far_own, 0, 1).reshape(n_own, -1)
+    grad_n1, two_far, down_c = product_to_owners(
+        "grad_norm_one",
+        6,
+        flat_query,
+        w_query,
+        True,
+        (down_a,),
+        guest=part_down(2 * group, hidden - 2 * group),
+        spread=two_swapped,
     )
+    down_c = over_seq(down_c)
     grad_n1 = grad_n1 * q_scale
-    two_swapped = jnp.swapaxes(two_far_own, 0, 1).reshape(n_own, -1)
-    flat_kv, two_far, pre_far_b = sum_grad_kv(7, grad_kv, two_swapped, (grad_pre,), (window(0, 1, 4),))
-    mlp_own, pre_far_c = product_to_owners("mlp_out", 5, act_low, w_down, False, (grad_pre, flat_kv), (window(0, 5, 3),))
-    mlp_own = mlp_own + b_down
-
-    grad_y_far = jnp.concatenate([grad_y_far_a, grad_y_far_b], 1)
-    grad_y_here = own_columns(grad_y_low)
-    two_here = own_columns(flat_two)
-    two_far = two_far.reshape(n_tok, n_dp - 1, half_width)
-
-    def part_down(first, count, far):
-        total = across_rows(act_low[:, first * chunk : (first + count) * chunk], grad_y_here)
-        for k in range(n_dp - 1):
-            total = total + across_rows(far[k], grad_y_far[k])
-        return lax.psum_scatter(total.astype(BF16), "seq", scatter_dimension=1, tiled=True)
-
-    def part_up(first, count, fars):
-        total = across_rows(two_here, grad_pre[:, first * chunk : (first + count) * chunk])
-        for k in range(n_dp - 1):
-            far = jnp.concatenate([piece[k] for piece in fars], 1) if len(fars) > 1 else fars[0][k]
-            total = total + across_rows(two_far[:, k], far)
-        return lax.psum_scatter(total.astype(BF16), "seq", scatter_dimension=0, tiled=True)
-
-    g_w_down = jnp.concatenate([part_down(0, 3, act_far_a), part_down(3, 3, act_far_b), part_down(6, 2, act_far_c)], 0)
-    g_w_up = jnp.concatenate([part_up(0, 5, (pre_far_a, pre_far_b)), part_up(5, 3, (pre_far_c,))], 1)
-    g_w_down = g_w_down.astype(F32)
-    g_w_up = g_w_up.astype(F32)
+    two_far = two_far.reshape(n_tok, (n_dp - 1) * half_width)
+    flat_kv, up_a = sum_grad_kv(7, grad_kv, (down_b,), (), part_up(0, half_hidden))
+    up_a = over_seq(up_a)
+    mlp_raw, up_b = product_to_owners(
+        "mlp_out", 5, act_low, w_down, False, (flat_kv, down_c), guest=part_up(half_hidden, half_hidden)
+    )
+    up_b = over_seq(up_b)
+    mlp_own = mlp_raw + b_down
+    g_w_down = jnp.concatenate([down_a, down_b, down_c], 0).astype(F32)
+    g_w_up = jnp.concatenate([up_a, up_b], 1).astype(F32)
 
     def by_owner(values_in, *between):
         return values_in.astype(BF16).reshape((n_dp, n_seq) + between + (-1, values_in.shape[1]))
@@ -949,7 +1068,6 @@
     q_part = by_owner(across_rows(flat_one, flat_query) * q_scale)
     kv_part = by_owner(across_rows(flat_one, flat_kv), n_tensor)
     out_part = by_owner(across_rows(flat_resid, mixed_heads))
-    g_w_query, g_w_kv, g_w_out = sum_last(9, q_part, kv_part, out_part)
     y_own = (valid_own * (resid_own + mlp_own)).astype(BF16).reshape(n_rows, share_len, model_width)
 
     own_kv = own_share(flat_kv)
@@ -957,42 +1075,44 @@
     normed_x1_own = own_share(normed_x1)
     x_grad_own = grad_resid + norm_back(grad_n1, normed_x1_own, own_share(inv_one), ln1_gain)
     x_grad_own = x_grad_own.reshape(n_rows, share_len, model_width)
-    g_ln2_gain = jnp.sum(grad_n2 * normed_x2, axis=0)
-    g_ln2_bias = jnp.sum(grad_n2, axis=0)
-    g_b_out = jnp.sum(grad_resid_low.astype(F32), axis=0)
-    g_b_down = jnp.sum(grad_y_own, axis=0)
-    g_ln1_gain = jnp.sum(grad_n1 * normed_x1_own, axis=0)
-    g_ln1_bias = jnp.sum(grad_n1, axis=0)
-    g_b_up = jnp.sum(grad_pre.astype(F32), axis=0)
-    g_b_query = jnp.sum(flat_query.astype(F32), axis=0) * q_scale
-    g_b_value = jnp.sum(own_kv[:, head_size:].astype(F32), axis=0)
+    def token_sum(values_in):
+        return jnp.sum(values_in.astype(F32), axis=0, keepdims=True)
+
+    over_all = [
+        token_sum(grad_n1 * normed_x1_own),
+        token_sum(grad_n1),
+        token_sum(grad_n2 * normed_x2),
+        token_sum(grad_n2),
+        token_sum(grad_resid_low),
+        token_sum(grad_y_own),
+        token_sum(own_kv[:, head_size:]),
+    ]
+    over_local = [token_sum(grad_pre), token_sum(flat_query) * q_scale]
+    g_w_query, g_w_kv, g_w_out, small = sum_last(9, q_part, kv_part, out_part, up_a, over_all, over_local)
     owners = n_dp * n_seq
-    small = jnp.stack([g_ln1_gain, g_ln1_bias, g_ln2_gain, g_ln2_bias, g_b_out, g_b_down])
-    mine = (lax.iota(jnp.int32, n_tensor) == tensor_index).astype(F32)[:, None, None]
-    query_piece = mine * jnp.moveaxis(g_b_query.reshape(num_heads, owners, -1), 1, 0).reshape(1, owners, -1)
-    up_piece = mine * jnp.moveaxis(g_b_up.reshape(-1, owners, 128 // owners), 1, 0).reshape(1, owners, -1)
-    small_piece = jnp.transpose(small.reshape(6, owners, n_tensor, -1), (2, 1, 0, 3)).reshape(n_tensor, owners, -1)
-    value_piece = jnp.moveaxis(g_b_value.reshape(owners, n_tensor, -1), 1, 0)
-    pieces = [query_piece, up_piece, small_piece, value_piece]
-    sizes = [p.shape[-1] for p in pieces]
-    room = -(-sum(sizes) // 1024) * 1024
-    pieces.append(jnp.zeros((n_tensor, owners, room - sum(sizes)), F32))
-    packed = jnp.concatenate(pieces, -1).reshape(2, 2, n_dp, n_seq, room // 128, 128)
-    packed = sum_small(8, packed).reshape(-1)
-    ends = [sum(sizes[: i + 1]) for i in range(len(sizes))]
-    query_out, up_out, small_out, value_out = [packed[e - s : e] for s, e in zip(sizes, ends)]
+    owner = dp_me * n_seq + seq_index
+    last_owner = owner * n_tensor + tensor_index
+
+    def owned(values_in, index, count):
+        width = values_in.shape[-1] // count
+        return lax.dynamic_slice_in_dim(values_in, index * width, width, values_in.ndim - 1)
+
+    query_out = owned(small[9, : num_heads * head_size].reshape(num_heads, head_size), owner, owners)
+    up_out = owned(small[8].reshape(-1, 128), owner, owners)
+    small_out = owned(small[:6], last_owner, owners * n_tensor)
+    value_out = owned(small[6, :head_size], last_owner, owners * n_tensor)
     return (
         y_own,
         x_grad_own,
         g_w_query,
-        query_out.reshape(num_heads, -1),
+        query_out,
         g_w_kv,
         value_out,
         g_w_out,
         g_w_up,
-        up_out.reshape(-1, 128 // owners),
+        up_out,
         g_w_down,
-        small_out.reshape(6, -1),
+        small_out,
     )
 
 

time: 532 us -> 518 us (0.974); the launches traced: 532 us -> 510 us
  matrix products: 69.2 us -> 43.7 us
  Pallas kernels: 363 us -> 381 us
  local copies, waits for them, and re-layouts: 47.9 us -> 36.9 us
    pallas_call x4, Pallas kernels: 114 us -> 139 us  [product_to_owners(): pl.pallas_call(functools.partial(reduce_kernel, transposed, plan, len(sou...]
    dot_general x13 -> x3, matrix products: 35.7 us -> 10.5 us  [across_rows(): lax.dot_general(left_in, right_in, (((0,), (0,)), ((), ())), preferred_el...]
    convert_element_type x5 -> x3, other arithmetic: 11.7 us -> 4.29 us  [the longest x1 2.81 us: shards(): g_w_up = jnp.concatenate([up_a, up_b], 1).astype(F32)]
    unnamed x153 -> x113, local copies, waits for them, and re-layouts: 23.1 us -> 30.5 us
    pallas_call x5 -> x4, Pallas kernels: 198 us -> 191 us  [the longest x1 75.6 us: sum_last(): pl.pallas_call(functools.partial(last_kernel, len(summed_all), len(summed...]
    convert_element_type x2 -> x0, local copies, waits for them, and re-layouts: 6.68 us -> none  [the longest x1 6.28 us: shards(): x_float = by_share(layer_input).reshape(n_tok, model_width).astype(F32)]
  transfers between devices with their start and end apart: 5 -> 5, of which waited for: 0 -> 0; matrix products, arithmetic and copies ran while one was open for 14% -> 6% of each run, Pallas kernels for 33% -> 50%
where the time goes in v4:
time: 518 us; the launch traced here: 510 us
  Pallas kernels  381 us (74%)
  matrix products  43.7 us (8%)
  local copies, waits for them, and re-layouts  36.9 us (7%)
  other arithmetic  33.2 us (6%)
  between operations  14.8 us (3%)
    pallas_call x4, Pallas kernels, product_to_owners(): pl.pallas_call(functools.partial(reduce_kernel, transposed, plan, len(sou...  139 us
    pallas_call x1, Pallas kernels, sum_last(): pl.pallas_call(functools.partial(last_kernel, len(summed_all), len(summed...  75.6 us
    pallas_call x1, Pallas kernels, sum_grad_kv(): pl.pallas_call(functools.partial(kv_kernel, plan, len(sources), guest), o...  61.8 us
    pallas_call x2, Pallas kernels, gather_shares(): pl.pallas_call(functools.partial(gather_kernel, plan, len(sources), guest...  53.7 us
    pallas_call x1, Pallas kernels, front(): pl.pallas_call(front_kernel, out_shape=(jax.ShapeDtypeStruct((4, share, w...  33.8 us
    unnamed x113, local copies, waits for them, and re-layouts  30.5 us
    dot_general x3, matrix products, times_transposed(): lax.dot_general(left_in, right_in, (((1,), (1,)), ((), ())), preferred_el...  20.1 us
    dot_general x1, matrix products, shards(): pre_act = jnp.dot(flat_two, w_up, preferred_element_type=F32) + b_up  11 us
  transfers between devices with their start and end apart: 5, of which 0 were waited for; matrix products, arithmetic and copies ran while one was open for 6% of the time, Pallas kernels for 50%

profile of v4, /device:TPU:0, one launch (start us, length us, event | category | flops | bytes accessed | tf_op | source)
XLA Modules:
  0.0 510.1 jit_solution(17321719527030414428)
XLA Ops:
  13.7 2.3 copy.28
  16.5 1.0 multiply_reduce_fusion
  17.7 3.5 convert.3
  22.6 5.0 subtract_multiply_fusion
  27.6 1.8 multiply_convert_fusion.3.q_ref
  29.8 33.8 %front.1 = (bf16[4,192,2048]{2,1,0:T(8,128)(2,1)S(1)}, bf16[4,4,192,256]{3,2,1,0:T(8,128)(2,1)S(1)}) custom-call(bf16[192,2048]{1,0:T(8,128)(2,1)S(1)} %fusion.12.grad_ref, bf16[192,256]{1,0:T(8,128)(2,1)S(1)} %fusion.13.kv_ref), custom_call_target="tpu_custom_call" | custom-call | flops 30000000 | tf_op jit(solution)/shard_map/front/pallas_call | solution.py:432
  63.6 1.6 copy-done.1
  65.2 7.2 %attention.1 = (bf16[768,512]{1,0:T(8,128)(2,1)S(1)}, f32[12,1,256]{2,1,0:T(1,128)S(1)}) custom-call(s32[3]{0:T(128)S(1)} %copy-done.35, bf16[768,512]{1,0:T(8,128)(2,1)S(1)} %multiply_convert_fusion.3.q_ref, bf16[4,4,192,256]{3,2,1,0:T(8,128)(2,1)S(1)} %get-tuple-element.37.kv_ref), custom_call_target="tpu_custom_call" | custom-call | flops 10000000 | tf_op jit(solution)/shard_map/attention/pallas_call | solution.py:648
  72.4 25.6 %attn_out.1 = (f32[192,2048]{1,0:T(8,128)}, bf16[1,480,1024]{2,1,0:T(8,128)(2,1)S(1)}) custom-call(bf16[768,512]{1,0:T(8,128)(2,1)S(1)} %get-tuple-element.38.a_ref, bf16[512,2048]{1,0:T(8,128)(2,1)} %w_ref.4, bf16[768,2048]{1,0:T(8,128)(2,1)} %bitcast.80), custom_call_target="tpu_custom_call" | custom-call | flops 25000000 | tf_op jit(solution)/shard_map/attn_out/pallas_call | solution.py:268
  98.1 2.5 fusion.20
  102.1 0.9 copy-done.2
  103.1 24.2 %gather_norm_two.1 = (bf16[4,192,2048]{2,1,0:T(8,128)(2,1)S(1)}, bf16[1,288,1024]{2,1,0:T(8,128)(2,1)S(1)}, bf16[1,192,1024]{2,1,0:T(8,128)(2,1)S(1)}) custom-call(bf16[192,2048]{1,0:T(8,128)(2,1)S(1)} %add_convert_fusion.1.own_ref.refs_1_, bf16[768,2048]{1,0:T(8,128)(2,1)S(1)} %bitcast.83, bf16[192,2048]{1,0:T(8,128)(2,1)S(1)} %add_convert_fusion.1.own_ref.refs_1_), custom_call_target="tpu_custom_call" | custom-call | flops 20000000 | tf_op jit(solution)/shard_map/gather_norm_two/pallas_call | solution.py:359
  127.3 11.0 %fusion.21 = f32[768,2048]{1,0:T(8,128)} fusion(bf16[768,2048]{1,0:T(8,128)(2,1)S(1)} %bitcast.86, bf16[2048,2048]{1,0:T(8,128)(2,1)} %w_ref.5), kind=kOutput, calls=%fused_computation.74 | convolution fusion | flops 6442450944 | bytes 17825792 | tf_op jit(solution)/shard_map/dot_general | solution.py:992
  138.3 1.7 copy-done.6
  140.0 14.7 %convert_reduce_fusion = (f32[2048]{0:T(1024)S(1)}, bf16[768,2048]{1,0:T(8,128)(2,1)}, bf16[768,2048]{1,0:T(8,128)(2,1)}) fusion(f32[768,2048]{1,0:T(8,128)} %fusion.21, f32[2048]{0:T(1024)S(1)} %convert_element_type.117, bf16[768,2048]{1,0:T(8,128)(2,1)S(1)} %bitcast.84, bf16[2048,2048]{1,0:T(8,128)(2,1)S(1)} %bitcast.116), kind=kOutput, calls=%fused_computation.9 | convolution fusion | flops 6481770496 | bytes 24133632 | tf_op jit(solution)/shard_map/dot_general | solution.py:37
  154.7 33.1 %grad_norm_two.1 = (f32[192,2048]{1,0:T(8,128)}, bf16[3072,256]{1,0:T(8,128)(2,1)}) custom-call(bf16[768,2048]{1,0:T(8,128)(2,1)} %get-tuple-element.72.a_ref.refs_3_.refs_4_, bf16[2048,2048]{1,0:T(8,128)(2,1)} %w_ref.5, bf16[768,2048]{1,0:T(8,128)(2,1)} %get-tuple-element.80.refs_0_.refs_2_.a_ref, bf16[768,2048]{1,0:T(8,128)(2,1)} %bitcast.81, ...), custom_call_target="tpu_custom_call" | custom-call | flops 25000000 | tf_op jit(solution)/shard_map/grad_norm_two/pallas_call | solution.py:268
  187.9 2.7 multiply_reduce_fusion.2
  190.7 3.5 convert_reduce_fusion.3
  194.2 29.5 %gather_grad_resid.1 = (bf16[4,192,2048]{2,1,0:T(8,128)(2,1)S(1)}, bf16[3072,256]{1,0:T(8,128)(2,1)S(1)}) custom-call(bf16[192,2048]{1,0:T(8,128)(2,1)S(1)} %get-tuple-element.76.own_ref, bf16[768,2048]{1,0:T(8,128)(2,1)S(1)} %copy-done.4, bf16[768,2048]{1,0:T(8,128)(2,1)S(1)} %bitcast.85, bf16[1,480,1024]{2,1,0:T(8,128)(2,1)S(1)} %get-tuple-element.42.refs_2_.refs_4_, ...), custom_call_target="tpu_custom_call" | custom-call | flops 20000000 | tf_op jit(solution)/shard_map/gather_grad_resid/pallas_call | solution.py:359
  223.7 1.1 copy-done.23
  224.8 1.7 copy-done.36
  226.6 4.5 convolution_convert_fusion.2.do_ref
  231.2 9.8 %attention_back.1 = (bf16[768,512]{1,0:T(8,128)(2,1)S(1)}, bf16[4,4,192,256]{3,2,1,0:T(8,128)(2,1)S(1)}) custom-call(s32[3]{0:T(128)S(1)} %copy-done.35, bf16[768,512]{1,0:T(8,128)(2,1)S(1)} %multiply_convert_fusion.3.q_ref, bf16[768,512]{1,0:T(8,128)(2,1)S(1)} %convolution_convert_fusion.2.do_ref, bf16[4,4,192,256]{3,2,1,0:T(8,128)(2,1)S(1)} %copy-done.11, ...), custom_call_target="tpu_custom_call" | custom-call | flops 25000000 | tf_op jit(solution)/shard_map/attention_back/pallas_call | solution.py:745
  241.0 0.9 copy-done.12
  241.8 1.1 copy-done.21
  243.0 1.0 copy-done.17
  244.0 37.5 %grad_norm_one.1 = (f32[192,2048]{1,0:T(8,128)}, bf16[4,192,1024]{2,1,0:T(8,128)(2,1)}, bf16[2048,256]{1,0:T(8,128)(2,1)}) custom-call(bf16[768,512]{1,0:T(8,128)(2,1)} %copy-done.12, bf16[2048,512]{1,0:T(8,128)(2,1)} %w_ref.6, bf16[192,1024]{1,0:T(8,128)(2,1)S(1)} %bitcast.95, bf16[768,256]{1,0:T(8,128)(2,1)S(1)} %copy-done.17, ...), custom_call_target="tpu_custom_call" | custom-call | flops 25000000 | tf_op jit(solution)/shard_map/grad_norm_one/pallas_call | solution.py:268
  281.6 1.9 copy-done.5
  283.5 1.9 copy-done.7
  285.4 1.4 copy-done.9
  286.8 1.0 copy-done.19
  287.8 1.4 copy-done.22
  289.2 61.8 %sum_grad_kv.1 = (bf16[4,192,256]{2,1,0:T(8,128)(2,1)S(1)}, bf16[1024,1024]{1,0:T(8,128)(2,1)S(1)}) custom-call(bf16[4,4,192,256]{3,2,1,0:T(8,128)(2,1)S(1)} %copy-done.22, bf16[768,256]{1,0:T(8,128)(2,1)S(1)} %copy-done.19, bf16[768,2048]{1,0:T(8,128)(2,1)S(1)} %bitcast.88, bf16[768,1024]{1,0:T(8,128)(2,1)S(1)} %bitcast.90, bf16[768,2048]{1,0:T(8,128)(2,1)S(1)} %copy-done.5), custom_call_target="tpu_custom_call" | custom-call | flops 30000000 | tf_op jit(solution)/shard_map/sum_grad_kv/pallas_call | solution.py:537
  351.0 1.3 copy-done.14
  352.5 0.9 copy-done.13
  353.9 0.9 copy-done.24
  354.9 43.2 %mlp_out.1 = (f32[192,2048]{1,0:T(8,128)}, bf16[1024,1024]{1,0:T(8,128)(2,1)}) custom-call(bf16[768,2048]{1,0:T(8,128)(2,1)} %get-tuple-element.80.refs_0_.refs_2_.a_ref, bf16[2048,2048]{1,0:T(8,128)(2,1)} %w_ref.7, bf16[768,256]{1,0:T(8,128)(2,1)S(1)} %bitcast.93, bf16[512,256]{1,0:T(8,128)(2,1)S(1)} %copy-done.24, bf16[768,2048]{1,0:T(8,128)(2,1)} %bitcast.87, ...), custom_call_target="tpu_custom_call" | custom-call | flops 25000000 | tf_op jit(solution)/shard_map/mlp_out/pallas_call | solution.py:268
  399.2 5.2 %convolution_convert_fusion = bf16[2048,512]{1,0:T(8,128)(2,1)} fusion(bf16[768,2048]{1,0:T(8,128)(2,1)} %bitcast.106, bf16[768,512]{1,0:T(8,128)(2,1)S(1)} %copy-done.28), kind=kOutput, calls=%fused_computation.16 | convolution fusion | flops 1611661312 | bytes 6029312 | tf_op jit(solution)/shard_map/dot_general | solution.py:33
  404.4 3.2 multiply_convert_fusion.1
  407.7 0.9 fusion.11
  408.6 2.0 convolution_convert_fusion.1
  410.7 1.6 fusion.10
  412.3 1.5 maximum_convert_fusion.1
  415.0 1.1 multiply_convert_fusion.2
  416.1 1.0 copy-done.16
  417.1 1.2 copy-done.26
  418.4 75.6 %sum_last.1 = (f32[256,512]{1,0:T(8,128)S(1)}, f32[64,256]{1,0:T(8,128)S(1)}, f32[512,256]{1,0:T(8,128)S(1)}, f32[16,2048]{1,0:T(8,128)S(1)}) custom-call(bf16[2,4,256,512]{3,2,1,0:T(8,128)(2,1)S(1)} %bitcast.91, bf16[2,4,4,64,256]{4,3,2,1,0:T(8,128)(2,1)S(1)} %bitcast.92, bf16[2,4,256,512]{3,2,1,0:T(8,128)(2,1)} %bitcast.119, ...), custom_call_target="tpu_custom_call" | custom-call | flops 70000000 | tf_op jit(solution)/shard_map/sum_last/pallas_call | solution.py:883
  498.1 2.8 maximum_convert_fusion
  (156 shorter events, 20.3 us)
Async XLA Ops:
  7.2 22.2 %copy-start = (bf16[2048,256]{1,0:T(8,128)(2,1)S(1)}, bf16[2048,256]{1,0:T(8,128)(2,1)}, u32[]{:S(2)}) copy-start(bf16[2048,256]{1,0:T(8,128)(2,1)} %param.24) | copy-start | bytes 3145732
  7.2 235.8 %reduce-scatter.8.cloned.1.call-start = ((), (), s32[]{:S(2)}) async-start(), calls=%async_computation.6 | async-start | bytes 1966080 | tf_op jit(solution)/shard_map/reduce_scatter | solution.py:1031
  16.0 1.7 copy-start.37
  17.7 4.7 copy-start.41
  22.6 5.0 copy-start.47
  27.6 1.8 copy-start.45
  29.4 35.8 %copy-start.35 = (s32[3]{0:T(128)S(1)}, s32[3]{0:T(128)}, u32[]{:S(2)}) copy-start(s32[3]{0:T(128)} %len_ref.3) | copy-start | bytes 40
  63.6 1.6 copy-start.1
  65.2 7.2 %copy-start.10 = (bf16[4,4,192,256]{3,2,1,0:T(8,128)(2,1)}, bf16[4,4,192,256]{3,2,1,0:T(8,128)(2,1)S(1)}, u32[]{:S(2)}) copy-start(bf16[4,4,192,256]{3,2,1,0:T(8,128)(2,1)S(1)} %get-tuple-element.37.kv_ref) | copy-start | bytes 4718596
  72.4 25.7 %copy-start.27 = (bf16[768,512]{1,0:T(8,128)(2,1)}, bf16[768,512]{1,0:T(8,128)(2,1)S(1)}, u32[]{:S(2)}) copy-start(bf16[768,512]{1,0:T(8,128)(2,1)S(1)} %get-tuple-element.38.a_ref) | copy-start | bytes 2359300
  98.1 96.0 %copy-start.8 = (bf16[1,480,1024]{2,1,0:T(8,128)(2,1)}, bf16[1,480,1024]{2,1,0:T(8,128)(2,1)S(1)}, u32[]{:S(2)}) copy-start(bf16[1,480,1024]{2,1,0:T(8,128)(2,1)S(1)} %get-tuple-element.42.refs_2_.refs_4_) | copy-start | bytes 2949124
  100.6 1.1 copy-start.38
  100.6 2.5 copy-start.2
  103.1 36.9 %slice-start.2 = ((s8[8388608]{0:T(1024)(128)(4,1)}), s8[4194304]{0:T(1024)(128)(4,1)S(1)}, s32[]{:S(2)}) async-start(s8[8388608]{0:T(1024)(128)(4,1)} %bitcast.115), calls=%async_computation.12 | async-start | bytes 8388608
  127.3 11.0 %copy-start.33 = (bf16[1,192,1024]{2,1,0:T(8,128)(2,1)}, bf16[1,192,1024]{2,1,0:T(8,128)(2,1)S(1)}, u32[]{:S(2)}) copy-start(bf16[1,192,1024]{2,1,0:T(8,128)(2,1)S(1)} %get-tuple-element.50) | copy-start | bytes 1179652
  127.3 12.7 %slice-start.3 = ((s8[8388608]{0:T(1024)(128)(4,1)}), s8[4194304]{0:T(1024)(128)(4,1)S(1)}, s32[]{:S(2)}) async-start(s8[8388608]{0:T(1024)(128)(4,1)} %bitcast.115), calls=%async_computation.13 | async-start | bytes 8388608
  138.3 1.7 copy-start.6
  187.8 93.8 %reduce-scatter.6.cloned.1.call-start = ((), (), s32[]{:S(2)}) async-start(), calls=%async_computation.5 | async-start | bytes 1966080 | tf_op jit(solution)/shard_map/reduce_scatter | solution.py:1031
  187.8 2.8 copy-start.39
  187.8 2.8 copy-start.42
  190.6 3.5 copy-start.3
  190.6 3.5 copy-start.4
  224.8 1.7 copy-start.36
  226.5 127.4 %reduce-scatter.10.cloned.1.call-start = ((), (), s32[]{:S(2)}) async-start(), calls=%async_computation.7 | async-start | bytes 1310720 | tf_op jit(solution)/shard_map/reduce_scatter | solution.py:1031
  226.6 4.5 copy-start.11
  231.1 11.9 %copy-start.34 = (bf16[1,192,1024]{2,1,0:T(8,128)(2,1)S(1)}, bf16[1,192,1024]{2,1,0:T(8,128)(2,1)}, u32[]{:S(2)}) copy-start(bf16[1,192,1024]{2,1,0:T(8,128)(2,1)} %copy-done.33) | copy-start | bytes 1179652
  281.5 134.6 %reduce-scatter.12.cloned.1.call-start = ((), (), s32[]{:S(2)}) async-start(), calls=%async_computation.8 | async-start | bytes 2621440 | tf_op jit(solution)/shard_map/reduce_scatter | solution.py:1031
  281.6 1.9 copy-start.5
  283.5 1.9 copy-start.7
  285.3 1.4 copy-start.9
  287.8 1.4 copy-start.22
  350.9 1.3 copy-start.14
  352.3 1.4 copy-start.43
  352.3 145.8 %reduce-scatter.14.cloned.1.call-start = ((), (), s32[]{:S(2)}) async-start(), calls=%async_computation.9 | async-start | bytes 2621440 | tf_op jit(solution)/shard_map/reduce_scatter | solution.py:1031
  399.2 5.2 %copy-start.46 = (bf16[768,2048]{1,0:T(8,128)(2,1)S(1)}, bf16[768,2048]{1,0:T(8,128)(2,1)}, u32[]{:S(2)}) copy-start(bf16[768,2048]{1,0:T(8,128)(2,1)} %copy-done.45) | copy-start | bytes 9437188
  399.2 8.5 %slice-start = ((s8[6291456]{0:T(1024)(128)(4,1)}), s8[4194304]{0:T(1024)(128)(4,1)S(1)}, s32[]{:S(2)}) async-start(s8[6291456]{0:T(1024)(128)(4,1)} %bitcast.111), calls=%async_computation.10 | async-start | bytes 8388608
  404.4 3.3 slice-start.1
  404.4 3.3 copy-start.49
  408.6 2.1 copy-start.44
  410.7 1.6 copy-start.18
  410.7 1.6 copy-start.20
  410.7 1.6 copy-start.25
  412.3 2.1 copy-start.40
  412.3 2.7 copy-start.48
  413.8 2.3 copy-start.15
  417.1 1.2 copy-start.26
  495.5 5.4 %copy-start.32 = (f32[256,512]{1,0:T(8,128)S(1)}, f32[256,512]{1,0:T(8,128)}, u32[]{:S(2)}) copy-start(f32[256,512]{1,0:T(8,128)} %copy-done.31) | copy-start | bytes 1572868
  498.1 4.2 copy-start.30
  (12 other events, 11.7 us)
Sparse Core Ops, SparseCore 0:
  187.9 42.1 reduce-scatter.7
  233.0 35.5 reduce-scatter.5
  281.6 47.4 reduce-scatter.9
  352.4 41.7 reduce-scatter.11
  398.2 42.8 reduce-scatter.13

commit v5 on v4

--- a/solution.py
+++ b/solution.py
@@ -810,7 +810,7 @@
                 d, b, here, i * lines : (i + 1) * lines
             ]
 
-    order = (beside, opposite, far, seq_me)
+    order = (opposite, far, beside, seq_me)
     for i, b in enumerate(order):
         for k, d in enumerate(dp_others):
             pack(d, b)
@@ -836,23 +836,23 @@
     def to_beside(i):
         return remote(near_out.at[i], near_in.at[i], ns.at[i], nr.at[i], {"seq": beside})
 
-    near_out[0] = summed(beside).astype(BF16)
-    to_beside(0).start()
+    near_out[1] = summed(opposite).astype(BF16)
+    to_beside(1).start()
     for k in range(len(dp_others)):
         small_to_dp(k).wait()
     for k in range(len(dp_others)):
         small[...] += small_dp[k]
     small_to_beside.start()
-    near_out[1] = summed(opposite).astype(BF16)
-    to_beside(1).start()
     total[...] = summed(far)
-    small_to_beside.wait()
-    small[...] += small_seq[0]
-    small_to_far.start()
     to_beside(1).wait_recv()
     far_out[...] = (total[...] + near_in[1].astype(F32)).astype(BF16)
     to_far = remote(far_out, far_in, fs.at[0], fr.at[0], {"seq": far})
     to_far.start()
+    small_to_beside.wait()
+    small[...] += small_seq[0]
+    small_to_far.start()
+    near_out[0] = summed(beside).astype(BF16)
+    to_beside(0).start()
     total[...] = summed(seq_me)
     to_beside(0).wait_recv()
     total[...] += near_in[0].astype(F32)

time: 518 us -> 504 us (0.973); the launches traced: 510 us -> 503 us
  Pallas kernels: 381 us -> 374 us
    pallas_call x1, Pallas kernels: 75.6 us -> 67.9 us  [sum_last(): pl.pallas_call(functools.partial(last_kernel, len(summed_all), len(summed...]
where the time goes in v5:
time: 504 us; the launch traced here: 503 us
  Pallas kernels  374 us (74%)
  matrix products  43.7 us (9%)
  local copies, waits for them, and re-layouts  36.9 us (7%)
  other arithmetic  33.2 us (7%)
  between operations  14.8 us (3%)
    pallas_call x4, Pallas kernels, product_to_owners(): pl.pallas_call(functools.partial(reduce_kernel, transposed, plan, len(sou...  139 us
    pallas_call x1, Pallas kernels, sum_last(): pl.pallas_call(functools.partial(last_kernel, len(summed_all), len(summed...  67.9 us
    pallas_call x1, Pallas kernels, sum_grad_kv(): pl.pallas_call(functools.partial(kv_kernel, plan, len(sources), guest), o...  62.6 us
    pallas_call x2, Pallas kernels, gather_shares(): pl.pallas_call(functools.partial(gather_kernel, plan, len(sources), guest...  53.7 us
    pallas_call x1, Pallas kernels, front(): pl.pallas_call(front_kernel, out_shape=(jax.ShapeDtypeStruct((4, share, w...  33.8 us
    unnamed x113, local copies, waits for them, and re-layouts  30.5 us
    dot_general x3, matrix products, times_transposed(): lax.dot_general(left_in, right_in, (((1,), (1,)), ((), ())), preferred_el...  20.1 us
    dot_general x1, matrix products, shards(): pre_act = jnp.dot(flat_two, w_up, preferred_element_type=F32) + b_up  11 us
  transfers between devices with their start and end apart: 5, of which 0 were waited for; matrix products, arithmetic and copies ran while one was open for 6% of the time, Pallas kernels for 50%

profile of v5, /device:TPU:0, one launch (start us, length us, event | category | flops | bytes accessed | tf_op | source)
XLA Modules:
  0.0 502.7 jit_solution(8634243721241102762)
XLA Ops:
  13.7 2.3 copy.28
  16.5 1.0 multiply_reduce_fusion
  17.7 3.5 convert.3
  22.6 5.0 subtract_multiply_fusion
  27.6 1.8 multiply_convert_fusion.3.q_ref
  29.8 33.8 %front.1 = (bf16[4,192,2048]{2,1,0:T(8,128)(2,1)S(1)}, bf16[4,4,192,256]{3,2,1,0:T(8,128)(2,1)S(1)}) custom-call(bf16[192,2048]{1,0:T(8,128)(2,1)S(1)} %fusion.12.grad_ref, bf16[192,256]{1,0:T(8,128)(2,1)S(1)} %fusion.13.kv_ref), custom_call_target="tpu_custom_call" | custom-call | flops 30000000 | tf_op jit(solution)/shard_map/front/pallas_call | solution.py:432
  63.6 1.6 copy-done.1
  65.2 7.2 %attention.1 = (bf16[768,512]{1,0:T(8,128)(2,1)S(1)}, f32[12,1,256]{2,1,0:T(1,128)S(1)}) custom-call(s32[3]{0:T(128)S(1)} %copy-done.35, bf16[768,512]{1,0:T(8,128)(2,1)S(1)} %multiply_convert_fusion.3.q_ref, bf16[4,4,192,256]{3,2,1,0:T(8,128)(2,1)S(1)} %get-tuple-element.37.kv_ref), custom_call_target="tpu_custom_call" | custom-call | flops 10000000 | tf_op jit(solution)/shard_map/attention/pallas_call | solution.py:648
  72.4 25.6 %attn_out.1 = (f32[192,2048]{1,0:T(8,128)}, bf16[1,480,1024]{2,1,0:T(8,128)(2,1)S(1)}) custom-call(bf16[768,512]{1,0:T(8,128)(2,1)S(1)} %get-tuple-element.38.a_ref, bf16[512,2048]{1,0:T(8,128)(2,1)} %w_ref.4, bf16[768,2048]{1,0:T(8,128)(2,1)} %bitcast.80), custom_call_target="tpu_custom_call" | custom-call | flops 25000000 | tf_op jit(solution)/shard_map/attn_out/pallas_call | solution.py:268
  98.1 2.5 fusion.20
  102.1 0.9 copy-done.2
  103.1 24.2 %gather_norm_two.1 = (bf16[4,192,2048]{2,1,0:T(8,128)(2,1)S(1)}, bf16[1,288,1024]{2,1,0:T(8,128)(2,1)S(1)}, bf16[1,192,1024]{2,1,0:T(8,128)(2,1)S(1)}) custom-call(bf16[192,2048]{1,0:T(8,128)(2,1)S(1)} %add_convert_fusion.1.own_ref.refs_1_, bf16[768,2048]{1,0:T(8,128)(2,1)S(1)} %bitcast.83, bf16[192,2048]{1,0:T(8,128)(2,1)S(1)} %add_convert_fusion.1.own_ref.refs_1_), custom_call_target="tpu_custom_call" | custom-call | flops 20000000 | tf_op jit(solution)/shard_map/gather_norm_two/pallas_call | solution.py:359
  127.3 11.0 %fusion.21 = f32[768,2048]{1,0:T(8,128)} fusion(bf16[768,2048]{1,0:T(8,128)(2,1)S(1)} %bitcast.86, bf16[2048,2048]{1,0:T(8,128)(2,1)} %w_ref.5), kind=kOutput, calls=%fused_computation.74 | convolution fusion | flops 6442450944 | bytes 17825792 | tf_op jit(solution)/shard_map/dot_general | solution.py:992
  138.3 1.7 copy-done.6
  140.0 14.7 %convert_reduce_fusion = (f32[2048]{0:T(1024)S(1)}, bf16[768,2048]{1,0:T(8,128)(2,1)}, bf16[768,2048]{1,0:T(8,128)(2,1)}) fusion(f32[768,2048]{1,0:T(8,128)} %fusion.21, f32[2048]{0:T(1024)S(1)} %convert_element_type.117, bf16[768,2048]{1,0:T(8,128)(2,1)S(1)} %bitcast.84, bf16[2048,2048]{1,0:T(8,128)(2,1)S(1)} %bitcast.116), kind=kOutput, calls=%fused_computation.9 | convolution fusion | flops 6481770496 | bytes 24133632 | tf_op jit(solution)/shard_map/dot_general | solution.py:37
  154.7 33.1 %grad_norm_two.1 = (f32[192,2048]{1,0:T(8,128)}, bf16[3072,256]{1,0:T(8,128)(2,1)}) custom-call(bf16[768,2048]{1,0:T(8,128)(2,1)} %get-tuple-element.72.a_ref.refs_3_.refs_4_, bf16[2048,2048]{1,0:T(8,128)(2,1)} %w_ref.5, bf16[768,2048]{1,0:T(8,128)(2,1)} %get-tuple-element.80.refs_0_.refs_2_.a_ref, bf16[768,2048]{1,0:T(8,128)(2,1)} %bitcast.81, ...), custom_call_target="tpu_custom_call" | custom-call | flops 25000000 | tf_op jit(solution)/shard_map/grad_norm_two/pallas_call | solution.py:268
  187.9 2.7 multiply_reduce_fusion.2
  190.7 3.5 convert_reduce_fusion.3
  194.2 29.5 %gather_grad_resid.1 = (bf16[4,192,2048]{2,1,0:T(8,128)(2,1)S(1)}, bf16[3072,256]{1,0:T(8,128)(2,1)S(1)}) custom-call(bf16[192,2048]{1,0:T(8,128)(2,1)S(1)} %get-tuple-element.76.own_ref, bf16[768,2048]{1,0:T(8,128)(2,1)S(1)} %copy-done.4, bf16[768,2048]{1,0:T(8,128)(2,1)S(1)} %bitcast.85, bf16[1,480,1024]{2,1,0:T(8,128)(2,1)S(1)} %get-tuple-element.42.refs_2_.refs_4_, ...), custom_call_target="tpu_custom_call" | custom-call | flops 20000000 | tf_op jit(solution)/shard_map/gather_grad_resid/pallas_call | solution.py:359
  223.7 1.1 copy-done.23
  224.8 1.7 copy-done.36
  226.6 4.5 convolution_convert_fusion.2.do_ref
  231.2 9.8 %attention_back.1 = (bf16[768,512]{1,0:T(8,128)(2,1)S(1)}, bf16[4,4,192,256]{3,2,1,0:T(8,128)(2,1)S(1)}) custom-call(s32[3]{0:T(128)S(1)} %copy-done.35, bf16[768,512]{1,0:T(8,128)(2,1)S(1)} %multiply_convert_fusion.3.q_ref, bf16[768,512]{1,0:T(8,128)(2,1)S(1)} %convolution_convert_fusion.2.do_ref, bf16[4,4,192,256]{3,2,1,0:T(8,128)(2,1)S(1)} %copy-done.11, ...), custom_call_target="tpu_custom_call" | custom-call | flops 25000000 | tf_op jit(solution)/shard_map/attention_back/pallas_call | solution.py:745
  241.0 0.9 copy-done.12
  241.8 1.1 copy-done.21
  243.0 1.0 copy-done.17
  244.0 37.5 %grad_norm_one.1 = (f32[192,2048]{1,0:T(8,128)}, bf16[4,192,1024]{2,1,0:T(8,128)(2,1)}, bf16[2048,256]{1,0:T(8,128)(2,1)}) custom-call(bf16[768,512]{1,0:T(8,128)(2,1)} %copy-done.12, bf16[2048,512]{1,0:T(8,128)(2,1)} %w_ref.6, bf16[192,1024]{1,0:T(8,128)(2,1)S(1)} %bitcast.95, bf16[768,256]{1,0:T(8,128)(2,1)S(1)} %copy-done.17, ...), custom_call_target="tpu_custom_call" | custom-call | flops 25000000 | tf_op jit(solution)/shard_map/grad_norm_one/pallas_call | solution.py:268
  281.6 1.9 copy-done.5
  283.5 1.9 copy-done.7
  285.4 1.4 copy-done.9
  286.8 1.0 copy-done.19
  287.8 1.4 copy-done.22
  289.2 62.6 %sum_grad_kv.1 = (bf16[4,192,256]{2,1,0:T(8,128)(2,1)S(1)}, bf16[1024,1024]{1,0:T(8,128)(2,1)S(1)}) custom-call(bf16[4,4,192,256]{3,2,1,0:T(8,128)(2,1)S(1)} %copy-done.22, bf16[768,256]{1,0:T(8,128)(2,1)S(1)} %copy-done.19, bf16[768,2048]{1,0:T(8,128)(2,1)S(1)} %bitcast.88, bf16[768,1024]{1,0:T(8,128)(2,1)S(1)} %bitcast.90, bf16[768,2048]{1,0:T(8,128)(2,1)S(1)} %copy-done.5), custom_call_target="tpu_custom_call" | custom-call | flops 30000000 | tf_op jit(solution)/shard_map/sum_grad_kv/pallas_call | solution.py:537
  351.8 1.3 copy-done.14
  353.3 0.9 copy-done.13
  354.8 0.9 copy-done.24
  355.7 42.6 %mlp_out.1 = (f32[192,2048]{1,0:T(8,128)}, bf16[1024,1024]{1,0:T(8,128)(2,1)}) custom-call(bf16[768,2048]{1,0:T(8,128)(2,1)} %get-tuple-element.80.refs_0_.refs_2_.a_ref, bf16[2048,2048]{1,0:T(8,128)(2,1)} %w_ref.7, bf16[768,256]{1,0:T(8,128)(2,1)S(1)} %bitcast.93, bf16[512,256]{1,0:T(8,128)(2,1)S(1)} %copy-done.24, bf16[768,2048]{1,0:T(8,128)(2,1)} %bitcast.87, ...), custom_call_target="tpu_custom_call" | custom-call | flops 25000000 | tf_op jit(solution)/shard_map/mlp_out/pallas_call | solution.py:268
  399.5 5.2 %convolution_convert_fusion = bf16[2048,512]{1,0:T(8,128)(2,1)} fusion(bf16[768,2048]{1,0:T(8,128)(2,1)} %bitcast.106, bf16[768,512]{1,0:T(8,128)(2,1)S(1)} %copy-done.28), kind=kOutput, calls=%fused_computation.16 | convolution fusion | flops 1611661312 | bytes 6029312 | tf_op jit(solution)/shard_map/dot_general | solution.py:33
  404.7 3.2 multiply_convert_fusion.1
  408.0 0.9 fusion.11
  408.9 2.0 convolution_convert_fusion.1
  411.0 1.6 fusion.10
  412.6 1.5 maximum_convert_fusion.1
  415.2 1.1 multiply_convert_fusion.2
  416.4 1.0 copy-done.16
  417.4 1.2 copy-done.26
  418.6 67.9 %sum_last.1 = (f32[256,512]{1,0:T(8,128)S(1)}, f32[64,256]{1,0:T(8,128)S(1)}, f32[512,256]{1,0:T(8,128)S(1)}, f32[16,2048]{1,0:T(8,128)S(1)}) custom-call(bf16[2,4,256,512]{3,2,1,0:T(8,128)(2,1)S(1)} %bitcast.91, bf16[2,4,4,64,256]{4,3,2,1,0:T(8,128)(2,1)S(1)} %bitcast.92, bf16[2,4,256,512]{3,2,1,0:T(8,128)(2,1)} %bitcast.119, ...), custom_call_target="tpu_custom_call" | custom-call | flops 70000000 | tf_op jit(solution)/shard_map/sum_last/pallas_call | solution.py:883
  490.7 2.8 maximum_convert_fusion
  (156 shorter events, 20.3 us)
Async XLA Ops:
  7.2 22.2 %copy-start = (bf16[2048,256]{1,0:T(8,128)(2,1)S(1)}, bf16[2048,256]{1,0:T(8,128)(2,1)}, u32[]{:S(2)}) copy-start(bf16[2048,256]{1,0:T(8,128)(2,1)} %param.24) | copy-start | bytes 3145732
  7.2 235.8 %reduce-scatter.8.cloned.1.call-start = ((), (), s32[]{:S(2)}) async-start(), calls=%async_computation.6 | async-start | bytes 1966080 | tf_op jit(solution)/shard_map/reduce_scatter | solution.py:1031
  16.0 1.7 copy-start.37
  17.7 4.7 copy-start.41
  22.6 5.0 copy-start.47
  27.6 1.8 copy-start.45
  29.4 35.8 %copy-start.35 = (s32[3]{0:T(128)S(1)}, s32[3]{0:T(128)}, u32[]{:S(2)}) copy-start(s32[3]{0:T(128)} %len_ref.3) | copy-start | bytes 40
  63.6 1.6 copy-start.1
  65.2 7.2 %copy-start.10 = (bf16[4,4,192,256]{3,2,1,0:T(8,128)(2,1)}, bf16[4,4,192,256]{3,2,1,0:T(8,128)(2,1)S(1)}, u32[]{:S(2)}) copy-start(bf16[4,4,192,256]{3,2,1,0:T(8,128)(2,1)S(1)} %get-tuple-element.37.kv_ref) | copy-start | bytes 4718596
  72.4 25.7 %copy-start.27 = (bf16[768,512]{1,0:T(8,128)(2,1)}, bf16[768,512]{1,0:T(8,128)(2,1)S(1)}, u32[]{:S(2)}) copy-start(bf16[768,512]{1,0:T(8,128)(2,1)S(1)} %get-tuple-element.38.a_ref) | copy-start | bytes 2359300
  98.1 96.0 %copy-start.8 = (bf16[1,480,1024]{2,1,0:T(8,128)(2,1)}, bf16[1,480,1024]{2,1,0:T(8,128)(2,1)S(1)}, u32[]{:S(2)}) copy-start(bf16[1,480,1024]{2,1,0:T(8,128)(2,1)S(1)} %get-tuple-element.42.refs_2_.refs_4_) | copy-start | bytes 2949124
  100.6 1.1 copy-start.38
  100.6 2.5 copy-start.2
  103.1 36.9 %slice-start.2 = ((s8[8388608]{0:T(1024)(128)(4,1)}), s8[4194304]{0:T(1024)(128)(4,1)S(1)}, s32[]{:S(2)}) async-start(s8[8388608]{0:T(1024)(128)(4,1)} %bitcast.115), calls=%async_computation.12 | async-start | bytes 8388608
  127.3 11.0 %copy-start.33 = (bf16[1,192,1024]{2,1,0:T(8,128)(2,1)}, bf16[1,192,1024]{2,1,0:T(8,128)(2,1)S(1)}, u32[]{:S(2)}) copy-start(bf16[1,192,1024]{2,1,0:T(8,128)(2,1)S(1)} %get-tuple-element.50) | copy-start | bytes 1179652
  127.3 12.7 %slice-start.3 = ((s8[8388608]{0:T(1024)(128)(4,1)}), s8[4194304]{0:T(1024)(128)(4,1)S(1)}, s32[]{:S(2)}) async-start(s8[8388608]{0:T(1024)(128)(4,1)} %bitcast.115), calls=%async_computation.13 | async-start | bytes 8388608
  138.3 1.7 copy-start.6
  187.8 93.8 %reduce-scatter.6.cloned.1.call-start = ((), (), s32[]{:S(2)}) async-start(), calls=%async_computation.5 | async-start | bytes 1966080 | tf_op jit(solution)/shard_map/reduce_scatter | solution.py:1031
  187.8 2.8 copy-start.39
  187.8 2.8 copy-start.42
  190.6 3.5 copy-start.3
  190.6 3.5 copy-start.4
  224.8 1.7 copy-start.36
  226.5 128.2 %reduce-scatter.10.cloned.1.call-start = ((), (), s32[]{:S(2)}) async-start(), calls=%async_computation.7 | async-start | bytes 1310720 | tf_op jit(solution)/shard_map/reduce_scatter | solution.py:1031
  226.6 4.5 copy-start.11
  231.1 11.9 %copy-start.34 = (bf16[1,192,1024]{2,1,0:T(8,128)(2,1)S(1)}, bf16[1,192,1024]{2,1,0:T(8,128)(2,1)}, u32[]{:S(2)}) copy-start(bf16[1,192,1024]{2,1,0:T(8,128)(2,1)} %copy-done.33) | copy-start | bytes 1179652
  281.5 134.9 %reduce-scatter.12.cloned.1.call-start = ((), (), s32[]{:S(2)}) async-start(), calls=%async_computation.8 | async-start | bytes 2621440 | tf_op jit(solution)/shard_map/reduce_scatter | solution.py:1031
  281.6 1.9 copy-start.5
  283.5 1.9 copy-start.7
  285.3 1.4 copy-start.9
  287.8 1.4 copy-start.22
  351.8 1.3 copy-start.14
  353.1 1.4 copy-start.43
  353.1 137.6 %reduce-scatter.14.cloned.1.call-start = ((), (), s32[]{:S(2)}) async-start(), calls=%async_computation.9 | async-start | bytes 2621440 | tf_op jit(solution)/shard_map/reduce_scatter | solution.py:1031
  399.5 5.2 %copy-start.46 = (bf16[768,2048]{1,0:T(8,128)(2,1)S(1)}, bf16[768,2048]{1,0:T(8,128)(2,1)}, u32[]{:S(2)}) copy-start(bf16[768,2048]{1,0:T(8,128)(2,1)} %copy-done.45) | copy-start | bytes 9437188
  399.5 8.5 %slice-start = ((s8[6291456]{0:T(1024)(128)(4,1)}), s8[4194304]{0:T(1024)(128)(4,1)S(1)}, s32[]{:S(2)}) async-start(s8[6291456]{0:T(1024)(128)(4,1)} %bitcast.111), calls=%async_computation.10 | async-start | bytes 8388608
  404.7 3.3 slice-start.1
  404.7 3.3 copy-start.49
  408.9 2.1 copy-start.44
  411.0 1.6 copy-start.18
  411.0 1.6 copy-start.20
  411.0 1.6 copy-start.25
  412.6 2.1 copy-start.40
  412.6 2.6 copy-start.48
  414.1 2.3 copy-start.15
  417.4 1.2 copy-start.26
  488.1 5.4 %copy-start.32 = (f32[256,512]{1,0:T(8,128)S(1)}, f32[256,512]{1,0:T(8,128)}, u32[]{:S(2)}) copy-start(f32[256,512]{1,0:T(8,128)} %copy-done.31) | copy-start | bytes 1572868
  490.7 4.2 copy-start.30
  (12 other events, 11.7 us)
Sparse Core Ops, SparseCore 0:
  187.9 42.3 reduce-scatter.7
  233.2 36.0 reduce-scatter.5
  281.6 48.5 reduce-scatter.9
  353.3 41.6 reduce-scatter.11
  398.5 44.1 reduce-scatter.13
